TPU v7x, 128 devices: a whole 4x4x4 slice. The times are simulated.
128 devices in a mesh: ctx: 8 (over y, core), grp: 16 (over x, z).
Axes of the slice: x: 4, y: 4, z: 4, core: 2. Of those that a mesh axis runs over, the one named last changes fastest.
Arguments:
- query_feat: bfloat16 [32768, 4096], P(('ctx', 'grp')), may hold values from 0.0099487305 to 1
- key_feat: bfloat16 [32768, 4096], P(('ctx', 'grp')), may hold values from 0.0099487305 to 1
- values: bfloat16 [32768, 2048], P(('ctx', 'grp')), may hold values from -6 to 6
- teacher: bfloat16 [32768, 2048], P('ctx', 'grp'), may hold values from -4 to 4
Outputs:
- query_grad: bfloat16 [32768, 4096], P(('ctx', 'grp'))
- key_grad: bfloat16 [32768, 4096], P(('ctx', 'grp'))
All inputs are finite; a program needn't handle non-finite values.
Results may differ from a plain program's by a relative error of at most 0.001.
Values may be sent and summed in bfloat16 or wider, within the bound.
No kernel may reach another device: no remote copies, remote signals or barrier semaphores. Data moves between devices by JAX's collectives and lax.ppermute only.
A program may use at most 576 MiB of HBM per device.

v0:
```python
import jax
import jax.numpy as jnp
from jax import lax
from jax.sharding import PartitionSpec as P

H = 16


HIGH = lax.Precision.HIGHEST


def entering(array, axis, combine, identity, reverse):
    size, mine = (lax.axis_size(axis), lax.axis_index(axis))
    everything = jax.tree.map(lambda part: lax.all_gather(part, axis), array)
    start = jax.tree.map(
        lambda part, zero: jnp.broadcast_to(jnp.asarray(zero, part.dtype), part.shape),
        array,
        identity,
    )

    def step(k, before):
        at = size - 1 - k if reverse else k
        reached = at > mine if reverse else at < mine
        new = combine(before, jax.tree.map(lambda part: part[at], everything))
        return jax.tree.map(lambda a, b: jnp.where(reached, a, b), new, before)

    return lax.fori_loop(0, size, step, start)


def add_pair(earlier, later):
    return (earlier[0] + later[0], earlier[1] + later[1])


def exclusive_blocks(stack, reverse):
    return lax.cumsum(stack, axis=0, reverse=reverse) - stack


def local_grads(query_feat, key_feat, values, teacher, heads, before_fn, after_fn, scale):
    rows = query_feat.shape[0]
    feat = query_feat.shape[1] // heads
    width = values.shape[1] // heads
    block = min(rows, 512)
    count = rows // block
    fq = query_feat.reshape(count, block, heads, feat)
    fk = key_feat.reshape(count, block, heads, feat)
    fq_wide = fq.astype(jnp.float32)
    fk_wide = fk.astype(jnp.float32)
    val_wide = values.reshape(count, block, heads, width).astype(jnp.float32)
    target = teacher.reshape(count, block, heads, width).astype(jnp.float32)
    rows_t = lax.broadcasted_iota(jnp.int32, (block, block), 0)
    rows_s = lax.broadcasted_iota(jnp.int32, (block, block), 1)
    causal = (rows_s <= rows_t).astype(jnp.float32)
    scores = jnp.einsum("bthf,bshf->bhts", fq, fk, preferred_element_type=jnp.float32) * causal
    kv_blocks = jnp.einsum("bshf,bshd->bhfd", fk_wide, val_wide, precision=HIGH)
    key_blocks = jnp.sum(fk_wide, axis=1)
    kv_before, key_before = before_fn(jnp.sum(kv_blocks, axis=0), jnp.sum(key_blocks, axis=0))
    kv_state = kv_before[None] + exclusive_blocks(kv_blocks, False)
    key_state = key_before[None] + exclusive_blocks(key_blocks, False)
    numer = jnp.einsum("bhts,bshd->bthd", scores, val_wide, precision=HIGH)
    numer = numer + jnp.einsum("bthf,bhfd->bthd", fq_wide, kv_state, precision=HIGH)
    denom = jnp.transpose(jnp.sum(scores, axis=3), (0, 2, 1))
    denom = denom + jnp.einsum("bthf,bhf->bth", fq_wide, key_state, precision=HIGH)
    student = numer / denom[..., None]
    resid = student - target
    d_numer = resid / denom[..., None]
    d_denom = -jnp.sum(resid * student, axis=3) / denom
    mixed = jnp.einsum("bthd,bshd->bhts", d_numer, val_wide, precision=HIGH)
    mixed = (mixed + jnp.transpose(d_denom, (0, 2, 1))[..., None]) * causal
    adj_blocks = jnp.einsum("bthf,bthd->bhfd", fq_wide, d_numer, precision=HIGH)
    query_blocks = jnp.einsum("bthf,bth->bhf", fq_wide, d_denom, precision=HIGH)
    adj_after, query_after = after_fn(jnp.sum(adj_blocks, axis=0), jnp.sum(query_blocks, axis=0))
    adj_state = adj_after[None] + exclusive_blocks(adj_blocks, True)
    query_state = query_after[None] + exclusive_blocks(query_blocks, True)
    q_grad = jnp.einsum("bhts,bshf->bthf", mixed, fk_wide, precision=HIGH)
    q_grad = q_grad + jnp.einsum("bhfd,bthd->bthf", kv_state, d_numer, precision=HIGH)
    q_grad = q_grad + key_state[:, None] * d_denom[..., None]
    k_grad = jnp.einsum("bhts,bthf->bshf", mixed, fq_wide, precision=HIGH)
    k_grad = k_grad + jnp.einsum("bhfd,bshd->bshf", adj_state, val_wide, precision=HIGH)
    k_grad = k_grad + query_state[:, None]
    query_out = (scale * q_grad).astype(jnp.bfloat16).reshape(rows, heads * feat)
    key_out = (scale * k_grad).astype(jnp.bfloat16).reshape(rows, heads * feat)
    return (query_out, key_out)


def on_device(query_feat, key_feat, values, teacher):
    groups = lax.axis_size("grp")
    total_tokens = query_feat.shape[0] * lax.axis_size("ctx") * groups
    scale = float(total_tokens) ** 0.5
    query_rows, key_rows, value_rows = (
        lax.all_to_all(query_feat, "grp", split_axis=1, concat_axis=0, tiled=True),
        lax.all_to_all(key_feat, "grp", split_axis=1, concat_axis=0, tiled=True),
        lax.all_to_all(values, "grp", split_axis=1, concat_axis=0, tiled=True),
    )
    heads_here = H // groups

    def before_fn(kv_sum, key_sum):
        zeros = (jnp.zeros_like(kv_sum), jnp.zeros_like(key_sum))
        return entering((kv_sum, key_sum), "ctx", add_pair, zeros, False)

    def after_fn(adj_sum, query_sum):
        zeros = (jnp.zeros_like(adj_sum), jnp.zeros_like(query_sum))
        return entering((adj_sum, query_sum), "ctx", add_pair, zeros, True)

    query_head, key_head = local_grads(
        query_rows, key_rows, value_rows, teacher, heads_here, before_fn, after_fn, scale
    )
    query_grad, key_grad = (
        lax.all_to_all(query_head, "grp", split_axis=0, concat_axis=1, tiled=True),
        lax.all_to_all(key_head, "grp", split_axis=0, concat_axis=1, tiled=True),
    )
    return (query_grad, key_grad)


def solution(mesh):
    placed = (
        P(("ctx", "grp"), None),
        P(("ctx", "grp"), None),
        P(("ctx", "grp"), None),
        P("ctx", "grp"),
    )
    return jax.shard_map(
        on_device,
        mesh=mesh,
        in_specs=placed,
        out_specs=(P(("ctx", "grp"), None), P(("ctx", "grp"), None)),
        check_vma=False,
    )
```

profile of v0, /device:TPU:0, one launch (start us, length us, event | category | flops | bytes accessed | tf_op | source)
XLA Modules:
  0.0 231.8 jit_solution(8206471984383794272)
XLA Ops:
  7.2 0.0 copy-start.12
  7.2 2.4 %copy.97 = bf16[256,2048]{0,1:T(8,128)(2,1)} copy(bf16[256,2048]{1,0:T(8,128)(2,1)} %param.10) | data formatting | bytes 2097152 | tf_op args[2]
  9.6 8.0 %all-to-all-start.2 = ((bf16[256,16,128]{0,2,1:T(8,128)(2,1)}), bf16[256,16,128]{0,2,1:T(8,128)(2,1)S(1)}, u32[]{:S(2)}, u32[]{:S(2)}) async-start(bf16[256,16,128]{0,2,1:T(8,128)(2,1)} %bitcast.4), calls=%async_computation.2 | async-start | bytes 2097152 | tf_op jit(solution)/shard_map/all_to_all | solution.py:92
  17.6 0.0 copy-done.12
  17.6 1.5 copy.147
  19.1 16.2 %all-to-all-done.2 = bf16[256,16,128]{0,2,1:T(8,128)(2,1)S(1)} async-done(((bf16[256,16,128]{0,2,1:T(8,128)(2,1)}), bf16[256,16,128]{0,2,1:T(8,128)(2,1)S(1)}, u32[]{:S(2)}, u32[]{:S(2)}) %all-to-all-start.2) | async-done | bytes 1048608 | tf_op jit(solution)/shard_map/all_to_all | solution.py:92
  35.3 1.0 copy-done.11
  36.3 3.7 %all-to-all-start.1 = ((bf16[256,16,256]{2,0,1:T(8,128)(2,1)}), bf16[256,16,256]{2,0,1:T(8,128)(2,1)S(1)}, u32[]{:S(2)}, u32[]{:S(2)}) async-start(bf16[256,16,256]{2,0,1:T(8,128)(2,1)} %bitcast.156), calls=%async_computation.1 | async-start | bytes 4194304 | tf_op jit(solution)/shard_map/all_to_all | solution.py:91
  40.0 3.1 %copy.148 = bf16[32,16,8,256]{3,2,0,1:T(8,128)(2,1)} copy(bf16[32,16,8,256]{3,2,1,0:T(8,128)(2,1)} %bitcast.163) | data formatting | bytes 4194304 | tf_op jit(solution)/shard_map/all_to_all | solution.py:90
  43.2 24.7 %all-to-all-done.1 = bf16[256,16,256]{2,0,1:T(8,128)(2,1)S(1)} async-done(((bf16[256,16,256]{2,0,1:T(8,128)(2,1)}), bf16[256,16,256]{2,0,1:T(8,128)(2,1)S(1)}, u32[]{:S(2)}, u32[]{:S(2)}) %all-to-all-start.1) | async-done | bytes 2097184 | tf_op jit(solution)/shard_map/all_to_all | solution.py:91
  67.9 1.3 copy-done
  69.2 3.8 %all-to-all-start = ((bf16[256,16,256]{2,0,1:T(8,128)(2,1)}), bf16[256,16,256]{2,0,1:T(8,128)(2,1)S(1)}, u32[]{:S(2)}, u32[]{:S(2)}) async-start(bf16[256,16,256]{2,0,1:T(8,128)(2,1)} %bitcast.154), calls=%async_computation | async-start | bytes 4194304 | tf_op jit(solution)/shard_map/all_to_all | solution.py:90
  73.0 0.0 all-gather.9.cloned.1.call-start
  73.0 1.6 copy.98
  74.6 0.0 copy-start.3
  74.7 4.5 %fusion.35 = (f32[256,128]{1,0:T(8,128)}, f32[8,256,128]{2,1,0:T(8,128)}) fusion(bf16[8,512,256]{2,1,0:T(8,128)(2,1)} %bitcast.146, bf16[8,512,128]{2,1,0:T(8,128)(2,1)S(1)} %bitcast.149), kind=kOutput, calls=%fused_computation.57 | convolution fusion | flops 268664832 | bytes 4325376 | tf_op jit(solution)/shard_map/bshf,bshd->bhfd/dot_general | solution.py:54
  79.2 0.0 copy-done.3
  79.2 0.0 all-gather.9.cloned.1.call-update
  79.2 0.0 all-gather.11.cloned.1.call-start
  79.3 2.6 %copy.104 = f32[8,512,1,128]{1,3,0,2:T(8,128)} copy(bf16[8,512,1,128]{3,1,0,2:T(8,128)(2,1)} %bitcast.166) | data formatting | bytes 3145728 | tf_op jit(solution)/shard_map/convert_element_type | solution.py:49
  81.8 0.1 fusion.29
  82.0 2.5 %convert_reduce_fusion = (f32[16,256]{1,0:T(8,128)S(1)}, f32[256]{0:T(256)S(1)}) fusion(bf16[256,16,256]{2,0,1:T(8,128)(2,1)} %copy-done), kind=kLoop, calls=%fused_computation.12 | loop fusion | flops 3141376 | bytes 2114560 | tf_op jit(solution)/shard_map/reduce_sum | solution.py:55
  84.6 11.0 %all-gather.4 = f32[8,1,256]{2,1,0:T(1,128)S(1)} all-gather(f32[1,1,256]{2,1,0:T(1,128)S(1)} %bitcast.173), channel_id=3, replica_groups=mesh['ctx'=8,'grp'=16] {'ctx'}, dimensions={0}, use_global_device_ids=true | all-gather | bytes 9216 | tf_op jit(solution)/shard_map/all_gather | solution.py:14
  95.6 5.3 %all-to-all-done = bf16[256,16,256]{2,0,1:T(8,128)(2,1)S(1)} async-done(((bf16[256,16,256]{2,0,1:T(8,128)(2,1)}), bf16[256,16,256]{2,0,1:T(8,128)(2,1)S(1)}, u32[]{:S(2)}, u32[]{:S(2)}) %all-to-all-start) | async-done | bytes 2097184 | tf_op jit(solution)/shard_map/all_to_all | solution.py:90
  100.9 6.1 %multiply_reduce_fusion = (f32[8,512]{1,0:T(8,128)S(1)}, f32[8,512,512]{1,2,0:T(8,128)}) fusion(f32[512,512]{0,1:T(8,128)S(1)} %fusion.29, bf16[8,512,256]{2,1,0:T(8,128)(2,1)S(1)} %bitcast.140, bf16[8,512,256]{2,1,0:T(8,128)(2,1)} %bitcast.147), kind=kOutput, calls=%fused_computation.7 | convolution fusion | flops 1077932032 | bytes 13647872 | tf_op jit(solution)/shard_map/bthf,bshf->bhts/dot_general | solution.py:53
  107.0 7.9 %while.34 = (s32[]{:T(128)}, f32[1,256,128]{2,1,0:T(8,128)S(1)}, f32[1,256]{1,0:T(1,128)S(1)}, s32[]{:T(128)}, f32[8,1,256,128]{3,2,1,0:T(8,128)}, /*index=5*/f32[8,1,256]{2,1,0:T(1,128)S(1)}, s32[]{:T(128)}, s32[]{:T(128)}) while((s32[]{:T(128)}, f32[1,256,128]{2,1,0:T(8,128)S(1)}, f32[1,256]{1,0:T(1,128)S(1)}, s32[]{:T(128)}, ...), condition=%wide.region_3.4_spmd.clone, body=%wide.region_2.0_spmd.clone.sunk | while | flops 99076 | bytes 396411 | solution.py:27
  107.0 0.9 add_select_fusion.4
  108.0 0.9 add_select_fusion.4
  109.0 0.9 add_select_fusion.4
  110.0 0.9 add_select_fusion.4
  111.0 0.9 add_select_fusion.4
  112.0 0.9 add_select_fusion.4
  113.0 0.9 add_select_fusion.4
  114.0 0.9 add_select_fusion.4
  114.9 0.0 copy-start.7
  115.0 0.0 copy-start.10
  115.0 1.7 fusion.32
  116.7 0.0 copy-done.7
  116.7 0.1 fusion.24
  116.9 2.3 fusion.37
  119.2 0.3 copy-done.4
  119.5 5.9 %fusion.20 = (f32[8,512]{1,0:T(8,128)S(1)}, f32[8,512,1,128]{1,3,0,2:T(8,128)S(1)}) fusion(f32[8,512,1,128]{1,3,0,2:T(8,128)} %copy.104, f32[8,512]{1,0:T(8,128)S(1)} %bitcast_add_fusion.3, f32[8,128,512]{2,1,0:T(8,128)S(1)} %fusion.37, bf16[8,512,128]{2,1,0:T(8,128)(2,1)S(1)} %bitcast.150, f32[8,512,512]{1,2,0:T(8,128)S(1)} %copy-done.10, ...), kind=kOutput, calls=%fused_computation.36 | convolution fusion | flops 3226464256 | bytes 16809984 | tf_op jit(solution)/shard_map/bhts,bshd->bthd/dot_general | solution.py:59
  125.3 0.0 copy-start.1
  125.4 5.7 %fusion.18 = f32[8,512,512]{1,2,0:T(8,128)} fusion(bf16[8,512,128]{2,1,0:T(8,128)(2,1)S(1)} %bitcast.151, f32[8,512,1,128]{1,3,0,2:T(8,128)S(1)} %get-tuple-element.358), kind=kOutput, calls=%fused_computation.32 | convolution fusion | flops 3221225472 | bytes 11534336 | tf_op jit(solution)/shard_map/bthd,bshd->bhts/dot_general | solution.py:67
  131.0 2.9 %fusion.36 = (f32[256,128]{0,1:T(8,128)}, f32[8,256,128]{1,2,0:T(8,128)}) fusion(bf16[8,512,256]{2,1,0:T(8,128)(2,1)S(1)} %bitcast.143, f32[8,512,1,128]{1,3,0,2:T(8,128)S(1)} %get-tuple-element.358), kind=kOutput, calls=%fused_computation.58 | convolution fusion | flops 1610842112 | bytes 5373952 | tf_op jit(solution)/shard_map/bthf,bthd->bhfd/dot_general | solution.py:69
  133.9 0.0 all-gather.11.cloned.1.call-update
  133.9 0.0 copy-start.2
  133.9 10.4 %fusion.3 = f32[8,512,256]{2,1,0:T(8,128)S(1)} fusion(bf16[8,512,256]{2,1,0:T(8,128)(2,1)} %bitcast.148, f32[8,512,512]{1,2,0:T(8,128)} %fusion.18, f32[8,512]{1,0:T(8,128)S(1)} %negate_divide_fusion, f32[512,512]{0,1:T(8,128)S(1)} %fusion.29), kind=kOutput, calls=%fused_computation.11 | convolution fusion | flops 6446645248 | bytes 15745024 | tf_op jit(solution)/shard_map/bhts,bshf->bthf/dot_general | solution.py:74
  144.4 5.6 %fusion.9 = bf16[8,512,1,256]{3,1,0,2:T(8,128)(2,1)} fusion(f32[8,512,256]{2,1,0:T(8,128)S(1)} %fusion.3, f32[8,256,128]{2,1,0:T(8,128)S(1)} %copy-done.9, f32[8,512,1,128]{1,3,0,2:T(8,128)S(1)} %copy-done.2, f32[8,512]{1,0:T(8,128)S(1)} %negate_divide_fusion, f32[8,256]{1,0:T(8,128)S(1)} %subtract_add_fusion.1), kind=kOutput, calls=%fused_computation.21 | convolution fusion | flops 1615855616 | bytes 9461760 | tf_op jit(solution)/shard_map/bhfd,bthd->bthf/dot_general | solution.py:75
  150.0 4.5 %all-to-all-start.3 = ((bf16[16,256,256]{2,1,0:T(8,128)(2,1)}), bf16[16,256,256]{2,1,0:T(8,128)(2,1)}, u32[]{:S(2)}, u32[]{:S(2)}) async-start(bf16[16,256,256]{2,1,0:T(8,128)(2,1)} %bitcast.157), calls=%async_computation.3 | async-start | bytes 4194304 | tf_op jit(solution)/shard_map/all_to_all | solution.py:108
  154.4 0.9 fusion.30
  155.4 10.8 %all-gather.5 = f32[8,1,256]{2,1,0:T(1,128)S(1)} all-gather(f32[1,1,256]{2,1,0:T(1,128)S(1)} %bitcast.174), channel_id=5, replica_groups=mesh['ctx'=8,'grp'=16] {'ctx'}, dimensions={0}, use_global_device_ids=true | all-gather | bytes 9216 | tf_op jit(solution)/shard_map/all_gather | solution.py:14
  166.2 9.7 %fusion.2 = f32[8,512,256]{2,1,0:T(8,128)} fusion(bf16[8,512,256]{2,1,0:T(8,128)(2,1)S(1)} %bitcast.145, f32[8,512,512]{1,2,0:T(8,128)} %fusion.18, f32[8,512]{1,0:T(8,128)S(1)} %negate_divide_fusion, f32[512,512]{0,1:T(8,128)S(1)} %fusion.29), kind=kOutput, calls=%fused_computation.10 | convolution fusion | flops 6446645248 | bytes 15745024 | tf_op jit(solution)/shard_map/bhts,bthf->bshf/dot_general | solution.py:77
  176.0 1.6 copy.129
  177.6 1.0 while.35
  178.6 0.1 copy.111
  178.7 0.3 fusion.25
  179.0 0.8 copy-done.5
  179.8 5.7 %fusion.6 = bf16[8,512,1,256]{3,1,0,2:T(8,128)(2,1)} fusion(f32[8,512,256]{2,1,0:T(8,128)} %fusion.2, f32[8,256,128]{1,2,0:T(8,128)S(1)} %fusion.25, bf16[8,512,128]{2,1,0:T(8,128)(2,1)S(1)} %bitcast.152, f32[8,256]{1,0:T(8,128)S(1)} %subtract_add_fusion), kind=kOutput, calls=%fused_computation.17 | convolution fusion | flops 1614807040 | bytes 8396800 | tf_op jit(solution)/shard_map/bhfd,bshd->bshf/dot_general | solution.py:78
  185.5 0.0 all-to-all-done.3
  185.5 7.1 %all-to-all-start.4 = ((bf16[16,256,256]{2,1,0:T(8,128)(2,1)}), bf16[16,256,256]{2,1,0:T(8,128)(2,1)S(1)}, u32[]{:S(2)}, u32[]{:S(2)}) async-start(bf16[16,256,256]{2,1,0:T(8,128)(2,1)} %bitcast.153), calls=%async_computation.4 | async-start | bytes 4194304 | tf_op jit(solution)/shard_map/all_to_all | solution.py:109
  192.6 3.2 %copy.133 = bf16[16,32,8,256]{3,2,0,1:T(8,128)(2,1)} copy(bf16[16,32,8,256]{3,2,1,0:T(8,128)(2,1)} %bitcast.54) | data formatting | bytes 4194304 | tf_op jit(solution)/shard_map/all_to_all | solution.py:108
  195.8 27.6 %all-to-all-done.4 = bf16[16,256,256]{2,1,0:T(8,128)(2,1)S(1)} async-done(((bf16[16,256,256]{2,1,0:T(8,128)(2,1)}), bf16[16,256,256]{2,1,0:T(8,128)(2,1)S(1)}, u32[]{:S(2)}, u32[]{:S(2)}) %all-to-all-start.4) | async-done | bytes 2097184 | tf_op jit(solution)/shard_map/all_to_all | solution.py:109
  223.4 1.6 copy.134
  (53 shorter events, 0.8 us)
Async XLA Ops:
  7.2 10.4 %copy-start.12 = (bf16[256,4096]{1,0:T(8,128)(2,1)S(1)}, bf16[256,4096]{1,0:T(8,128)(2,1)}, u32[]{:S(2)}) copy-start(bf16[256,4096]{1,0:T(8,128)(2,1)} %param.9) | copy-start | bytes 6291460
  9.6 25.7 %all-to-all-start.2 = ((bf16[256,16,128]{0,2,1:T(8,128)(2,1)}), bf16[256,16,128]{0,2,1:T(8,128)(2,1)S(1)}, u32[]{:S(2)}, u32[]{:S(2)}) async-start(bf16[256,16,128]{0,2,1:T(8,128)(2,1)} %bitcast.4), calls=%async_computation.2 | async-start | bytes 2097152 | tf_op jit(solution)/shard_map/all_to_all | solution.py:92
  35.3 1.0 copy-start.11
  36.3 31.6 %all-to-all-start.1 = ((bf16[256,16,256]{2,0,1:T(8,128)(2,1)}), bf16[256,16,256]{2,0,1:T(8,128)(2,1)S(1)}, u32[]{:S(2)}, u32[]{:S(2)}) async-start(bf16[256,16,256]{2,0,1:T(8,128)(2,1)} %bitcast.156), calls=%async_computation.1 | async-start | bytes 4194304 | tf_op jit(solution)/shard_map/all_to_all | solution.py:91
  67.9 1.3 copy-start
  69.2 31.7 %all-to-all-start = ((bf16[256,16,256]{2,0,1:T(8,128)(2,1)}), bf16[256,16,256]{2,0,1:T(8,128)(2,1)S(1)}, u32[]{:S(2)}, u32[]{:S(2)}) async-start(bf16[256,16,256]{2,0,1:T(8,128)(2,1)} %bitcast.154), calls=%async_computation | async-start | bytes 4194304 | tf_op jit(solution)/shard_map/all_to_all | solution.py:90
  73.0 34.1 %all-gather.9.cloned.1.call-start = ((), (), s32[]{:S(2)}) async-start(), calls=%async_computation.5 | async-start | bytes 1179648 | tf_op jit(solution)/shard_map/all_gather | solution.py:14
  74.6 4.5 %copy-start.3 = (bf16[16,256,128]{2,1,0:T(8,128)(2,1)}, bf16[16,256,128]{2,1,0:T(8,128)(2,1)S(1)}, u32[]{:S(2)}) copy-start(bf16[16,256,128]{2,1,0:T(8,128)(2,1)S(1)} %copy.98) | copy-start | bytes 3145732
  79.2 96.8 %all-gather.11.cloned.1.call-start = ((), (), s32[]{:S(2)}) async-start(), calls=%async_computation.6 | async-start | bytes 1179648 | tf_op jit(solution)/shard_map/all_gather | solution.py:14
  114.9 1.8 copy-start.7
  115.0 4.2 %copy-start.10 = (f32[8,512,512]{1,2,0:T(8,128)S(1)}, f32[8,512,512]{1,2,0:T(8,128)}, u32[]{:S(2)}) copy-start(f32[8,512,512]{1,2,0:T(8,128)} %get-tuple-element.362) | copy-start | bytes 25165828
  116.8 2.3 %copy-start.8 = (f32[8,256,128]{2,1,0:T(8,128)}, f32[8,256,128]{2,1,0:T(8,128)S(1)}, u32[]{:S(2)}) copy-start(f32[8,256,128]{2,1,0:T(8,128)S(1)} %fusion.24) | copy-start | bytes 3145732
  116.8 2.6 %copy-start.4 = (bf16[16,256,128]{2,1,0:T(8,128)(2,1)S(1)}, bf16[16,256,128]{2,1,0:T(8,128)(2,1)}, u32[]{:S(2)}) copy-start(bf16[16,256,128]{2,1,0:T(8,128)(2,1)} %copy-done.3) | copy-start | bytes 3145732
  125.3 5.7 %copy-start.1 = (f32[8,512,1,128]{1,3,0,2:T(8,128)}, f32[8,512,1,128]{1,3,0,2:T(8,128)S(1)}, u32[]{:S(2)}) copy-start(f32[8,512,1,128]{1,3,0,2:T(8,128)S(1)} %get-tuple-element.358) | copy-start | bytes 6291460
  133.9 10.5 %copy-start.2 = (f32[8,512,1,128]{1,3,0,2:T(8,128)S(1)}, f32[8,512,1,128]{1,3,0,2:T(8,128)}, u32[]{:S(2)}) copy-start(f32[8,512,1,128]{1,3,0,2:T(8,128)} %copy-done.1) | copy-start | bytes 6291460
  133.9 10.5 %copy-start.9 = (f32[8,256,128]{2,1,0:T(8,128)S(1)}, f32[8,256,128]{2,1,0:T(8,128)}, u32[]{:S(2)}) copy-start(f32[8,256,128]{2,1,0:T(8,128)} %copy-done.8) | copy-start | bytes 3145732
  150.0 35.6 %all-to-all-start.3 = ((bf16[16,256,256]{2,1,0:T(8,128)(2,1)}), bf16[16,256,256]{2,1,0:T(8,128)(2,1)}, u32[]{:S(2)}, u32[]{:S(2)}) async-start(bf16[16,256,256]{2,1,0:T(8,128)(2,1)} %bitcast.157), calls=%async_computation.3 | async-start | bytes 4194304 | tf_op jit(solution)/shard_map/all_to_all | solution.py:108
  175.9 2.8 %copy-start.6 = (f32[8,256,128]{1,2,0:T(8,128)S(1)}, f32[8,256,128]{1,2,0:T(8,128)}, u32[]{:S(2)}) copy-start(f32[8,256,128]{1,2,0:T(8,128)} %get-tuple-element.364) | copy-start | bytes 3145732
  178.6 1.2 copy-start.5
  185.5 37.9 %all-to-all-start.4 = ((bf16[16,256,256]{2,1,0:T(8,128)(2,1)}), bf16[16,256,256]{2,1,0:T(8,128)(2,1)S(1)}, u32[]{:S(2)}, u32[]{:S(2)}) async-start(bf16[16,256,256]{2,1,0:T(8,128)(2,1)} %bitcast.153), calls=%async_computation.4 | async-start | bytes 4194304 | tf_op jit(solution)/shard_map/all_to_all | solution.py:109
Sparse Core Ops, SparseCore 0:
  79.3 24.9 all-gather.8
  134.0 21.5 all-gather.10
where the time goes:
time: 233 us; the launch traced here: 232 us
  waiting for transfers between devices  73.9 us (32%)
  matrix products  61.3 us (26%)
  starting transfers between devices  27.1 us (12%)
  blocking collectives  21.8 us (9%)
  local copies, waits for them, and re-layouts  21.2 us (9%)
  between operations  14.4 us (6%)
  other arithmetic  11.3 us (5%)
    all_to_all x1, waiting for transfers between devices, on_device(): lax.all_to_all(key_head, 'grp', split_axis=0, concat_axis=1, tiled=True)  27.6 us
    all_to_all x1, waiting for transfers between devices, on_device(): lax.all_to_all(key_feat, 'grp', split_axis=1, concat_axis=0, tiled=True)  24.7 us
    all_gather x2, blocking collectives, entering(): everything = jax.tree.map(lambda part: lax.all_gather(part, axis), array)  21.8 us
    all_to_all x1, waiting for transfers between devices, on_device(): lax.all_to_all(values, 'grp', split_axis=1, concat_axis=0, tiled=True)  16.2 us
    dot_general x1, matrix products, local_grads(): q_grad = jnp.einsum('bhts,bshf->bthf', mixed, fk_wide, precision=HIGH)  10.4 us
    dot_general x1, matrix products, local_grads(): k_grad = jnp.einsum('bhts,bthf->bshf', mixed, fq_wide, precision=HIGH)  9.71 us
    select_n x32, other arithmetic, step(): return jax.tree.map(lambda a, b: jnp.where(reached, a, b), new, before)  8.17 us
    all_to_all x1, starting transfers between devices, on_device(): lax.all_to_all(values, 'grp', split_axis=1, concat_axis=0, tiled=True)  7.99 us
  transfers between devices with their start and end apart: 7, of which 4 were waited for; matrix products, arithmetic and copies ran while one was open for 26% of the time, Pallas kernels for 0%

commit v1 on v0

v1 whole, which is shorter than its diff:
```python
import functools

import jax
import jax.numpy as jnp
from jax import lax
from jax.experimental import pallas as pl
from jax.experimental.pallas import tpu as pltpu
from jax.sharding import PartitionSpec as P


NX, NZ, NY = 4, 4, 4
HL = 4
TB = 256
F = 256
D = 128
SR = D + 8
BF, F32 = jnp.bfloat16, jnp.float32
VMEM_LIMIT = 8 * 1024 * 1024


def grp_pairs(dx, dz):
    return [(x * NZ + z, ((x + dx) % NX) * NZ + (z + dz) % NZ) for x in range(NX) for z in range(NZ)]


def y_pairs(d):
    return [(y * 2 + c, ((y + d) % NY) * 2 + c) for y in range(NY) for c in range(2)]


CORE_PAIRS = [(y * 2 + c, y * 2 + 1 - c) for y in range(NY) for c in range(2)]


def params():
    return pltpu.CompilerParams(vmem_limit_bytes=VMEM_LIMIT)


def nn(a, b):
    return lax.dot_general(a, b, (((1,), (0,)), ((), ())), preferred_element_type=F32)


def nt(a, b):
    return lax.dot_general(a, b, (((1,), (1,)), ((), ())), preferred_element_type=F32)


def tn(a, b):
    return lax.dot_general(a, b, (((0,), (0,)), ((), ())), preferred_element_type=F32)


def split(x):
    hi = x.astype(BF)
    return hi, (x - hi.astype(F32)).astype(BF)


def mod4(a):
    return lax.rem(a + 8, 4)


def vmem(n):
    return [pl.BlockSpec(memory_space=pltpu.VMEM)] * n


def hbm(n):
    return [pl.BlockSpec(memory_space=pltpu.HBM)] * n


def place():
    return [pl.BlockSpec(memory_space=pltpu.SMEM)]


def shape(*dims, kind=F32):
    return jax.ShapeDtypeStruct(dims, kind)


def piece(cols):
    return shape(HL, TB, cols, kind=BF)


def call(kernel, out_shape, in_specs, out_specs, args, scratch=()):
    return pl.pallas_call(
        kernel,
        out_shape=out_shape,
        in_specs=in_specs,
        out_specs=out_specs,
        scratch_shapes=list(scratch),
        compiler_params=params(),
    )(*args)


def run_copies(copies):
    for c in copies:
        c.start()
    for c in copies:
        c.wait()


def pack_kv_kernel(shifts, pos, k_ref, v_ref, *refs):
    outs, sem = refs[:-1], refs[-1]
    z = pos[1]
    copies = []
    for i, r in enumerate(shifts):
        zd = mod4(z + r)
        for j in range(HL):
            kc = pl.ds(pl.multiple_of((j * NZ + zd) * F, F), F)
            vc = pl.ds(pl.multiple_of((j * NZ + zd) * D, D), D)
            copies.append(pltpu.make_async_copy(k_ref.at[:, kc], outs[i].at[j, :, 0:F], sem.at[i, j, 0]))
            copies.append(pltpu.make_async_copy(v_ref.at[:, vc], outs[i].at[j, :, F : F + D], sem.at[i, j, 1]))
    run_copies(copies)


def pack_kv(pos, k, v, shifts):
    n = len(shifts)
    return call(
        functools.partial(pack_kv_kernel, shifts),
        [piece(F + D)] * n,
        place() + hbm(2),
        vmem(n),
        (pos, k, v),
        [pltpu.SemaphoreType.DMA((n, HL, 2))],
    )


def pack_q_kernel(shifts, pos, q_ref, *refs):
    outs, sem = refs[:-1], refs[-1]
    z = pos[1]
    copies = []
    for i, r in enumerate(shifts):
        for j in range(HL):
            qc = pl.ds(pl.multiple_of((j * NZ + mod4(z + r)) * F, F), F)
            copies.append(pltpu.make_async_copy(q_ref.at[:, qc], outs[i].at[j], sem.at[i, j]))
    run_copies(copies)


def pack_q(pos, q, shifts):
    n = len(shifts)
    return call(
        functools.partial(pack_q_kernel, shifts),
        [piece(F)] * n,
        place() + hbm(1),
        vmem(n),
        (pos, q),
        [pltpu.SemaphoreType.DMA((n, HL))],
    )


def pack_teacher_kernel(pos, t_ref, *refs):
    outs, sem = refs[:-1], refs[-1]
    n = NZ * TB
    copies = []
    for r in range(NX):
        rows = pl.ds(pl.multiple_of(mod4(pos[0] + r) * n, n), n)
        copies.append(pltpu.make_async_copy(t_ref.at[rows, :], outs[r], sem.at[r]))
    run_copies(copies)


def pack_teacher(pos, teacher):
    return call(
        pack_teacher_kernel,
        [shape(NZ * TB, D, kind=BF)] * NX,
        place() + hbm(1),
        vmem(NX),
        (pos, teacher),
        [pltpu.SemaphoreType.DMA((NX,))],
    )


def unpack_kernel(pos, *refs):
    parts, out = refs[0:NZ], refs[NZ]
    z = pos[1]
    for r in (0, 2, 1, 3):
        for j in range(HL):
            out[:, pl.ds(pl.multiple_of((j * NZ + mod4(z - r)) * F, F), F)] = parts[r][j]


def unpack_all(pos, parts):
    return call(
        unpack_kernel,
        shape(TB, HL * NZ * F, kind=BF),
        place() + vmem(NZ),
        pl.BlockSpec(),
        (pos, *parts),
    )


def block_state(k, v):
    return jnp.concatenate([tn(v, k), nn(jnp.ones((8, TB), BF), k)], axis=0)


def sums_a_kernel(pos, kv0, kv2, out):
    for r in range(NX):
        hd = mod4(pos[0] + r)
        acc = jnp.zeros((SR, F), F32)
        for kv in (kv0, kv2):
            acc = acc + block_state(kv[hd, :, 0:F], kv[hd, :, F : F + D])
        out[r] = acc


def sums_a(pos, kv0, kv2):
    return call(sums_a_kernel, shape(NX, SR, F), place() + vmem(2), vmem(1)[0], (pos, kv0, kv2))


def sums_b_kernel(pos, kv1, kv3, part, *outs):
    for r in range(NX):
        hd = mod4(pos[0] + r)
        acc = part[r]
        for kv in (kv1, kv3):
            acc = acc + block_state(kv[hd, :, 0:F], kv[hd, :, F : F + D])
        outs[r][...] = acc


def sums_b(pos, kv1, kv3, part):
    return call(
        sums_b_kernel, [shape(SR, F)] * NX, place() + vmem(3), vmem(NX), (pos, kv1, kv3, part)
    )


def full_state(ref):
    return jnp.concatenate([ref[0:D, :], jnp.broadcast_to(ref[D : D + 1, :], (D, F))], axis=0)


def augmented(v):
    return jnp.concatenate([v, jnp.ones((TB, D), BF)], axis=1)


def causal_mask():
    t = lax.broadcasted_iota(jnp.int32, (TB, TB), 0)
    s = lax.broadcasted_iota(jnp.int32, (TB, TB), 1)
    return s <= t


def order_sums(z, parts, reverse):
    out = []
    for b in range(NZ):
        acc = jnp.zeros(parts[0].shape, F32)
        for o in range(NZ):
            if o == b:
                continue
            mine, other = mod4(z - b), mod4(z - o)
            take = (other > mine) if reverse else (other < mine)
            acc = acc + parts[o] * take.astype(F32)
        out.append(acc)
    return out


def rows_of(x):
    return jnp.concatenate(split(x), axis=0)


def halves(x):
    n = x.shape[0] // 2
    return x[:n] + x[n:]


def lines_kernel(pos, *refs):
    kvs, l_out = refs[0:4], refs[4]
    x, z = pos[0], pos[1]
    for r in range(HL):
        hd = mod4(x - r)
        parts = [block_state(kvs[b][hd, :, 0:F], kvs[b][hd, :, F : F + D]) for b in range(NZ)]
        for b, line in enumerate(order_sums(z, parts, False)):
            l_out[r, b] = line


def earlier_in_line(pos, kvs):
    return call(lines_kernel, shape(HL, NZ, SR, F), place() + vmem(4), vmem(1)[0], (pos, *kvs))


def pre_kernel(pos, *refs):
    kvs, qs, lines, nd_out = refs[0:4], refs[4:8], refs[8], refs[9]
    x = pos[0]
    mask = causal_mask()
    for r in range(HL):
        hd = mod4(x - r)
        for b in range(NZ):
            q, k = qs[b][hd], kvs[b][hd, :, 0:F]
            va = augmented(kvs[b][hd, :, F : F + D])
            st_hi, st_lo = split(full_state(lines[r, b]))
            sc = rows_of(jnp.where(mask, nt(q, k), 0.0))
            nd_out[r, b] = halves(nn(sc, va)) + nt(q, st_hi) + nt(q, st_lo)


def pre(pos, kvs, qs, lines):
    return call(
        pre_kernel, shape(HL, NZ, TB, 2 * D), place() + vmem(9), vmem(1)[0], (pos, *kvs, *qs, lines)
    )


def post_kernel(pos, *refs):
    qs, nd, teas, states = refs[0:4], refs[4], refs[5:9], refs[9:13]
    dhi_out, dlo_out, adj_out, sums = refs[13], refs[14], refs[15], refs[16:20]
    x, z = pos[0], pos[1]
    for r in range(HL):
        hd = mod4(x - r)
        e_hi, e_lo = split(full_state(states[r]))
        total = jnp.zeros((SR, F), F32)
        for b in range(NZ):
            q = qs[b][hd]
            both = nd[r, b] + nt(q, e_hi) + nt(q, e_lo)
            inverse = 1.0 / both[:, D:]
            student = both[:, 0:D] * inverse
            rows = pl.ds(pl.multiple_of(mod4(z - b) * TB, TB), TB)
            resid = student - teas[r][rows, :].astype(F32)
            dn = resid * inverse
            dd = -jnp.sum(resid * student, axis=1, keepdims=True) * inverse
            d_hi, d_lo = split(jnp.concatenate([dn, dd * (1.0 / D)], axis=1))
            dhi_out[r, b] = d_hi
            dlo_out[r, b] = d_lo
            adj = tn(d_hi, q)[0:SR] + tn(d_lo, q)[0:SR]
            adj_out[r, b] = adj
            total = total + adj
        sums[(-r) % NX][...] = total


def post(pos, qs, nd, teas, states):
    out = call(
        post_kernel,
        [shape(HL, NZ, TB, 2 * D, kind=BF)] * 2 + [shape(HL, NZ, SR, F)] + [shape(SR, F)] * NX,
        place() + vmem(13),
        vmem(3 + NX),
        (pos, *qs, nd, *teas, *states),
    )
    return out[0], out[1], out[2], out[3:7]


def qgrad_kernel(scale, pos, *refs):
    kvs, dhi, dlo, lines, states, outs = refs[0:4], refs[4], refs[5], refs[6], refs[7:11], refs[11:15]
    x = pos[0]
    mask = causal_mask()
    for r in range(HL):
        hd = mod4(x - r)
        for b in range(NZ):
            k = kvs[b][hd, :, 0:F]
            va = augmented(kvs[b][hd, :, F : F + D])
            d_hi = dhi[r, b]
            d_rows = jnp.concatenate([d_hi, dlo[r, b]], axis=0)
            mixed = rows_of(jnp.where(mask, halves(nt(d_rows, va)), 0.0))
            st_hi, st_lo = split(full_state(states[r][...] + lines[r, b]))
            qg = halves(nn(mixed, k) + nn(d_rows, st_hi)) + nn(d_hi, st_lo)
            outs[(-b) % NZ][hd] = (qg * scale).astype(BF)


def qgrad(pos, kvs, dhi, dlo, lines, states, scale):
    return call(
        functools.partial(qgrad_kernel, scale),
        [piece(F)] * NZ,
        place() + vmem(11),
        vmem(NZ),
        (pos, *kvs, dhi, dlo, lines, *states),
    )


def inner_kernel(pos, *refs):
    kvs, qs, dhi, dlo, adj, out = refs[0:4], refs[4:8], refs[8], refs[9], refs[10], refs[11]
    x, z = pos[0], pos[1]
    mask = causal_mask()
    for r in range(HL):
        hd = mod4(x - r)
        lines = order_sums(z, [adj[r, b] for b in range(NZ)], True)
        for b in range(NZ):
            q = qs[b][hd]
            va = augmented(kvs[b][hd, :, F : F + D])
            d_rows = jnp.concatenate([dhi[r, b], dlo[r, b]], axis=0)
            m_hi, m_lo = split(jnp.where(mask, halves(nt(d_rows, va)), 0.0))
            a_hi, a_lo = split(full_state(lines[b]))
            out[r, b] = tn(m_hi, q) + tn(m_lo, q) + nn(va, a_hi) + nn(va, a_lo)


def inner(pos, kvs, qs, dhi, dlo, adj):
    return call(
        inner_kernel,
        shape(HL, NZ, TB, F),
        place() + vmem(11),
        vmem(1)[0],
        (pos, *kvs, *qs, dhi, dlo, adj),
    )


def last_kernel(scale, blocks, pos, *refs):
    n = len(blocks)
    kvs, part, states, outs = refs[0:n], refs[n], refs[n + 1 : n + 5], refs[n + 5 :]
    x = pos[0]
    for r in range(HL):
        hd = mod4(x - r)
        a_hi, a_lo = split(full_state(states[r]))
        for i, b in enumerate(blocks):
            va = augmented(kvs[i][hd, :, F : F + D])
            kg = part[r, b] + nn(va, a_hi) + nn(va, a_lo)
            outs[i][hd] = (kg * scale).astype(BF)


def last(pos, kvs, part, states, scale, blocks):
    n = len(blocks)
    return call(
        functools.partial(last_kernel, scale, blocks),
        [piece(F)] * n,
        place() + vmem(n + 5),
        vmem(n),
        (pos, *[kvs[b] for b in blocks], part, *states),
    )


def send_z(part, r):
    return lax.ppermute(part, "grp", grp_pairs(0, r))


def send_x(part, r):
    return lax.ppermute(part, "grp", grp_pairs(r, 0))


def exchange_z(parts):
    far, up, down = send_z(parts[2], 2), send_z(parts[1], 1), send_z(parts[3], 3)
    return [parts[0], up, far, down]


def exchange_x(parts):
    far, up, down = send_x(parts[2], 2), send_x(parts[1], 1), send_x(parts[3], 3)
    return [parts[0], up, far, down]


def total_kernel(m0, m1, m2, m3, out):
    out[...] = (m0[...] + m1[...]) + (m2[...] + m3[...])


def core_kernel(reverse, pos, o1, o2, o3, total, outer, other):
    y, c = pos[2], pos[3]
    acc = jnp.zeros((SR, F), F32)
    for d, o in ((1, o1), (2, o2), (3, o3)):
        at = mod4(y - d)
        take = (at > y) if reverse else (at < y)
        acc = acc + o[...] * take.astype(F32)
    outer[...] = acc
    first = (c == (1 if reverse else 0)).astype(F32)
    other[...] = acc + total[...] * first


def back_kernel(reverse, pos, outer, other_core, *refs):
    mine, outs = refs[0:NX], refs[NX:]
    x = pos[0]
    base = outer[...] + other_core[...]
    for r in range(NX):
        to = mod4(x + r)
        acc = base
        for s in range(NX):
            at = mod4(x - s)
            take = (at > to) if reverse else (at < to)
            acc = acc + mine[s][...] * take.astype(F32)
        outs[r][...] = acc


def scan_states(sums, pos, reverse):
    one = shape(SR, F)
    mine = exchange_x(sums)
    total = call(total_kernel, one, vmem(4), vmem(1)[0], mine)
    others = [lax.ppermute(total, "ctx", y_pairs(d)) for d in (1, 2, 3)]
    outer, mixed = call(
        functools.partial(core_kernel, reverse), [one] * 2, place() + vmem(4), vmem(2), (pos, *others, total)
    )
    other_core = lax.ppermute(mixed, "ctx", CORE_PAIRS)
    back = call(
        functools.partial(back_kernel, reverse),
        [one] * NX,
        place() + vmem(2 + NX),
        vmem(NX),
        (pos, outer, other_core, *mine),
    )
    return exchange_x(back)


def local_step(query_feat, key_feat, values, teacher):
    total_tokens = query_feat.shape[0] * lax.axis_size("ctx") * lax.axis_size("grp")
    scale = float(total_tokens) ** 0.5
    g = lax.axis_index("grp").astype(jnp.int32)
    x, z = g // NZ, lax.rem(g, NZ)
    t = lax.axis_index("ctx").astype(jnp.int32)
    pos = jnp.stack([x, z, t // 2, lax.rem(t, 2)])
    query_feat, key_feat, values, teacher = (
        pltpu.with_memory_space_constraint(a, pltpu.HBM) for a in (query_feat, key_feat, values, teacher)
    )
    kv = [None] * NZ
    kv[2], kv[1], kv[3] = pack_kv(pos, key_feat, values, (2, 1, 3))
    (kv[0],) = pack_kv(pos, key_feat, values, (0,))
    kvs = exchange_z(kv)
    q = [None] * NZ
    q[2], q[1], q[3] = pack_q(pos, query_feat, (2, 1, 3))
    (q[0],) = pack_q(pos, query_feat, (0,))
    qs = exchange_z(q)
    teas = exchange_x(pack_teacher(pos, teacher))
    sums = sums_b(pos, kvs[1], kvs[3], sums_a(pos, kvs[0], kvs[2]))
    lines = earlier_in_line(pos, kvs)
    nd = pre(pos, kvs, qs, lines)
    states = scan_states(sums, pos, False)
    d_hi, d_lo, adj, adj_sums = post(pos, qs, nd, teas, states)
    qparts = qgrad(pos, kvs, d_hi, d_lo, lines, states, scale)
    query_grad = unpack_all(pos, exchange_z(qparts))
    part = inner(pos, kvs, qs, d_hi, d_lo, adj)
    after = scan_states(adj_sums, pos, True)
    kg = [None] * NZ
    (kg[2],) = last(pos, kvs, part, after, scale, (2,))
    kg[3], kg[1] = last(pos, kvs, part, after, scale, (1, 3))
    (kg[0],) = last(pos, kvs, part, after, scale, (0,))
    key_grad = unpack_all(pos, exchange_z(kg))
    return query_grad, key_grad


def solution(mesh):
    placed = (
        P(("ctx", "grp"), None),
        P(("ctx", "grp"), None),
        P(("ctx", "grp"), None),
        P("ctx", "grp"),
    )
    return jax.shard_map(
        local_step,
        mesh=mesh,
        in_specs=placed,
        out_specs=(P(("ctx", "grp"), None), P(("ctx", "grp"), None)),
        check_vma=False,
    )
```

time: 233 us -> 178 us (0.76)
  the two profiles are of different devices: /device:TPU:0 before, /device:TPU:34 now
where the time goes in v1:
time: 178 us
  waiting for transfers between devices  83.4 us (47%)
  starting transfers between devices  51.1 us (29%)
  Pallas kernels  42.5 us (24%)
    ppermute x12, waiting for transfers between devices, send_z(): return lax.ppermute(part, 'grp', grp_pairs(0, r))  64.2 us
    pallas_call x23, Pallas kernels, call(): pl.pallas_call(kernel, out_shape=out_shape, in_specs=in_specs, out_specs=...  42.5 us
    ppermute x15, starting transfers between devices, send_x(): return lax.ppermute(part, 'grp', grp_pairs(r, 0))  23.7 us
    ppermute x12, starting transfers between devices, send_z(): return lax.ppermute(part, 'grp', grp_pairs(0, r))  18.1 us
    ppermute x15, waiting for transfers between devices, send_x(): return lax.ppermute(part, 'grp', grp_pairs(r, 0))  9.58 us
    ppermute x6, starting transfers between devices, scan_states(): others = [lax.ppermute(total, 'ctx', y_pairs(d)) for d in (1, 2, 3)]  9.07 us
    ppermute x6, waiting for transfers between devices, scan_states(): others = [lax.ppermute(total, 'ctx', y_pairs(d)) for d in (1, 2, 3)]  8.33 us
  transfers between devices with their start and end apart: 35, of which 18 were waited for; matrix products, arithmetic and copies ran while one was open for 0% of the time, Pallas kernels for 18%

profile of v1, /device:TPU:34, one launch (start us, length us, event | category | flops | bytes accessed | tf_op | source)
XLA Modules:
  0.0 178.0 jit_solution(12733197816841355384)
XLA Ops:
  0.7 2.5 %shard_map.60 = (bf16[4,256,384]{2,1,0:T(8,128)(2,1)S(1)}, bf16[4,256,384]{2,1,0:T(8,128)(2,1)S(1)}, bf16[4,256,384]{2,1,0:T(8,128)(2,1)S(1)}) custom-call(s32[4]{0:T(128)S(1)} %pad_add_fusion.pos, bf16[256,4096]{1,0:T(8,128)(2,1)} %k_ref.3, bf16[256,2048]{1,0:T(8,128)(2,1)} %v_ref.3), custom_call_target="tpu_custom_call" | custom-call | tf_op jit(solution)/shard_map/pallas_call | solution.py:78
  3.2 3.1 %collective-permute-start.1 = (bf16[4,256,384]{2,1,0:T(8,128)(2,1)S(1)}, bf16[4,256,384]{2,1,0:T(8,128)(2,1)S(1)}, u32[]{:S(2)}, u32[]{:S(2)}) collective-permute-start(bf16[4,256,384]{2,1,0:T(8,128)(2,1)S(1)} %get-tuple-element.42), channel_id=1, source_target_pairs={{0,2},{1,3},{2,0},{3,1},{4,6},{5,7},{6,4},{7,5},{8,10},{9,11},{10,... | collective-permute-start | bytes 2359304 | tf_op jit(solution)/shard_map/ppermute | solution.py:401
  6.3 2.0 %collective-permute-start.2 = (bf16[4,256,384]{2,1,0:T(8,128)(2,1)S(1)}, bf16[4,256,384]{2,1,0:T(8,128)(2,1)S(1)}, u32[]{:S(2)}, u32[]{:S(2)}) collective-permute-start(bf16[4,256,384]{2,1,0:T(8,128)(2,1)S(1)} %get-tuple-element.43), channel_id=1, source_target_pairs={{0,3},{1,0},{2,1},{3,2},{4,7},{5,4},{6,5},{7,6},{8,11},{9,8},{10,9... | collective-permute-start | bytes 2359304 | tf_op jit(solution)/shard_map/ppermute | solution.py:401
  8.3 1.8 %shard_map.59.refs_0_.kv0 = bf16[4,256,384]{2,1,0:T(8,128)(2,1)S(1)} custom-call(s32[4]{0:T(128)S(1)} %pad_add_fusion.pos, bf16[256,4096]{1,0:T(8,128)(2,1)} %k_ref.3, bf16[256,2048]{1,0:T(8,128)(2,1)} %v_ref.3), custom_call_target="tpu_custom_call" | custom-call | tf_op jit(solution)/shard_map/pallas_call | solution.py:78
  10.1 15.1 %collective-permute-done.1.refs_2_.kv2.refs_0_ = bf16[4,256,384]{2,1,0:T(8,128)(2,1)S(1)} collective-permute-done((bf16[4,256,384]{2,1,0:T(8,128)(2,1)S(1)}, bf16[4,256,384]{2,1,0:T(8,128)(2,1)S(1)}, u32[]{:S(2)}, u32[]{:S(2)}) %collective-permute-start.1) | collective-permute-done | bytes 786464 | tf_op jit(solution)/shard_map/ppermute | solution.py:401
  25.3 1.0 shard_map.66.part
  26.2 15.2 %collective-permute-done.refs_1_.kv1.refs_0_ = bf16[4,256,384]{2,1,0:T(8,128)(2,1)S(1)} collective-permute-done((bf16[4,256,384]{2,1,0:T(8,128)(2,1)S(1)}, bf16[4,256,384]{2,1,0:T(8,128)(2,1)S(1)}, u32[]{:S(2)}, u32[]{:S(2)}) %collective-permute-start) | collective-permute-done | bytes 786464 | tf_op jit(solution)/shard_map/ppermute | solution.py:401
  41.4 1.0 shard_map.67
  42.4 1.6 collective-permute-start.9
  44.0 1.1 collective-permute-start.10
  45.1 2.2 %collective-permute-start.11 = (f32[136,256]{1,0:T(8,128)S(1)}, f32[136,256]{1,0:T(8,128)S(1)}, u32[]{:S(2)}, u32[]{:S(2)}) collective-permute-start(f32[136,256]{1,0:T(8,128)S(1)} %get-tuple-element.54), channel_id=1, source_target_pairs={{0,12},{1,13},{2,14},{3,15},{4,0},{5,1},{6,2},{7,3},{8,4},{9,5},{1... | collective-permute-start | bytes 417800 | tf_op jit(solution)/shard_map/ppermute | solution.py:405
  47.3 0.9 collective-permute-done.9.m1.refs_1_
  48.1 3.7 %collective-permute-done.10.m2.refs_2_ = f32[136,256]{1,0:T(8,128)S(1)} collective-permute-done((f32[136,256]{1,0:T(8,128)S(1)}, f32[136,256]{1,0:T(8,128)S(1)}, u32[]{:S(2)}, u32[]{:S(2)}) %collective-permute-start.10) | collective-permute-done | bytes 139296 | tf_op jit(solution)/shard_map/ppermute | solution.py:405
  51.8 0.8 collective-permute-done.11.m3.refs_3_
  52.7 3.1 %collective-permute-start.14 = (f32[136,256]{1,0:T(8,128)S(1)}, f32[136,256]{1,0:T(8,128)S(1)}, u32[]{:S(2)}, u32[]{:S(2)}) collective-permute-start(f32[136,256]{1,0:T(8,128)S(1)} %shard_map.68.total), channel_id=1, source_target_pairs={{0,96},{16,112},{32,0},{48,16},{64,32},{80,48},{96,64},{112,80},{1... | collective-permute-start | bytes 417800 | tf_op jit(solution)/shard_map/ppermute | solution.py:452
  55.7 0.6 collective-permute-start.13
  56.4 2.1 %shard_map.62 = (bf16[4,256,256]{2,1,0:T(8,128)(2,1)S(1)}, bf16[4,256,256]{2,1,0:T(8,128)(2,1)S(1)}, bf16[4,256,256]{2,1,0:T(8,128)(2,1)S(1)}) custom-call(s32[4]{0:T(128)S(1)} %pad_add_fusion.pos, bf16[256,4096]{1,0:T(8,128)(2,1)} %q_ref.3), custom_call_target="tpu_custom_call" | custom-call | tf_op jit(solution)/shard_map/pallas_call | solution.py:78
  58.5 1.1 collective-permute-start.3
  59.6 2.0 %collective-permute-start.4 = (bf16[4,256,256]{2,1,0:T(8,128)(2,1)S(1)}, bf16[4,256,256]{2,1,0:T(8,128)(2,1)S(1)}, u32[]{:S(2)}, u32[]{:S(2)}) collective-permute-start(bf16[4,256,256]{2,1,0:T(8,128)(2,1)S(1)} %get-tuple-element.45), channel_id=1, source_target_pairs={{0,2},{1,3},{2,0},{3,1},{4,6},{5,7},{6,4},{7,5},{8,10},{9,11},{10,... | collective-permute-start | bytes 1572872 | tf_op jit(solution)/shard_map/ppermute | solution.py:401
  61.6 2.5 %collective-permute-start.5 = (bf16[4,256,256]{2,1,0:T(8,128)(2,1)S(1)}, bf16[4,256,256]{2,1,0:T(8,128)(2,1)S(1)}, u32[]{:S(2)}, u32[]{:S(2)}) collective-permute-start(bf16[4,256,256]{2,1,0:T(8,128)(2,1)S(1)} %get-tuple-element.46), channel_id=1, source_target_pairs={{0,3},{1,0},{2,1},{3,2},{4,7},{5,4},{6,5},{7,6},{8,11},{9,8},{10,9... | collective-permute-start | bytes 1572872 | tf_op jit(solution)/shard_map/ppermute | solution.py:401
  64.2 1.0 collective-permute-start.12
  65.1 1.8 shard_map.65
  66.9 1.4 collective-permute-start.6
  68.3 2.2 %collective-permute-done.12.o1 = f32[136,256]{1,0:T(8,128)S(1)} collective-permute-done((f32[136,256]{1,0:T(8,128)S(1)}, f32[136,256]{1,0:T(8,128)S(1)}, u32[]{:S(2)}, u32[]{:S(2)}) %collective-permute-start.12) | collective-permute-done | bytes 139296 | tf_op jit(solution)/shard_map/ppermute | solution.py:452
  70.4 0.6 shard_map.69
  71.1 2.2 %collective-permute-done.6.refs_6_ = bf16[1024,128]{1,0:T(8,128)(2,1)S(1)} collective-permute-done((bf16[1024,128]{1,0:T(8,128)(2,1)S(1)}, bf16[1024,128]{1,0:T(8,128)(2,1)S(1)}, u32[]{:S(2)}, u32[]{:S(2)}) %collective-permute-start.6) | collective-permute-done | bytes 262176 | tf_op jit(solution)/shard_map/ppermute | solution.py:405
  73.4 1.8 %collective-permute-start.7 = (bf16[1024,128]{1,0:T(8,128)(2,1)S(1)}, bf16[1024,128]{1,0:T(8,128)(2,1)S(1)}, u32[]{:S(2)}, u32[]{:S(2)}) collective-permute-start(bf16[1024,128]{1,0:T(8,128)(2,1)S(1)} %get-tuple-element.49), channel_id=1, source_target_pairs={{0,8},{1,9},{2,10},{3,11},{4,12},{5,13},{6,14},{7,15},{8,0},{9,1},... | collective-permute-start | bytes 786440 | tf_op jit(solution)/shard_map/ppermute | solution.py:405
  75.2 1.6 collective-permute-start.8
  76.7 0.7 shard_map.70
  78.0 3.0 %collective-permute-start.17 = (f32[136,256]{1,0:T(8,128)S(1)}, f32[136,256]{1,0:T(8,128)S(1)}, u32[]{:S(2)}, u32[]{:S(2)}) collective-permute-start(f32[136,256]{1,0:T(8,128)S(1)} %get-tuple-element.59), channel_id=1, source_target_pairs={{0,8},{1,9},{2,10},{3,11},{4,12},{5,13},{6,14},{7,15},{8,0},{9,1},... | collective-permute-start | bytes 417800 | tf_op jit(solution)/shard_map/ppermute | solution.py:405
  81.0 3.6 %collective-permute-done.5.refs_7_.refs_3_ = bf16[4,256,256]{2,1,0:T(8,128)(2,1)S(1)} collective-permute-done((bf16[4,256,256]{2,1,0:T(8,128)(2,1)S(1)}, bf16[4,256,256]{2,1,0:T(8,128)(2,1)S(1)}, u32[]{:S(2)}, u32[]{:S(2)}) %collective-permute-start.5) | collective-permute-done | bytes 524320 | tf_op jit(solution)/shard_map/ppermute | solution.py:401
  84.7 1.7 shard_map.61.refs_4_.refs_0_
  86.4 1.4 shard_map.63.refs_8_.refs_6_
  87.8 4.1 %shard_map.64.refs_4_ = f32[4,4,256,256]{3,2,1,0:T(8,128)S(1)} custom-call(s32[4]{0:T(128)S(1)} %pad_add_fusion.pos, bf16[4,256,384]{2,1,0:T(8,128)(2,1)S(1)} %shard_map.59.refs_0_.kv0, bf16[4,256,384]{2,1,0:T(8,128)(2,1)S(1)} %collective-permute-done.refs_1_.kv1.refs_0_, bf16[4,256,384]{2,1,0:T(8,128)(2,1)S(1)} %collective-permute-done.1.refs_2_.kv2.refs_0_, ...), custom_call_target="tpu_custom_call" | custom-call | tf_op jit(solution)/shard_map/pallas_call | solution.py:78
  91.9 1.0 collective-permute-done.18.refs_12_.refs_10_
  92.9 4.8 %shard_map.71 = (bf16[4,4,256,256]{3,2,1,0:T(8,128)(2,1)S(1)}, bf16[4,4,256,256]{3,2,1,0:T(8,128)(2,1)S(1)}, f32[4,4,136,256]{3,2,1,0:T(8,128)S(1)}, f32[136,256...) custom-call(s32[4]{0:T(128)S(1)} %pad_add_fusion.pos, ...), custom_call_target="tpu_custom_call" | custom-call | tf_op jit(solution)/shard_map/pallas_call | solution.py:78
  97.7 0.9 collective-permute-start.22
  98.6 3.1 %collective-permute-start.23 = (f32[136,256]{1,0:T(8,128)S(1)}, f32[136,256]{1,0:T(8,128)S(1)}, u32[]{:S(2)}, u32[]{:S(2)}) collective-permute-start(f32[136,256]{1,0:T(8,128)S(1)} %get-tuple-element.70), channel_id=1, source_target_pairs={{0,8},{1,9},{2,10},{3,11},{4,12},{5,13},{6,14},{7,15},{8,0},{9,1},... | collective-permute-start | bytes 417800 | tf_op jit(solution)/shard_map/ppermute | solution.py:405
  102.2 4.6 %shard_map.72 = (bf16[4,256,256]{2,1,0:T(8,128)(2,1)S(1)}, bf16[4,256,256]{2,1,0:T(8,128)(2,1)S(1)}, bf16[4,256,256]{2,1,0:T(8,128)(2,1)S(1)}, bf16[4,256,256]{2,1,0:T(8,128)(2,1)S(1)}) custom-call(s32[4]{0:T(128)S(1)} %pad_add_fusion.pos, bf16[4,256,384]{2,1,0:T(8,128)(2,1)S(1)} %shard_map.59.refs_0_.kv0, ...), custom_call_target="tpu_custom_call" | custom-call | tf_op jit(solution)/shard_map/pallas_call | solution.py:78
  107.2 1.0 collective-permute-done.24.m3.refs_3_
  108.2 1.1 collective-permute-start.27
  109.3 2.2 %collective-permute-start.26 = (f32[136,256]{1,0:T(8,128)S(1)}, f32[136,256]{1,0:T(8,128)S(1)}, u32[]{:S(2)}, u32[]{:S(2)}) collective-permute-start(f32[136,256]{1,0:T(8,128)S(1)} %shard_map.75.total), channel_id=1, source_target_pairs={{0,64},{16,80},{32,96},{48,112},{64,0},{80,16},{96,32},{112,48},{1... | collective-permute-start | bytes 417800 | tf_op jit(solution)/shard_map/ppermute | solution.py:452
  111.5 1.1 collective-permute-start.25
  112.6 1.9 %collective-permute-done.27.o3 = f32[136,256]{1,0:T(8,128)S(1)} collective-permute-done((f32[136,256]{1,0:T(8,128)S(1)}, f32[136,256]{1,0:T(8,128)S(1)}, u32[]{:S(2)}, u32[]{:S(2)}) %collective-permute-start.27) | collective-permute-done | bytes 139296 | tf_op jit(solution)/shard_map/ppermute | solution.py:452
  114.5 2.5 %collective-permute-done.26.o2 = f32[136,256]{1,0:T(8,128)S(1)} collective-permute-done((f32[136,256]{1,0:T(8,128)S(1)}, f32[136,256]{1,0:T(8,128)S(1)}, u32[]{:S(2)}, u32[]{:S(2)}) %collective-permute-start.26) | collective-permute-done | bytes 139296 | tf_op jit(solution)/shard_map/ppermute | solution.py:452
  117.0 1.8 collective-permute-done.25.o1
  118.7 0.6 shard_map.76
  119.4 1.3 collective-permute-done.28.other_core
  120.8 0.7 shard_map.77
  121.6 3.3 %collective-permute-start.30 = (f32[136,256]{1,0:T(8,128)S(1)}, f32[136,256]{1,0:T(8,128)S(1)}, u32[]{:S(2)}, u32[]{:S(2)}) collective-permute-start(f32[136,256]{1,0:T(8,128)S(1)} %get-tuple-element.76), channel_id=1, source_target_pairs={{0,8},{1,9},{2,10},{3,11},{4,12},{5,13},{6,14},{7,15},{8,0},{9,1},... | collective-permute-start | bytes 417800 | tf_op jit(solution)/shard_map/ppermute | solution.py:405
  125.0 2.5 %collective-permute-start.31 = (f32[136,256]{1,0:T(8,128)S(1)}, f32[136,256]{1,0:T(8,128)S(1)}, u32[]{:S(2)}, u32[]{:S(2)}) collective-permute-start(f32[136,256]{1,0:T(8,128)S(1)} %get-tuple-element.77), channel_id=1, source_target_pairs={{0,12},{1,13},{2,14},{3,15},{4,0},{5,1},{6,2},{7,3},{8,4},{9,5},{1... | collective-permute-start | bytes 417800 | tf_op jit(solution)/shard_map/ppermute | solution.py:405
  127.5 2.5 %collective-permute-start.20 = (bf16[4,256,256]{2,1,0:T(8,128)(2,1)S(1)}, bf16[4,256,256]{2,1,0:T(8,128)(2,1)S(1)}, u32[]{:S(2)}, u32[]{:S(2)}) collective-permute-start(bf16[4,256,256]{2,1,0:T(8,128)(2,1)S(1)} %get-tuple-element.65), channel_id=1, source_target_pairs={{0,2},{1,3},{2,0},{3,1},{4,6},{5,7},{6,4},{7,5},{8,10},{9,11},{10,... | collective-permute-start | bytes 1572872 | tf_op jit(solution)/shard_map/ppermute | solution.py:401
  130.0 5.7 %shard_map.74.refs_1_.refs_2_ = f32[4,4,256,256]{3,2,1,0:T(8,128)S(1)} custom-call(s32[4]{0:T(128)S(1)} %pad_add_fusion.pos, bf16[4,256,384]{2,1,0:T(8,128)(2,1)S(1)} %shard_map.59.refs_0_.kv0, bf16[4,256,384]{2,1,0:T(8,128)(2,1)S(1)} %collective-permute-done.refs_1_.kv1.refs_0_, bf16[4,256,384]{2,1,0:T(8,128)(2,1)S(1)} %collective-permute-done.1.refs_2_.kv2.refs_0_, ...), custom_call_target="tpu_custom_call" | custom-call | tf_op jit(solution)/shard_map/pallas_call | solution.py:78
  135.8 1.3 shard_map.79
  137.0 2.1 %collective-permute-start.32 = (bf16[4,256,256]{2,1,0:T(8,128)(2,1)S(1)}, bf16[4,256,256]{2,1,0:T(8,128)(2,1)S(1)}, u32[]{:S(2)}, u32[]{:S(2)}) collective-permute-start(bf16[4,256,256]{2,1,0:T(8,128)(2,1)S(1)} %get-tuple-element.78), channel_id=1, source_target_pairs={{0,1},{1,2},{2,3},{3,0},{4,5},{5,6},{6,7},{7,4},{8,9},{9,10},{10,1... | collective-permute-start | bytes 1572872 | tf_op jit(solution)/shard_map/ppermute | solution.py:401
  139.4 1.0 shard_map.80
  140.4 2.1 %collective-permute-start.33 = (bf16[4,256,256]{2,1,0:T(8,128)(2,1)S(1)}, bf16[4,256,256]{2,1,0:T(8,128)(2,1)S(1)}, u32[]{:S(2)}, u32[]{:S(2)}) collective-permute-start(bf16[4,256,256]{2,1,0:T(8,128)(2,1)S(1)} %shard_map.80), channel_id=1, source_target_pairs={{0,2},{1,3},{2,0},{3,1},{4,6},{5,7},{6,4},{7,5},{8,10},{9,11},{10,... | collective-permute-start | bytes 1572872 | tf_op jit(solution)/shard_map/ppermute | solution.py:401
  142.5 1.4 collective-permute-done.20.refs_2_
  143.8 9.7 %collective-permute-done.21.refs_3_ = bf16[4,256,256]{2,1,0:T(8,128)(2,1)S(1)} collective-permute-done((bf16[4,256,256]{2,1,0:T(8,128)(2,1)S(1)}, bf16[4,256,256]{2,1,0:T(8,128)(2,1)S(1)}, u32[]{:S(2)}, u32[]{:S(2)}) %collective-permute-start.21) | collective-permute-done | bytes 524320 | tf_op jit(solution)/shard_map/ppermute | solution.py:401
  153.6 2.1 %shard_map.73 = bf16[256,4096]{1,0:T(8,128)(2,1)} custom-call(s32[4]{0:T(128)S(1)} %pad_add_fusion.pos, bf16[4,256,256]{2,1,0:T(8,128)(2,1)S(1)} %get-tuple-element.63.refs_0_, bf16[4,256,256]{2,1,0:T(8,128)(2,1)S(1)} %collective-permute-done.19.refs_1_, bf16[4,256,256]{2,1,0:T(8,128)(2,1)S(1)} %collective-permute-done.20.refs_2_, ...), custom_call_target="tpu_custom_call" | custom-call | tf_op jit(solution)/shard_map/pallas_call | solution.py:78
  155.7 1.0 shard_map.78.refs_0_
  156.7 9.5 %collective-permute-done.34.refs_3_ = bf16[4,256,256]{2,1,0:T(8,128)(2,1)S(1)} collective-permute-done((bf16[4,256,256]{2,1,0:T(8,128)(2,1)S(1)}, bf16[4,256,256]{2,1,0:T(8,128)(2,1)S(1)}, u32[]{:S(2)}, u32[]{:S(2)}) %collective-permute-start.34) | collective-permute-done | bytes 524320 | tf_op jit(solution)/shard_map/ppermute | solution.py:401
  166.2 9.7 %collective-permute-done.33.refs_2_ = bf16[4,256,256]{2,1,0:T(8,128)(2,1)S(1)} collective-permute-done((bf16[4,256,256]{2,1,0:T(8,128)(2,1)S(1)}, bf16[4,256,256]{2,1,0:T(8,128)(2,1)S(1)}, u32[]{:S(2)}, u32[]{:S(2)}) %collective-permute-start.33) | collective-permute-done | bytes 524320 | tf_op jit(solution)/shard_map/ppermute | solution.py:401
  175.9 2.1 %shard_map.81 = bf16[256,4096]{1,0:T(8,128)(2,1)} custom-call(s32[4]{0:T(128)S(1)} %pad_add_fusion.pos, bf16[4,256,256]{2,1,0:T(8,128)(2,1)S(1)} %shard_map.78.refs_0_, bf16[4,256,256]{2,1,0:T(8,128)(2,1)S(1)} %collective-permute-done.32.refs_1_, bf16[4,256,256]{2,1,0:T(8,128)(2,1)S(1)} %collective-permute-done.33.refs_2_, ...), custom_call_target="tpu_custom_call" | custom-call | tf_op jit(solution)/shard_map/pallas_call | solution.py:78
  (30 shorter events, 2.4 us)
Async XLA Ops:
  3.2 22.0 %collective-permute-start.1 = (bf16[4,256,384]{2,1,0:T(8,128)(2,1)S(1)}, bf16[4,256,384]{2,1,0:T(8,128)(2,1)S(1)}, u32[]{:S(2)}, u32[]{:S(2)}) collective-permute-start(bf16[4,256,384]{2,1,0:T(8,128)(2,1)S(1)} %get-tuple-element.42), channel_id=1, source_target_pairs={{0,2},{1,3},{2,0},{3,1},{4,6},{5,7},{6,4},{7,5},{8,10},{9,11},{10,... | collective-permute-start | bytes 2359304 | tf_op jit(solution)/shard_map/ppermute | solution.py:401
  6.3 35.2 %collective-permute-start = (bf16[4,256,384]{2,1,0:T(8,128)(2,1)S(1)}, bf16[4,256,384]{2,1,0:T(8,128)(2,1)S(1)}, u32[]{:S(2)}, u32[]{:S(2)}) collective-permute-start(bf16[4,256,384]{2,1,0:T(8,128)(2,1)S(1)} %get-tuple-element.41), channel_id=1, source_target_pairs={{0,1},{1,2},{2,3},{3,0},{4,5},{5,6},{6,7},{7,4},{8,9},{9,10},{10,1... | collective-permute-start | bytes 2359304 | tf_op jit(solution)/shard_map/ppermute | solution.py:401
  6.3 35.2 %collective-permute-start.2 = (bf16[4,256,384]{2,1,0:T(8,128)(2,1)S(1)}, bf16[4,256,384]{2,1,0:T(8,128)(2,1)S(1)}, u32[]{:S(2)}, u32[]{:S(2)}) collective-permute-start(bf16[4,256,384]{2,1,0:T(8,128)(2,1)S(1)} %get-tuple-element.43), channel_id=1, source_target_pairs={{0,3},{1,0},{2,1},{3,2},{4,7},{5,4},{6,5},{7,6},{8,11},{9,8},{10,9... | collective-permute-start | bytes 2359304 | tf_op jit(solution)/shard_map/ppermute | solution.py:401
  42.4 5.7 %collective-permute-start.9 = (f32[136,256]{1,0:T(8,128)S(1)}, f32[136,256]{1,0:T(8,128)S(1)}, u32[]{:S(2)}, u32[]{:S(2)}) collective-permute-start(f32[136,256]{1,0:T(8,128)S(1)} %get-tuple-element.52), channel_id=1, source_target_pairs={{0,4},{1,5},{2,6},{3,7},{4,8},{5,9},{6,10},{7,11},{8,12},{9,13},{1... | collective-permute-start | bytes 417800 | tf_op jit(solution)/shard_map/ppermute | solution.py:405
  44.0 7.9 %collective-permute-start.10 = (f32[136,256]{1,0:T(8,128)S(1)}, f32[136,256]{1,0:T(8,128)S(1)}, u32[]{:S(2)}, u32[]{:S(2)}) collective-permute-start(f32[136,256]{1,0:T(8,128)S(1)} %get-tuple-element.53), channel_id=1, source_target_pairs={{0,8},{1,9},{2,10},{3,11},{4,12},{5,13},{6,14},{7,15},{8,0},{9,1},... | collective-permute-start | bytes 417800 | tf_op jit(solution)/shard_map/ppermute | solution.py:405
  45.1 7.5 %collective-permute-start.11 = (f32[136,256]{1,0:T(8,128)S(1)}, f32[136,256]{1,0:T(8,128)S(1)}, u32[]{:S(2)}, u32[]{:S(2)}) collective-permute-start(f32[136,256]{1,0:T(8,128)S(1)} %get-tuple-element.54), channel_id=1, source_target_pairs={{0,12},{1,13},{2,14},{3,15},{4,0},{5,1},{6,2},{7,3},{8,4},{9,5},{1... | collective-permute-start | bytes 417800 | tf_op jit(solution)/shard_map/ppermute | solution.py:405
  52.7 11.5 %collective-permute-start.14 = (f32[136,256]{1,0:T(8,128)S(1)}, f32[136,256]{1,0:T(8,128)S(1)}, u32[]{:S(2)}, u32[]{:S(2)}) collective-permute-start(f32[136,256]{1,0:T(8,128)S(1)} %shard_map.68.total), channel_id=1, source_target_pairs={{0,96},{16,112},{32,0},{48,16},{64,32},{80,48},{96,64},{112,80},{1... | collective-permute-start | bytes 417800 | tf_op jit(solution)/shard_map/ppermute | solution.py:452
  55.7 11.2 %collective-permute-start.13 = (f32[136,256]{1,0:T(8,128)S(1)}, f32[136,256]{1,0:T(8,128)S(1)}, u32[]{:S(2)}, u32[]{:S(2)}) collective-permute-start(f32[136,256]{1,0:T(8,128)S(1)} %shard_map.68.total), channel_id=1, source_target_pairs={{0,64},{16,80},{32,96},{48,112},{64,0},{80,16},{96,32},{112,48},{1... | collective-permute-start | bytes 417800 | tf_op jit(solution)/shard_map/ppermute | solution.py:452
  58.5 19.0 %collective-permute-start.3 = (bf16[4,256,256]{2,1,0:T(8,128)(2,1)S(1)}, bf16[4,256,256]{2,1,0:T(8,128)(2,1)S(1)}, u32[]{:S(2)}, u32[]{:S(2)}) collective-permute-start(bf16[4,256,256]{2,1,0:T(8,128)(2,1)S(1)} %get-tuple-element.44), channel_id=1, source_target_pairs={{0,1},{1,2},{2,3},{3,0},{4,5},{5,6},{6,7},{7,4},{8,9},{9,10},{10,1... | collective-permute-start | bytes 1572872 | tf_op jit(solution)/shard_map/ppermute | solution.py:401
  59.6 18.4 %collective-permute-start.4 = (bf16[4,256,256]{2,1,0:T(8,128)(2,1)S(1)}, bf16[4,256,256]{2,1,0:T(8,128)(2,1)S(1)}, u32[]{:S(2)}, u32[]{:S(2)}) collective-permute-start(bf16[4,256,256]{2,1,0:T(8,128)(2,1)S(1)} %get-tuple-element.45), channel_id=1, source_target_pairs={{0,2},{1,3},{2,0},{3,1},{4,6},{5,7},{6,4},{7,5},{8,10},{9,11},{10,... | collective-permute-start | bytes 1572872 | tf_op jit(solution)/shard_map/ppermute | solution.py:401
  61.6 22.9 %collective-permute-start.5 = (bf16[4,256,256]{2,1,0:T(8,128)(2,1)S(1)}, bf16[4,256,256]{2,1,0:T(8,128)(2,1)S(1)}, u32[]{:S(2)}, u32[]{:S(2)}) collective-permute-start(bf16[4,256,256]{2,1,0:T(8,128)(2,1)S(1)} %get-tuple-element.46), channel_id=1, source_target_pairs={{0,3},{1,0},{2,1},{3,2},{4,7},{5,4},{6,5},{7,6},{8,11},{9,8},{10,9... | collective-permute-start | bytes 1572872 | tf_op jit(solution)/shard_map/ppermute | solution.py:401
  64.2 6.3 %collective-permute-start.12 = (f32[136,256]{1,0:T(8,128)S(1)}, f32[136,256]{1,0:T(8,128)S(1)}, u32[]{:S(2)}, u32[]{:S(2)}) collective-permute-start(f32[136,256]{1,0:T(8,128)S(1)} %shard_map.68.total), channel_id=1, source_target_pairs={{0,32},{16,48},{32,64},{48,80},{64,96},{80,112},{96,0},{112,16},{1... | collective-permute-start | bytes 417800 | tf_op jit(solution)/shard_map/ppermute | solution.py:452
  66.9 6.4 %collective-permute-start.6 = (bf16[1024,128]{1,0:T(8,128)(2,1)S(1)}, bf16[1024,128]{1,0:T(8,128)(2,1)S(1)}, u32[]{:S(2)}, u32[]{:S(2)}) collective-permute-start(bf16[1024,128]{1,0:T(8,128)(2,1)S(1)} %get-tuple-element.48), channel_id=1, source_target_pairs={{0,4},{1,5},{2,6},{3,7},{4,8},{5,9},{6,10},{7,11},{8,12},{9,13},{1... | collective-permute-start | bytes 786440 | tf_op jit(solution)/shard_map/ppermute | solution.py:405
  71.0 4.1 %collective-permute-start.15 = (f32[136,256]{1,0:T(8,128)S(1)}, f32[136,256]{1,0:T(8,128)S(1)}, u32[]{:S(2)}, u32[]{:S(2)}) collective-permute-start(f32[136,256]{1,0:T(8,128)S(1)} %get-tuple-element.56), channel_id=1, source_target_pairs={{0,16},{16,0},{32,48},{48,32},{64,80},{80,64},{96,112},{112,96},{1... | collective-permute-start | bytes 417800 | tf_op jit(solution)/shard_map/ppermute | solution.py:456
  73.4 18.5 %collective-permute-start.7 = (bf16[1024,128]{1,0:T(8,128)(2,1)S(1)}, bf16[1024,128]{1,0:T(8,128)(2,1)S(1)}, u32[]{:S(2)}, u32[]{:S(2)}) collective-permute-start(bf16[1024,128]{1,0:T(8,128)(2,1)S(1)} %get-tuple-element.49), channel_id=1, source_target_pairs={{0,8},{1,9},{2,10},{3,11},{4,12},{5,13},{6,14},{7,15},{8,0},{9,1},... | collective-permute-start | bytes 786440 | tf_op jit(solution)/shard_map/ppermute | solution.py:405
  75.2 16.7 %collective-permute-start.8 = (bf16[1024,128]{1,0:T(8,128)(2,1)S(1)}, bf16[1024,128]{1,0:T(8,128)(2,1)S(1)}, u32[]{:S(2)}, u32[]{:S(2)}) collective-permute-start(bf16[1024,128]{1,0:T(8,128)(2,1)S(1)} %get-tuple-element.50), channel_id=1, source_target_pairs={{0,12},{1,13},{2,14},{3,15},{4,0},{5,1},{6,2},{7,3},{8,4},{9,5},{1... | collective-permute-start | bytes 786440 | tf_op jit(solution)/shard_map/ppermute | solution.py:405
  77.5 14.4 %collective-permute-start.16 = (f32[136,256]{1,0:T(8,128)S(1)}, f32[136,256]{1,0:T(8,128)S(1)}, u32[]{:S(2)}, u32[]{:S(2)}) collective-permute-start(f32[136,256]{1,0:T(8,128)S(1)} %get-tuple-element.58), channel_id=1, source_target_pairs={{0,4},{1,5},{2,6},{3,7},{4,8},{5,9},{6,10},{7,11},{8,12},{9,13},{1... | collective-permute-start | bytes 417800 | tf_op jit(solution)/shard_map/ppermute | solution.py:405
  78.0 13.9 %collective-permute-start.17 = (f32[136,256]{1,0:T(8,128)S(1)}, f32[136,256]{1,0:T(8,128)S(1)}, u32[]{:S(2)}, u32[]{:S(2)}) collective-permute-start(f32[136,256]{1,0:T(8,128)S(1)} %get-tuple-element.59), channel_id=1, source_target_pairs={{0,8},{1,9},{2,10},{3,11},{4,12},{5,13},{6,14},{7,15},{8,0},{9,1},... | collective-permute-start | bytes 417800 | tf_op jit(solution)/shard_map/ppermute | solution.py:405
  84.5 8.4 %collective-permute-start.18 = (f32[136,256]{1,0:T(8,128)S(1)}, f32[136,256]{1,0:T(8,128)S(1)}, u32[]{:S(2)}, u32[]{:S(2)}) collective-permute-start(f32[136,256]{1,0:T(8,128)S(1)} %get-tuple-element.60), channel_id=1, source_target_pairs={{0,12},{1,13},{2,14},{3,15},{4,0},{5,1},{6,2},{7,3},{8,4},{9,5},{1... | collective-permute-start | bytes 417800 | tf_op jit(solution)/shard_map/ppermute | solution.py:405
  97.7 9.5 %collective-permute-start.22 = (f32[136,256]{1,0:T(8,128)S(1)}, f32[136,256]{1,0:T(8,128)S(1)}, u32[]{:S(2)}, u32[]{:S(2)}) collective-permute-start(f32[136,256]{1,0:T(8,128)S(1)} %get-tuple-element.69), channel_id=1, source_target_pairs={{0,4},{1,5},{2,6},{3,7},{4,8},{5,9},{6,10},{7,11},{8,12},{9,13},{1... | collective-permute-start | bytes 417800 | tf_op jit(solution)/shard_map/ppermute | solution.py:405
  98.6 8.6 %collective-permute-start.23 = (f32[136,256]{1,0:T(8,128)S(1)}, f32[136,256]{1,0:T(8,128)S(1)}, u32[]{:S(2)}, u32[]{:S(2)}) collective-permute-start(f32[136,256]{1,0:T(8,128)S(1)} %get-tuple-element.70), channel_id=1, source_target_pairs={{0,8},{1,9},{2,10},{3,11},{4,12},{5,13},{6,14},{7,15},{8,0},{9,1},... | collective-permute-start | bytes 417800 | tf_op jit(solution)/shard_map/ppermute | solution.py:405
  101.7 6.4 %collective-permute-start.24 = (f32[136,256]{1,0:T(8,128)S(1)}, f32[136,256]{1,0:T(8,128)S(1)}, u32[]{:S(2)}, u32[]{:S(2)}) collective-permute-start(f32[136,256]{1,0:T(8,128)S(1)} %get-tuple-element.71), channel_id=1, source_target_pairs={{0,12},{1,13},{2,14},{3,15},{4,0},{5,1},{6,2},{7,3},{8,4},{9,5},{1... | collective-permute-start | bytes 417800 | tf_op jit(solution)/shard_map/ppermute | solution.py:405
  106.8 33.6 %collective-permute-start.19 = (bf16[4,256,256]{2,1,0:T(8,128)(2,1)S(1)}, bf16[4,256,256]{2,1,0:T(8,128)(2,1)S(1)}, u32[]{:S(2)}, u32[]{:S(2)}) collective-permute-start(bf16[4,256,256]{2,1,0:T(8,128)(2,1)S(1)} %get-tuple-element.64), channel_id=1, source_target_pairs={{0,1},{1,2},{2,3},{3,0},{4,5},{5,6},{6,7},{7,4},{8,9},{9,10},{10,1... | collective-permute-start | bytes 1572872 | tf_op jit(solution)/shard_map/ppermute | solution.py:401
  108.2 6.3 %collective-permute-start.27 = (f32[136,256]{1,0:T(8,128)S(1)}, f32[136,256]{1,0:T(8,128)S(1)}, u32[]{:S(2)}, u32[]{:S(2)}) collective-permute-start(f32[136,256]{1,0:T(8,128)S(1)} %shard_map.75.total), channel_id=1, source_target_pairs={{0,96},{16,112},{32,0},{48,16},{64,32},{80,48},{96,64},{112,80},{1... | collective-permute-start | bytes 417800 | tf_op jit(solution)/shard_map/ppermute | solution.py:452
  109.3 7.7 %collective-permute-start.26 = (f32[136,256]{1,0:T(8,128)S(1)}, f32[136,256]{1,0:T(8,128)S(1)}, u32[]{:S(2)}, u32[]{:S(2)}) collective-permute-start(f32[136,256]{1,0:T(8,128)S(1)} %shard_map.75.total), channel_id=1, source_target_pairs={{0,64},{16,80},{32,96},{48,112},{64,0},{80,16},{96,32},{112,48},{1... | collective-permute-start | bytes 417800 | tf_op jit(solution)/shard_map/ppermute | solution.py:452
  111.5 7.3 %collective-permute-start.25 = (f32[136,256]{1,0:T(8,128)S(1)}, f32[136,256]{1,0:T(8,128)S(1)}, u32[]{:S(2)}, u32[]{:S(2)}) collective-permute-start(f32[136,256]{1,0:T(8,128)S(1)} %shard_map.75.total), channel_id=1, source_target_pairs={{0,32},{16,48},{32,64},{48,80},{64,96},{80,112},{96,0},{112,16},{1... | collective-permute-start | bytes 417800 | tf_op jit(solution)/shard_map/ppermute | solution.py:452
  119.3 1.4 collective-permute-start.28
  121.5 14.2 %collective-permute-start.29 = (f32[136,256]{1,0:T(8,128)S(1)}, f32[136,256]{1,0:T(8,128)S(1)}, u32[]{:S(2)}, u32[]{:S(2)}) collective-permute-start(f32[136,256]{1,0:T(8,128)S(1)} %get-tuple-element.75), channel_id=1, source_target_pairs={{0,4},{1,5},{2,6},{3,7},{4,8},{5,9},{6,10},{7,11},{8,12},{9,13},{1... | collective-permute-start | bytes 417800 | tf_op jit(solution)/shard_map/ppermute | solution.py:405
  121.6 14.1 %collective-permute-start.30 = (f32[136,256]{1,0:T(8,128)S(1)}, f32[136,256]{1,0:T(8,128)S(1)}, u32[]{:S(2)}, u32[]{:S(2)}) collective-permute-start(f32[136,256]{1,0:T(8,128)S(1)} %get-tuple-element.76), channel_id=1, source_target_pairs={{0,8},{1,9},{2,10},{3,11},{4,12},{5,13},{6,14},{7,15},{8,0},{9,1},... | collective-permute-start | bytes 417800 | tf_op jit(solution)/shard_map/ppermute | solution.py:405
  125.0 10.8 %collective-permute-start.31 = (f32[136,256]{1,0:T(8,128)S(1)}, f32[136,256]{1,0:T(8,128)S(1)}, u32[]{:S(2)}, u32[]{:S(2)}) collective-permute-start(f32[136,256]{1,0:T(8,128)S(1)} %get-tuple-element.77), channel_id=1, source_target_pairs={{0,12},{1,13},{2,14},{3,15},{4,0},{5,1},{6,2},{7,3},{8,4},{9,5},{1... | collective-permute-start | bytes 417800 | tf_op jit(solution)/shard_map/ppermute | solution.py:405
  127.5 16.3 %collective-permute-start.20 = (bf16[4,256,256]{2,1,0:T(8,128)(2,1)S(1)}, bf16[4,256,256]{2,1,0:T(8,128)(2,1)S(1)}, u32[]{:S(2)}, u32[]{:S(2)}) collective-permute-start(bf16[4,256,256]{2,1,0:T(8,128)(2,1)S(1)} %get-tuple-element.65), channel_id=1, source_target_pairs={{0,2},{1,3},{2,0},{3,1},{4,6},{5,7},{6,4},{7,5},{8,10},{9,11},{10,... | collective-permute-start | bytes 1572872 | tf_op jit(solution)/shard_map/ppermute | solution.py:401
  135.7 17.9 %collective-permute-start.21 = (bf16[4,256,256]{2,1,0:T(8,128)(2,1)S(1)}, bf16[4,256,256]{2,1,0:T(8,128)(2,1)S(1)}, u32[]{:S(2)}, u32[]{:S(2)}) collective-permute-start(bf16[4,256,256]{2,1,0:T(8,128)(2,1)S(1)} %get-tuple-element.66), channel_id=1, source_target_pairs={{0,3},{1,0},{2,1},{3,2},{4,7},{5,4},{6,5},{7,6},{8,11},{9,8},{10,9... | collective-permute-start | bytes 1572872 | tf_op jit(solution)/shard_map/ppermute | solution.py:401
  137.0 19.7 %collective-permute-start.32 = (bf16[4,256,256]{2,1,0:T(8,128)(2,1)S(1)}, bf16[4,256,256]{2,1,0:T(8,128)(2,1)S(1)}, u32[]{:S(2)}, u32[]{:S(2)}) collective-permute-start(bf16[4,256,256]{2,1,0:T(8,128)(2,1)S(1)} %get-tuple-element.78), channel_id=1, source_target_pairs={{0,1},{1,2},{2,3},{3,0},{4,5},{5,6},{6,7},{7,4},{8,9},{9,10},{10,1... | collective-permute-start | bytes 1572872 | tf_op jit(solution)/shard_map/ppermute | solution.py:401
  139.1 27.1 %collective-permute-start.34 = (bf16[4,256,256]{2,1,0:T(8,128)(2,1)S(1)}, bf16[4,256,256]{2,1,0:T(8,128)(2,1)S(1)}, u32[]{:S(2)}, u32[]{:S(2)}) collective-permute-start(bf16[4,256,256]{2,1,0:T(8,128)(2,1)S(1)} %get-tuple-element.79), channel_id=1, source_target_pairs={{0,3},{1,0},{2,1},{3,2},{4,7},{5,4},{6,5},{7,6},{8,11},{9,8},{10,9... | collective-permute-start | bytes 1572872 | tf_op jit(solution)/shard_map/ppermute | solution.py:401
  140.4 35.5 %collective-permute-start.33 = (bf16[4,256,256]{2,1,0:T(8,128)(2,1)S(1)}, bf16[4,256,256]{2,1,0:T(8,128)(2,1)S(1)}, u32[]{:S(2)}, u32[]{:S(2)}) collective-permute-start(bf16[4,256,256]{2,1,0:T(8,128)(2,1)S(1)} %shard_map.80), channel_id=1, source_target_pairs={{0,2},{1,3},{2,0},{3,1},{4,6},{5,7},{6,4},{7,5},{8,10},{9,11},{10,... | collective-permute-start | bytes 1572872 | tf_op jit(solution)/shard_map/ppermute | solution.py:401

commit v2 on v1

--- a/solution.py
+++ b/solution.py
@@ -10,6 +10,7 @@
 
 NX, NZ, NY = 4, 4, 4
 HL = 4
+YR = 72
 TB = 256
 F = 256
 D = 128
@@ -23,7 +24,7 @@
 
 
 def y_pairs(d):
-    return [(y * 2 + c, ((y + d) % NY) * 2 + c) for y in range(NY) for c in range(2)]
+    return [(y * 2 + c, ((y + (d if c == 0 else -d)) % NY) * 2 + c) for y in range(NY) for c in range(2)]
 
 
 CORE_PAIRS = [(y * 2 + c, y * 2 + 1 - c) for y in range(NY) for c in range(2)]
@@ -62,8 +63,12 @@
     return [pl.BlockSpec(memory_space=pltpu.HBM)] * n
 
 
-def place():
-    return [pl.BlockSpec(memory_space=pltpu.SMEM)]
+HERE = object()
+
+
+def here():
+    g, t = lax.axis_index("grp").astype(jnp.int32), lax.axis_index("ctx").astype(jnp.int32)
+    return lax.div(g, NZ), lax.rem(g, NZ), lax.div(t, 2), lax.rem(t, 2)
 
 
 def shape(*dims, kind=F32):
@@ -75,8 +80,15 @@
 
 
 def call(kernel, out_shape, in_specs, out_specs, args, scratch=()):
+    body = kernel
+    if args[0] is HERE:
+        args = args[1:]
+
+        def body(*refs):
+            kernel(here(), *refs)
+
     return pl.pallas_call(
-        kernel,
+        body,
         out_shape=out_shape,
         in_specs=in_specs,
         out_specs=out_specs,
@@ -92,9 +104,9 @@
         c.wait()
 
 
-def pack_kv_kernel(shifts, pos, k_ref, v_ref, *refs):
+def pack_kv_kernel(shifts, k_ref, v_ref, *refs):
     outs, sem = refs[:-1], refs[-1]
-    z = pos[1]
+    z = lax.rem(lax.axis_index("grp").astype(jnp.int32), NZ)
     copies = []
     for i, r in enumerate(shifts):
         zd = mod4(z + r)
@@ -106,14 +118,14 @@
     run_copies(copies)
 
 
-def pack_kv(pos, k, v, shifts):
+def pack_kv(k, v, shifts):
     n = len(shifts)
     return call(
         functools.partial(pack_kv_kernel, shifts),
         [piece(F + D)] * n,
-        place() + hbm(2),
+        hbm(2),
         vmem(n),
-        (pos, k, v),
+        (k, v),
         [pltpu.SemaphoreType.DMA((n, HL, 2))],
     )
 
@@ -134,7 +146,7 @@
     return call(
         functools.partial(pack_q_kernel, shifts),
         [piece(F)] * n,
-        place() + hbm(1),
+        hbm(1),
         vmem(n),
         (pos, q),
         [pltpu.SemaphoreType.DMA((n, HL))],
@@ -155,28 +167,39 @@
     return call(
         pack_teacher_kernel,
         [shape(NZ * TB, D, kind=BF)] * NX,
-        place() + hbm(1),
+        hbm(1),
         vmem(NX),
         (pos, teacher),
         [pltpu.SemaphoreType.DMA((NX,))],
     )
 
 
+UR = 64
+
+
 def unpack_kernel(pos, *refs):
-    parts, out = refs[0:NZ], refs[NZ]
+    parts, out, held, sem = refs[0:NZ], refs[NZ], refs[NZ + 1], refs[NZ + 2]
     z = pos[1]
-    for r in (0, 2, 1, 3):
-        for j in range(HL):
-            out[:, pl.ds(pl.multiple_of((j * NZ + mod4(z - r)) * F, F), F)] = parts[r][j]
+    copies = []
+    for i in range(TB // UR):
+        rows = slice(i * UR, (i + 1) * UR)
+        for r in range(NZ):
+            for j in range(HL):
+                held[rows, pl.ds(pl.multiple_of((j * NZ + mod4(z - r)) * F, F), F)] = parts[r][j, rows, :]
+        copies.append(pltpu.make_async_copy(held.at[rows, :], out.at[rows, :], sem.at[i]))
+        copies[-1].start()
+    for c in copies:
+        c.wait()
 
 
 def unpack_all(pos, parts):
     return call(
         unpack_kernel,
         shape(TB, HL * NZ * F, kind=BF),
-        place() + vmem(NZ),
-        pl.BlockSpec(),
+        vmem(NZ),
+        hbm(1)[0],
         (pos, *parts),
+        [pltpu.VMEM((TB, HL * NZ * F), BF), pltpu.SemaphoreType.DMA((TB // UR,))],
     )
 
 
@@ -194,7 +217,7 @@
 
 
 def sums_a(pos, kv0, kv2):
-    return call(sums_a_kernel, shape(NX, SR, F), place() + vmem(2), vmem(1)[0], (pos, kv0, kv2))
+    return call(sums_a_kernel, shape(NX, SR, F), vmem(2), vmem(1)[0], (pos, kv0, kv2))
 
 
 def sums_b_kernel(pos, kv1, kv3, part, *outs):
@@ -207,9 +230,7 @@
 
 
 def sums_b(pos, kv1, kv3, part):
-    return call(
-        sums_b_kernel, [shape(SR, F)] * NX, place() + vmem(3), vmem(NX), (pos, kv1, kv3, part)
-    )
+    return call(sums_b_kernel, [shape(SR, F)] * NX, vmem(3), vmem(NX), (pos, kv1, kv3, part))
 
 
 def full_state(ref):
@@ -260,7 +281,7 @@
 
 
 def earlier_in_line(pos, kvs):
-    return call(lines_kernel, shape(HL, NZ, SR, F), place() + vmem(4), vmem(1)[0], (pos, *kvs))
+    return call(lines_kernel, shape(HL, NZ, SR, F), vmem(4), vmem(1)[0], (pos, *kvs))
 
 
 def pre_kernel(pos, *refs):
@@ -278,14 +299,15 @@
 
 
 def pre(pos, kvs, qs, lines):
-    return call(
-        pre_kernel, shape(HL, NZ, TB, 2 * D), place() + vmem(9), vmem(1)[0], (pos, *kvs, *qs, lines)
-    )
+    return call(pre_kernel, shape(HL, NZ, TB, 2 * D), vmem(9), vmem(1)[0], (pos, *kvs, *qs, lines))
+
+
+PR = 64
 
 
 def post_kernel(pos, *refs):
     qs, nd, teas, states = refs[0:4], refs[4], refs[5:9], refs[9:13]
-    dhi_out, dlo_out, adj_out, sums = refs[13], refs[14], refs[15], refs[16:20]
+    dhi_out, dlo_out, adj_out, sums, both_s = refs[13], refs[14], refs[15], refs[16:20], refs[20]
     x, z = pos[0], pos[1]
     for r in range(HL):
         hd = mod4(x - r)
@@ -293,17 +315,24 @@
         total = jnp.zeros((SR, F), F32)
         for b in range(NZ):
             q = qs[b][hd]
-            both = nd[r, b] + nt(q, e_hi) + nt(q, e_lo)
-            inverse = 1.0 / both[:, D:]
-            student = both[:, 0:D] * inverse
-            rows = pl.ds(pl.multiple_of(mod4(z - b) * TB, TB), TB)
-            resid = student - teas[r][rows, :].astype(F32)
-            dn = resid * inverse
-            dd = -jnp.sum(resid * student, axis=1, keepdims=True) * inverse
-            d_hi, d_lo = split(jnp.concatenate([dn, dd * (1.0 / D)], axis=1))
-            dhi_out[r, b] = d_hi
-            dlo_out[r, b] = d_lo
-            adj = tn(d_hi, q)[0:SR] + tn(d_lo, q)[0:SR]
+            held = both_s.at[b % 2]
+            held[...] = nd[r, b] + nt(q, e_hi) + nt(q, e_lo)
+            for i in range(TB // PR):
+                rows = slice(i * PR, (i + 1) * PR)
+                inverse = 1.0 / held[rows, D:]
+                student = held[rows, 0:D] * inverse
+                there = pl.ds(pl.multiple_of(mod4(z - b) * TB + i * PR, PR), PR)
+                resid = student - teas[r][there, :].astype(F32)
+                n_hi, n_lo = split(resid * inverse)
+                dd = -jnp.sum(resid * student, axis=1, keepdims=True) * inverse
+                c_hi, c_lo = split(dd * (1.0 / D))
+                dhi_out[r, b, rows, 0:D] = n_hi
+                dhi_out[r, b, rows, D:] = c_hi
+                dlo_out[r, b, rows, 0:D] = n_lo
+                dlo_out[r, b, rows, D:] = c_lo
+            sides = tn(jnp.concatenate([dhi_out[r, b, :, 0:D], dlo_out[r, b, :, 0:D]], axis=1), q)
+            ends = tn(dhi_out[r, b, :, D : D + 8], q) + tn(dlo_out[r, b, :, D : D + 8], q)
+            adj = jnp.concatenate([sides[0:D] + sides[D:], ends], axis=0)
             adj_out[r, b] = adj
             total = total + adj
         sums[(-r) % NX][...] = total
@@ -313,64 +342,65 @@
     out = call(
         post_kernel,
         [shape(HL, NZ, TB, 2 * D, kind=BF)] * 2 + [shape(HL, NZ, SR, F)] + [shape(SR, F)] * NX,
-        place() + vmem(13),
+        vmem(13),
         vmem(3 + NX),
         (pos, *qs, nd, *teas, *states),
+        [pltpu.VMEM((2, TB, 2 * D), F32)],
     )
     return out[0], out[1], out[2], out[3:7]
 
 
-def qgrad_kernel(scale, pos, *refs):
-    kvs, dhi, dlo, lines, states, outs = refs[0:4], refs[4], refs[5], refs[6], refs[7:11], refs[11:15]
+def qgrad_kernel(scale, blocks, pos, *refs):
+    n = len(blocks)
+    kvs, dhi, dlo, lines, states = refs[0:n], refs[n], refs[n + 1], refs[n + 2], refs[n + 3 : n + 7]
+    outs, mixed_out = refs[n + 7 : 2 * n + 7], refs[2 * n + 7]
     x = pos[0]
     mask = causal_mask()
     for r in range(HL):
         hd = mod4(x - r)
-        for b in range(NZ):
-            k = kvs[b][hd, :, 0:F]
-            va = augmented(kvs[b][hd, :, F : F + D])
+        for i, b in enumerate(blocks):
+            k = kvs[i][hd, :, 0:F]
+            va = augmented(kvs[i][hd, :, F : F + D])
             d_hi = dhi[r, b]
             d_rows = jnp.concatenate([d_hi, dlo[r, b]], axis=0)
             mixed = rows_of(jnp.where(mask, halves(nt(d_rows, va)), 0.0))
+            mixed_out[r, i] = mixed
             st_hi, st_lo = split(full_state(states[r][...] + lines[r, b]))
             qg = halves(nn(mixed, k) + nn(d_rows, st_hi)) + nn(d_hi, st_lo)
-            outs[(-b) % NZ][hd] = (qg * scale).astype(BF)
-
-
-def qgrad(pos, kvs, dhi, dlo, lines, states, scale):
-    return call(
-        functools.partial(qgrad_kernel, scale),
-        [piece(F)] * NZ,
-        place() + vmem(11),
-        vmem(NZ),
-        (pos, *kvs, dhi, dlo, lines, *states),
-    )
+            outs[i][hd] = (qg * scale).astype(BF)
+
+
+def qgrad(pos, kvs, dhi, dlo, lines, states, scale, blocks):
+    n = len(blocks)
+    out = call(
+        functools.partial(qgrad_kernel, scale, blocks),
+        [piece(F)] * n + [shape(HL, n, 2 * TB, TB, kind=BF)],
+        vmem(n + 7),
+        vmem(n + 1),
+        (pos, *[kvs[b] for b in blocks], dhi, dlo, lines, *states),
+    )
+    return out[0:n], out[n]
+
+
+REST = (1, 3, 0)
 
 
 def inner_kernel(pos, *refs):
-    kvs, qs, dhi, dlo, adj, out = refs[0:4], refs[4:8], refs[8], refs[9], refs[10], refs[11]
+    kvs, qs, far, rest, adj, out = refs[0:4], refs[4:8], refs[8], refs[9], refs[10], refs[11]
     x, z = pos[0], pos[1]
-    mask = causal_mask()
     for r in range(HL):
         hd = mod4(x - r)
         lines = order_sums(z, [adj[r, b] for b in range(NZ)], True)
         for b in range(NZ):
             q = qs[b][hd]
             va = augmented(kvs[b][hd, :, F : F + D])
-            d_rows = jnp.concatenate([dhi[r, b], dlo[r, b]], axis=0)
-            m_hi, m_lo = split(jnp.where(mask, halves(nt(d_rows, va)), 0.0))
+            mixed = far.at[r, 0] if b == 2 else rest.at[r, REST.index(b)]
             a_hi, a_lo = split(full_state(lines[b]))
-            out[r, b] = tn(m_hi, q) + tn(m_lo, q) + nn(va, a_hi) + nn(va, a_lo)
-
-
-def inner(pos, kvs, qs, dhi, dlo, adj):
-    return call(
-        inner_kernel,
-        shape(HL, NZ, TB, F),
-        place() + vmem(11),
-        vmem(1)[0],
-        (pos, *kvs, *qs, dhi, dlo, adj),
-    )
+            out[r, b] = tn(mixed[0:TB, :], q) + tn(mixed[TB:, :], q) + nn(va, a_hi) + nn(va, a_lo)
+
+
+def inner(pos, kvs, qs, far, rest, adj):
+    return call(inner_kernel, shape(HL, NZ, TB, F), vmem(11), vmem(1)[0], (pos, *kvs, *qs, far, rest, adj))
 
 
 def last_kernel(scale, blocks, pos, *refs):
@@ -391,7 +421,7 @@
     return call(
         functools.partial(last_kernel, scale, blocks),
         [piece(F)] * n,
-        place() + vmem(n + 5),
+        vmem(n + 5),
         vmem(n),
         (pos, *[kvs[b] for b in blocks], part, *states),
     )
@@ -419,22 +449,29 @@
     out[...] = (m0[...] + m1[...]) + (m2[...] + m3[...])
 
 
-def core_kernel(reverse, pos, o1, o2, o3, total, outer, other):
+def chip_kernel(pos, total, other, out, half):
+    out[...] = total[...] + other[...]
+    half[...] = out[pl.ds(pl.multiple_of(pos[3] * (SR - YR), 8), YR), :]
+
+
+def spans_kernel(reverse, pos, near, far, out):
     y, c = pos[2], pos[3]
-    acc = jnp.zeros((SR, F), F32)
-    for d, o in ((1, o1), (2, o2), (3, o3)):
-        at = mod4(y - d)
-        take = (at > y) if reverse else (at < y)
-        acc = acc + o[...] * take.astype(F32)
-    outer[...] = acc
-    first = (c == (1 if reverse else 0)).astype(F32)
-    other[...] = acc + total[...] * first
-
-
-def back_kernel(reverse, pos, outer, other_core, *refs):
+
+    def wanted(at):
+        return ((at > y) if reverse else (at < y)).astype(F32)
+
+    out[...] = near[...] * wanted(mod4(y - 1 + 2 * c))
+    far_wanted = wanted(mod4(y + 2))
+    mine = c.astype(F32)
+    out[0:YR, :] += far[...] * (far_wanted * (1.0 - mine))
+    out[YR:SR, :] += far[2 * YR - SR :, :] * (far_wanted * mine)
+
+
+def back_kernel(reverse, pos, base_a, base_b, other, *refs):
     mine, outs = refs[0:NX], refs[NX:]
-    x = pos[0]
-    base = outer[...] + other_core[...]
+    x, c = pos[0], pos[3]
+    second = (c == (0 if reverse else 1)).astype(F32)
+    base = base_a[...] + base_b[...] + other[...] * second
     for r in range(NX):
         to = mod4(x + r)
         acc = base
@@ -449,17 +486,18 @@
     one = shape(SR, F)
     mine = exchange_x(sums)
     total = call(total_kernel, one, vmem(4), vmem(1)[0], mine)
-    others = [lax.ppermute(total, "ctx", y_pairs(d)) for d in (1, 2, 3)]
-    outer, mixed = call(
-        functools.partial(core_kernel, reverse), [one] * 2, place() + vmem(4), vmem(2), (pos, *others, total)
-    )
-    other_core = lax.ppermute(mixed, "ctx", CORE_PAIRS)
+    other = lax.ppermute(total, "ctx", CORE_PAIRS)
+    chip, half = call(chip_kernel, [one, shape(YR, F)], vmem(2), vmem(2), (pos, total, other))
+    far = lax.ppermute(half, "ctx", y_pairs(2))
+    near = lax.ppermute(chip, "ctx", y_pairs(1))
+    base = call(functools.partial(spans_kernel, reverse), one, vmem(2), vmem(1)[0], (pos, near, far))
+    base_other = lax.ppermute(base, "ctx", CORE_PAIRS)
     back = call(
         functools.partial(back_kernel, reverse),
         [one] * NX,
-        place() + vmem(2 + NX),
+        vmem(3 + NX),
         vmem(NX),
-        (pos, outer, other_core, *mine),
+        (pos, base, base_other, other, *mine),
     )
     return exchange_x(back)
 
@@ -467,16 +505,14 @@
 def local_step(query_feat, key_feat, values, teacher):
     total_tokens = query_feat.shape[0] * lax.axis_size("ctx") * lax.axis_size("grp")
     scale = float(total_tokens) ** 0.5
-    g = lax.axis_index("grp").astype(jnp.int32)
-    x, z = g // NZ, lax.rem(g, NZ)
-    t = lax.axis_index("ctx").astype(jnp.int32)
-    pos = jnp.stack([x, z, t // 2, lax.rem(t, 2)])
+    pos = HERE
     query_feat, key_feat, values, teacher = (
         pltpu.with_memory_space_constraint(a, pltpu.HBM) for a in (query_feat, key_feat, values, teacher)
     )
     kv = [None] * NZ
-    kv[2], kv[1], kv[3] = pack_kv(pos, key_feat, values, (2, 1, 3))
-    (kv[0],) = pack_kv(pos, key_feat, values, (0,))
+    (kv[2],) = pack_kv(key_feat, values, (2,))
+    kv[1], kv[3] = pack_kv(key_feat, values, (1, 3))
+    (kv[0],) = pack_kv(key_feat, values, (0,))
     kvs = exchange_z(kv)
     q = [None] * NZ
     q[2], q[1], q[3] = pack_q(pos, query_feat, (2, 1, 3))
@@ -488,9 +524,11 @@
     nd = pre(pos, kvs, qs, lines)
     states = scan_states(sums, pos, False)
     d_hi, d_lo, adj, adj_sums = post(pos, qs, nd, teas, states)
-    qparts = qgrad(pos, kvs, d_hi, d_lo, lines, states, scale)
+    qparts = [None] * NZ
+    (qparts[2],), far = qgrad(pos, kvs, d_hi, d_lo, lines, states, scale, (2,))
+    (qparts[3], qparts[1], qparts[0]), rest = qgrad(pos, kvs, d_hi, d_lo, lines, states, scale, REST)
     query_grad = unpack_all(pos, exchange_z(qparts))
-    part = inner(pos, kvs, qs, d_hi, d_lo, adj)
+    part = inner(pos, kvs, qs, far, rest, adj)
     after = scan_states(adj_sums, pos, True)
     kg = [None] * NZ
     (kg[2],) = last(pos, kvs, part, after, scale, (2,))

time: 178 us -> 167 us (0.938)
  the two profiles are of different devices: /device:TPU:34 before, /device:TPU:0 now
where the time goes in v2:
time: 167 us; the launch traced here: 165 us
  waiting for transfers between devices  80.2 us (48%)
  starting transfers between devices  54.6 us (33%)
  Pallas kernels  28.6 us (17%)
    ppermute x12, waiting for transfers between devices, send_z(): return lax.ppermute(part, 'grp', grp_pairs(0, r))  57.2 us
    pallas_call x27, Pallas kernels, call(): pl.pallas_call(body, out_shape=out_shape, in_specs=in_specs, out_specs=ou...  28.6 us
    ppermute x15, starting transfers between devices, send_x(): return lax.ppermute(part, 'grp', grp_pairs(r, 0))  24.2 us
    ppermute x12, starting transfers between devices, send_z(): return lax.ppermute(part, 'grp', grp_pairs(0, r))  21.7 us
    ppermute x15, waiting for transfers between devices, send_x(): return lax.ppermute(part, 'grp', grp_pairs(r, 0))  14 us
    ppermute x2, starting transfers between devices, scan_states(): far = lax.ppermute(half, 'ctx', y_pairs(2))  6.17 us
    ppermute x2, waiting for transfers between devices, scan_states(): far = lax.ppermute(half, 'ctx', y_pairs(2))  5.37 us
  transfers between devices with their start and end apart: 35, of which 18 were waited for; matrix products, arithmetic and copies ran while one was open for 0% of the time, Pallas kernels for 13%

profile of v2, /device:TPU:0, one launch (start us, length us, event | category | flops | bytes accessed | tf_op | source)
XLA Modules:
  0.0 164.6 jit_solution(15774055422543089250)
XLA Ops:
  0.6 1.3 shard_map.63
  1.9 4.1 %collective-permute-start.5 = (bf16[4,256,384]{2,1,0:T(8,128)(2,1)S(1)}, bf16[4,256,384]{2,1,0:T(8,128)(2,1)S(1)}, u32[]{:S(2)}, u32[]{:S(2)}) collective-permute-start(bf16[4,256,384]{2,1,0:T(8,128)(2,1)S(1)} %shard_map.63), channel_id=1, source_target_pairs={{0,2},{1,3},{2,0},{3,1},{4,6},{5,7},{6,4},{7,5},{8,10},{9,11},{10,... | collective-permute-start | bytes 2359304 | tf_op jit(solution)/shard_map/ppermute | solution.py:431
  6.0 1.6 shard_map.59
  7.6 1.1 collective-permute-start
  8.7 2.2 %collective-permute-start.1 = (bf16[4,256,384]{2,1,0:T(8,128)(2,1)S(1)}, bf16[4,256,384]{2,1,0:T(8,128)(2,1)S(1)}, u32[]{:S(2)}, u32[]{:S(2)}) collective-permute-start(bf16[4,256,384]{2,1,0:T(8,128)(2,1)S(1)} %get-tuple-element.43), channel_id=1, source_target_pairs={{0,3},{1,0},{2,1},{3,2},{4,7},{5,4},{6,5},{7,6},{8,11},{9,8},{10,9... | collective-permute-start | bytes 2359304 | tf_op jit(solution)/shard_map/ppermute | solution.py:431
  10.9 1.3 shard_map.60.refs_0_.refs_2_
  12.2 12.3 %collective-permute-done.5.refs_2_.refs_1_.refs_0_ = bf16[4,256,384]{2,1,0:T(8,128)(2,1)S(1)} collective-permute-done((bf16[4,256,384]{2,1,0:T(8,128)(2,1)S(1)}, bf16[4,256,384]{2,1,0:T(8,128)(2,1)S(1)}, u32[]{:S(2)}, u32[]{:S(2)}) %collective-permute-start.5) | collective-permute-done | bytes 786464 | tf_op jit(solution)/shard_map/ppermute | solution.py:431
  24.9 15.5 %collective-permute-done.refs_1_.refs_0_ = bf16[4,256,384]{2,1,0:T(8,128)(2,1)S(1)} collective-permute-done((bf16[4,256,384]{2,1,0:T(8,128)(2,1)S(1)}, bf16[4,256,384]{2,1,0:T(8,128)(2,1)S(1)}, u32[]{:S(2)}, u32[]{:S(2)}) %collective-permute-start) | collective-permute-done | bytes 786464 | tf_op jit(solution)/shard_map/ppermute | solution.py:431
  40.4 0.8 collective-permute-done.1.refs_3_.refs_1_
  41.6 1.6 collective-permute-start.9
  43.2 2.7 %collective-permute-start.10 = (f32[136,256]{1,0:T(8,128)S(1)}, f32[136,256]{1,0:T(8,128)S(1)}, u32[]{:S(2)}, u32[]{:S(2)}) collective-permute-start(f32[136,256]{1,0:T(8,128)S(1)} %get-tuple-element.53), channel_id=1, source_target_pairs={{0,8},{1,9},{2,10},{3,11},{4,12},{5,13},{6,14},{7,15},{8,0},{9,1},... | collective-permute-start | bytes 417800 | tf_op jit(solution)/shard_map/ppermute | solution.py:435
  45.9 1.4 collective-permute-start.11
  47.3 1.6 collective-permute-done.9.m1.refs_4_
  48.9 2.8 %collective-permute-done.10.m2.refs_5_ = f32[136,256]{1,0:T(8,128)S(1)} collective-permute-done((f32[136,256]{1,0:T(8,128)S(1)}, f32[136,256]{1,0:T(8,128)S(1)}, u32[]{:S(2)}, u32[]{:S(2)}) %collective-permute-start.10) | collective-permute-done | bytes 139296 | tf_op jit(solution)/shard_map/ppermute | solution.py:435
  51.8 1.6 shard_map.62
  53.4 1.4 collective-permute-start.2
  54.8 3.6 %collective-permute-start.3 = (bf16[4,256,256]{2,1,0:T(8,128)(2,1)S(1)}, bf16[4,256,256]{2,1,0:T(8,128)(2,1)S(1)}, u32[]{:S(2)}, u32[]{:S(2)}) collective-permute-start(bf16[4,256,256]{2,1,0:T(8,128)(2,1)S(1)} %get-tuple-element.45), channel_id=1, source_target_pairs={{0,2},{1,3},{2,0},{3,1},{4,6},{5,7},{6,4},{7,5},{8,10},{9,11},{10,... | collective-permute-start | bytes 1572872 | tf_op jit(solution)/shard_map/ppermute | solution.py:431
  58.3 1.0 collective-permute-start.4
  59.4 3.3 %collective-permute-start.14 = (f32[72,256]{1,0:T(8,128)S(1)}, f32[72,256]{1,0:T(8,128)S(1)}, u32[]{:S(2)}, u32[]{:S(2)}) collective-permute-start(f32[72,256]{1,0:T(8,128)S(1)} %get-tuple-element.56), channel_id=1, source_target_pairs={{0,64},{16,80},{32,96},{48,112},{64,0},{80,16},{96,32},{112,48},{1... | collective-permute-start | bytes 221192 | tf_op jit(solution)/shard_map/ppermute | solution.py:491
  62.7 0.7 collective-permute-start.13
  63.3 1.2 shard_map.66
  64.6 0.8 collective-permute-done.14.refs_1_
  65.3 1.3 collective-permute-start.6
  66.7 2.3 %collective-permute-done.13.refs_0_ = f32[136,256]{1,0:T(8,128)S(1)} collective-permute-done((f32[136,256]{1,0:T(8,128)S(1)}, f32[136,256]{1,0:T(8,128)S(1)}, u32[]{:S(2)}, u32[]{:S(2)}) %collective-permute-start.13) | collective-permute-done | bytes 139296 | tf_op jit(solution)/shard_map/ppermute | solution.py:492
  69.1 4.5 %collective-permute-done.6.refs_6_ = bf16[1024,128]{1,0:T(8,128)(2,1)S(1)} collective-permute-done((bf16[1024,128]{1,0:T(8,128)(2,1)S(1)}, bf16[1024,128]{1,0:T(8,128)(2,1)S(1)}, u32[]{:S(2)}, u32[]{:S(2)}) %collective-permute-start.6) | collective-permute-done | bytes 262176 | tf_op jit(solution)/shard_map/ppermute | solution.py:435
  73.5 1.4 collective-permute-start.7
  75.0 1.4 collective-permute-start.8
  76.5 0.7 collective-permute-start.16
  77.3 4.6 %collective-permute-done.3.refs_6_.refs_2_ = bf16[4,256,256]{2,1,0:T(8,128)(2,1)S(1)} collective-permute-done((bf16[4,256,256]{2,1,0:T(8,128)(2,1)S(1)}, bf16[4,256,256]{2,1,0:T(8,128)(2,1)S(1)}, u32[]{:S(2)}, u32[]{:S(2)}) %collective-permute-start.3) | collective-permute-done | bytes 524320 | tf_op jit(solution)/shard_map/ppermute | solution.py:431
  81.9 2.7 %collective-permute-start.17 = (f32[136,256]{1,0:T(8,128)S(1)}, f32[136,256]{1,0:T(8,128)S(1)}, u32[]{:S(2)}, u32[]{:S(2)}) collective-permute-start(f32[136,256]{1,0:T(8,128)S(1)} %get-tuple-element.59), channel_id=1, source_target_pairs={{0,8},{1,9},{2,10},{3,11},{4,12},{5,13},{6,14},{7,15},{8,0},{9,1},... | collective-permute-start | bytes 417800 | tf_op jit(solution)/shard_map/ppermute | solution.py:435
  84.5 1.4 collective-permute-start.18
  85.9 1.1 shard_map.61.refs_4_.refs_0_
  87.0 0.8 shard_map.64.refs_8_.refs_5_.refs_3_
  87.8 3.5 %shard_map.65.refs_4_ = f32[4,4,256,256]{3,2,1,0:T(8,128)S(1)} custom-call(bf16[4,256,384]{2,1,0:T(8,128)(2,1)S(1)} %shard_map.60.refs_0_.refs_2_, bf16[4,256,384]{2,1,0:T(8,128)(2,1)S(1)} %collective-permute-done.refs_1_.refs_0_, bf16[4,256,384]{2,1,0:T(8,128)(2,1)S(1)} %collective-permute-done.5.refs_2_.refs_1_.refs_0_, ...), custom_call_target="tpu_custom_call" | custom-call | tf_op jit(solution)/shard_map/pallas_call | solution.py:90
  91.4 3.6 %shard_map.73 = (bf16[4,4,256,256]{3,2,1,0:T(8,128)(2,1)S(1)}, bf16[4,4,256,256]{3,2,1,0:T(8,128)(2,1)S(1)}, f32[4,4,136,256]{3,2,1,0:T(8,128)S(1)}, f32[136,256...) custom-call(bf16[4,256,256]{2,1,0:T(8,128)(2,1)S(1)} %shard_map.61.refs_4_.refs_0_, ...), custom_call_target="tpu_custom_call" | custom-call | tf_op jit(solution)/shard_map/pallas_call | solution.py:90
  94.9 1.5 collective-permute-start.22
  96.5 2.4 %collective-permute-start.23 = (f32[136,256]{1,0:T(8,128)S(1)}, f32[136,256]{1,0:T(8,128)S(1)}, u32[]{:S(2)}, u32[]{:S(2)}) collective-permute-start(f32[136,256]{1,0:T(8,128)S(1)} %get-tuple-element.72), channel_id=1, source_target_pairs={{0,8},{1,9},{2,10},{3,11},{4,12},{5,13},{6,14},{7,15},{8,0},{9,1},... | collective-permute-start | bytes 417800 | tf_op jit(solution)/shard_map/ppermute | solution.py:435
  98.9 0.9 collective-permute-start.24
  99.8 2.2 %collective-permute-done.22.m1.refs_4_ = f32[136,256]{1,0:T(8,128)S(1)} collective-permute-done((f32[136,256]{1,0:T(8,128)S(1)}, f32[136,256]{1,0:T(8,128)S(1)}, u32[]{:S(2)}, u32[]{:S(2)}) %collective-permute-start.22) | collective-permute-done | bytes 139296 | tf_op jit(solution)/shard_map/ppermute | solution.py:435
  101.9 3.0 %collective-permute-done.23.m2.refs_5_ = f32[136,256]{1,0:T(8,128)S(1)} collective-permute-done((f32[136,256]{1,0:T(8,128)S(1)}, f32[136,256]{1,0:T(8,128)S(1)}, u32[]{:S(2)}, u32[]{:S(2)}) %collective-permute-start.23) | collective-permute-done | bytes 139296 | tf_op jit(solution)/shard_map/ppermute | solution.py:435
  105.1 1.2 shard_map.75
  106.3 0.5 collective-permute-start.20
  106.9 1.6 collective-permute-start.26
  108.4 2.9 %collective-permute-start.27 = (f32[72,256]{1,0:T(8,128)S(1)}, f32[72,256]{1,0:T(8,128)S(1)}, u32[]{:S(2)}, u32[]{:S(2)}) collective-permute-start(f32[72,256]{1,0:T(8,128)S(1)} %get-tuple-element.75), channel_id=1, source_target_pairs={{0,64},{16,80},{32,96},{48,112},{64,0},{80,16},{96,32},{112,48},{1... | collective-permute-start | bytes 221192 | tf_op jit(solution)/shard_map/ppermute | solution.py:491
  111.3 4.6 %collective-permute-done.27.refs_1_ = f32[72,256]{1,0:T(8,128)S(1)} collective-permute-done((f32[72,256]{1,0:T(8,128)S(1)}, f32[72,256]{1,0:T(8,128)S(1)}, u32[]{:S(2)}, u32[]{:S(2)}) %collective-permute-start.27) | collective-permute-done | bytes 73760 | tf_op jit(solution)/shard_map/ppermute | solution.py:491
  116.1 1.3 collective-permute-done.28.refs_1_
  117.6 1.0 collective-permute-start.29
  118.7 3.1 %collective-permute-start.30 = (f32[136,256]{1,0:T(8,128)S(1)}, f32[136,256]{1,0:T(8,128)S(1)}, u32[]{:S(2)}, u32[]{:S(2)}) collective-permute-start(f32[136,256]{1,0:T(8,128)S(1)} %get-tuple-element.78), channel_id=1, source_target_pairs={{0,8},{1,9},{2,10},{3,11},{4,12},{5,13},{6,14},{7,15},{8,0},{9,1},... | collective-permute-start | bytes 417800 | tf_op jit(solution)/shard_map/ppermute | solution.py:435
  121.8 0.6 collective-permute-start.31
  122.4 3.2 %shard_map.74 = (bf16[4,256,256]{2,1,0:T(8,128)(2,1)S(1)}, bf16[4,256,256]{2,1,0:T(8,128)(2,1)S(1)}, bf16[4,256,256]{2,1,0:T(8,128)(2,1)S(1)}, bf16[4,3,512,256]{3,2,1,0:T(8,128)(2,1)S(1)}) custom-call(bf16[4,256,384]{2,1,0:T(8,128)(2,1)S(1)} %collective-permute-done.refs_1_.refs_0_, bf16[4,256,384]{2,1,0:T(8,128)(2,1)S(1)} %collective-permute-done.1.refs_3_.refs_1_, ...), custom_call_target="tpu_custom_call" | custom-call | tf_op jit(solution)/shard_map/pallas_call | solution.py:90
  125.5 0.6 collective-permute-start.19
  126.1 2.4 %shard_map.77.refs_1_.refs_2_ = f32[4,4,256,256]{3,2,1,0:T(8,128)S(1)} custom-call(bf16[4,256,384]{2,1,0:T(8,128)(2,1)S(1)} %shard_map.60.refs_0_.refs_2_, bf16[4,256,384]{2,1,0:T(8,128)(2,1)S(1)} %collective-permute-done.refs_1_.refs_0_, bf16[4,256,384]{2,1,0:T(8,128)(2,1)S(1)} %collective-permute-done.5.refs_2_.refs_1_.refs_0_, ...), custom_call_target="tpu_custom_call" | custom-call | tf_op jit(solution)/shard_map/pallas_call | solution.py:90
  128.5 2.8 %collective-permute-start.21 = (bf16[4,256,256]{2,1,0:T(8,128)(2,1)S(1)}, bf16[4,256,256]{2,1,0:T(8,128)(2,1)S(1)}, u32[]{:S(2)}, u32[]{:S(2)}) collective-permute-start(bf16[4,256,256]{2,1,0:T(8,128)(2,1)S(1)} %get-tuple-element.66), channel_id=1, source_target_pairs={{0,3},{1,0},{2,1},{3,2},{4,7},{5,4},{6,5},{7,6},{8,11},{9,8},{10,9... | collective-permute-start | bytes 1572872 | tf_op jit(solution)/shard_map/ppermute | solution.py:431
  131.4 0.7 shard_map.83
  132.4 3.0 %collective-permute-start.34 = (bf16[4,256,256]{2,1,0:T(8,128)(2,1)S(1)}, bf16[4,256,256]{2,1,0:T(8,128)(2,1)S(1)}, u32[]{:S(2)}, u32[]{:S(2)}) collective-permute-start(bf16[4,256,256]{2,1,0:T(8,128)(2,1)S(1)} %get-tuple-element.81), channel_id=1, source_target_pairs={{0,3},{1,0},{2,1},{3,2},{4,7},{5,4},{6,5},{7,6},{8,11},{9,8},{10,9... | collective-permute-start | bytes 1572872 | tf_op jit(solution)/shard_map/ppermute | solution.py:431
  135.8 1.1 collective-permute-start.33
  137.0 4.6 %collective-permute-done.19.refs_1_ = bf16[4,256,256]{2,1,0:T(8,128)(2,1)S(1)} collective-permute-done((bf16[4,256,256]{2,1,0:T(8,128)(2,1)S(1)}, bf16[4,256,256]{2,1,0:T(8,128)(2,1)S(1)}, u32[]{:S(2)}, u32[]{:S(2)}) %collective-permute-start.19) | collective-permute-done | bytes 524320 | tf_op jit(solution)/shard_map/ppermute | solution.py:431
  141.6 2.7 %collective-permute-done.21.refs_3_ = bf16[4,256,256]{2,1,0:T(8,128)(2,1)S(1)} collective-permute-done((bf16[4,256,256]{2,1,0:T(8,128)(2,1)S(1)}, bf16[4,256,256]{2,1,0:T(8,128)(2,1)S(1)}, u32[]{:S(2)}, u32[]{:S(2)}) %collective-permute-start.21) | collective-permute-done | bytes 524320 | tf_op jit(solution)/shard_map/ppermute | solution.py:431
  144.3 1.4 shard_map.76
  145.8 0.4 shard_map.82.refs_0_
  146.2 5.9 %collective-permute-done.32.refs_1_ = bf16[4,256,256]{2,1,0:T(8,128)(2,1)S(1)} collective-permute-done((bf16[4,256,256]{2,1,0:T(8,128)(2,1)S(1)}, bf16[4,256,256]{2,1,0:T(8,128)(2,1)S(1)}, u32[]{:S(2)}, u32[]{:S(2)}) %collective-permute-start.32) | collective-permute-done | bytes 524320 | tf_op jit(solution)/shard_map/ppermute | solution.py:431
  152.1 3.5 %collective-permute-done.34.refs_3_ = bf16[4,256,256]{2,1,0:T(8,128)(2,1)S(1)} collective-permute-done((bf16[4,256,256]{2,1,0:T(8,128)(2,1)S(1)}, bf16[4,256,256]{2,1,0:T(8,128)(2,1)S(1)}, u32[]{:S(2)}, u32[]{:S(2)}) %collective-permute-start.34) | collective-permute-done | bytes 524320 | tf_op jit(solution)/shard_map/ppermute | solution.py:431
  155.6 7.4 %collective-permute-done.33.refs_2_ = bf16[4,256,256]{2,1,0:T(8,128)(2,1)S(1)} collective-permute-done((bf16[4,256,256]{2,1,0:T(8,128)(2,1)S(1)}, bf16[4,256,256]{2,1,0:T(8,128)(2,1)S(1)}, u32[]{:S(2)}, u32[]{:S(2)}) %collective-permute-start.33) | collective-permute-done | bytes 524320 | tf_op jit(solution)/shard_map/ppermute | solution.py:431
  163.0 1.4 shard_map.85
  (33 shorter events, 2.6 us)
Async XLA Ops:
  1.9 22.5 %collective-permute-start.5 = (bf16[4,256,384]{2,1,0:T(8,128)(2,1)S(1)}, bf16[4,256,384]{2,1,0:T(8,128)(2,1)S(1)}, u32[]{:S(2)}, u32[]{:S(2)}) collective-permute-start(bf16[4,256,384]{2,1,0:T(8,128)(2,1)S(1)} %shard_map.63), channel_id=1, source_target_pairs={{0,2},{1,3},{2,0},{3,1},{4,6},{5,7},{6,4},{7,5},{8,10},{9,11},{10,... | collective-permute-start | bytes 2359304 | tf_op jit(solution)/shard_map/ppermute | solution.py:431
  7.6 32.8 %collective-permute-start = (bf16[4,256,384]{2,1,0:T(8,128)(2,1)S(1)}, bf16[4,256,384]{2,1,0:T(8,128)(2,1)S(1)}, u32[]{:S(2)}, u32[]{:S(2)}) collective-permute-start(bf16[4,256,384]{2,1,0:T(8,128)(2,1)S(1)} %get-tuple-element.42), channel_id=1, source_target_pairs={{0,1},{1,2},{2,3},{3,0},{4,5},{5,6},{6,7},{7,4},{8,9},{9,10},{10,1... | collective-permute-start | bytes 2359304 | tf_op jit(solution)/shard_map/ppermute | solution.py:431
  8.7 32.5 %collective-permute-start.1 = (bf16[4,256,384]{2,1,0:T(8,128)(2,1)S(1)}, bf16[4,256,384]{2,1,0:T(8,128)(2,1)S(1)}, u32[]{:S(2)}, u32[]{:S(2)}) collective-permute-start(bf16[4,256,384]{2,1,0:T(8,128)(2,1)S(1)} %get-tuple-element.43), channel_id=1, source_target_pairs={{0,3},{1,0},{2,1},{3,2},{4,7},{5,4},{6,5},{7,6},{8,11},{9,8},{10,9... | collective-permute-start | bytes 2359304 | tf_op jit(solution)/shard_map/ppermute | solution.py:431
  41.6 7.3 %collective-permute-start.9 = (f32[136,256]{1,0:T(8,128)S(1)}, f32[136,256]{1,0:T(8,128)S(1)}, u32[]{:S(2)}, u32[]{:S(2)}) collective-permute-start(f32[136,256]{1,0:T(8,128)S(1)} %get-tuple-element.52), channel_id=1, source_target_pairs={{0,4},{1,5},{2,6},{3,7},{4,8},{5,9},{6,10},{7,11},{8,12},{9,13},{1... | collective-permute-start | bytes 417800 | tf_op jit(solution)/shard_map/ppermute | solution.py:435
  43.2 8.5 %collective-permute-start.10 = (f32[136,256]{1,0:T(8,128)S(1)}, f32[136,256]{1,0:T(8,128)S(1)}, u32[]{:S(2)}, u32[]{:S(2)}) collective-permute-start(f32[136,256]{1,0:T(8,128)S(1)} %get-tuple-element.53), channel_id=1, source_target_pairs={{0,8},{1,9},{2,10},{3,11},{4,12},{5,13},{6,14},{7,15},{8,0},{9,1},... | collective-permute-start | bytes 417800 | tf_op jit(solution)/shard_map/ppermute | solution.py:435
  45.9 5.8 %collective-permute-start.11 = (f32[136,256]{1,0:T(8,128)S(1)}, f32[136,256]{1,0:T(8,128)S(1)}, u32[]{:S(2)}, u32[]{:S(2)}) collective-permute-start(f32[136,256]{1,0:T(8,128)S(1)} %get-tuple-element.54), channel_id=1, source_target_pairs={{0,12},{1,13},{2,14},{3,15},{4,0},{5,1},{6,2},{7,3},{8,4},{9,5},{1... | collective-permute-start | bytes 417800 | tf_op jit(solution)/shard_map/ppermute | solution.py:435
  51.7 7.6 %collective-permute-start.12 = (f32[136,256]{1,0:T(8,128)S(1)}, f32[136,256]{1,0:T(8,128)S(1)}, u32[]{:S(2)}, u32[]{:S(2)}) collective-permute-start(f32[136,256]{1,0:T(8,128)S(1)} %shard_map.69.refs_0_), channel_id=1, source_target_pairs={{0,16},{16,0},{32,48},{48,32},{64,80},{80,64},{96,112},{112,96},{1... | collective-permute-start | bytes 417800 | tf_op jit(solution)/shard_map/ppermute | solution.py:489
  53.4 23.1 %collective-permute-start.2 = (bf16[4,256,256]{2,1,0:T(8,128)(2,1)S(1)}, bf16[4,256,256]{2,1,0:T(8,128)(2,1)S(1)}, u32[]{:S(2)}, u32[]{:S(2)}) collective-permute-start(bf16[4,256,256]{2,1,0:T(8,128)(2,1)S(1)} %get-tuple-element.44), channel_id=1, source_target_pairs={{0,1},{1,2},{2,3},{3,0},{4,5},{5,6},{6,7},{7,4},{8,9},{9,10},{10,1... | collective-permute-start | bytes 1572872 | tf_op jit(solution)/shard_map/ppermute | solution.py:431
  54.8 27.1 %collective-permute-start.3 = (bf16[4,256,256]{2,1,0:T(8,128)(2,1)S(1)}, bf16[4,256,256]{2,1,0:T(8,128)(2,1)S(1)}, u32[]{:S(2)}, u32[]{:S(2)}) collective-permute-start(bf16[4,256,256]{2,1,0:T(8,128)(2,1)S(1)} %get-tuple-element.45), channel_id=1, source_target_pairs={{0,2},{1,3},{2,0},{3,1},{4,6},{5,7},{6,4},{7,5},{8,10},{9,11},{10,... | collective-permute-start | bytes 1572872 | tf_op jit(solution)/shard_map/ppermute | solution.py:431
  58.3 26.2 %collective-permute-start.4 = (bf16[4,256,256]{2,1,0:T(8,128)(2,1)S(1)}, bf16[4,256,256]{2,1,0:T(8,128)(2,1)S(1)}, u32[]{:S(2)}, u32[]{:S(2)}) collective-permute-start(bf16[4,256,256]{2,1,0:T(8,128)(2,1)S(1)} %get-tuple-element.46), channel_id=1, source_target_pairs={{0,3},{1,0},{2,1},{3,2},{4,7},{5,4},{6,5},{7,6},{8,11},{9,8},{10,9... | collective-permute-start | bytes 1572872 | tf_op jit(solution)/shard_map/ppermute | solution.py:431
  59.4 5.9 %collective-permute-start.14 = (f32[72,256]{1,0:T(8,128)S(1)}, f32[72,256]{1,0:T(8,128)S(1)}, u32[]{:S(2)}, u32[]{:S(2)}) collective-permute-start(f32[72,256]{1,0:T(8,128)S(1)} %get-tuple-element.56), channel_id=1, source_target_pairs={{0,64},{16,80},{32,96},{48,112},{64,0},{80,16},{96,32},{112,48},{1... | collective-permute-start | bytes 221192 | tf_op jit(solution)/shard_map/ppermute | solution.py:491
  62.7 6.3 %collective-permute-start.13 = (f32[136,256]{1,0:T(8,128)S(1)}, f32[136,256]{1,0:T(8,128)S(1)}, u32[]{:S(2)}, u32[]{:S(2)}) collective-permute-start(f32[136,256]{1,0:T(8,128)S(1)} %get-tuple-element.55), channel_id=1, source_target_pairs={{0,32},{16,112},{32,64},{48,16},{64,96},{80,48},{96,0},{112,80},{1... | collective-permute-start | bytes 417800 | tf_op jit(solution)/shard_map/ppermute | solution.py:492
  65.3 8.2 %collective-permute-start.6 = (bf16[1024,128]{1,0:T(8,128)(2,1)S(1)}, bf16[1024,128]{1,0:T(8,128)(2,1)S(1)}, u32[]{:S(2)}, u32[]{:S(2)}) collective-permute-start(bf16[1024,128]{1,0:T(8,128)(2,1)S(1)} %get-tuple-element.48), channel_id=1, source_target_pairs={{0,4},{1,5},{2,6},{3,7},{4,8},{5,9},{6,10},{7,11},{8,12},{9,13},{1... | collective-permute-start | bytes 786440 | tf_op jit(solution)/shard_map/ppermute | solution.py:435
  69.0 6.0 %collective-permute-start.15 = (f32[136,256]{1,0:T(8,128)S(1)}, f32[136,256]{1,0:T(8,128)S(1)}, u32[]{:S(2)}, u32[]{:S(2)}) collective-permute-start(f32[136,256]{1,0:T(8,128)S(1)} %shard_map.71.refs_0_), channel_id=1, source_target_pairs={{0,16},{16,0},{32,48},{48,32},{64,80},{80,64},{96,112},{112,96},{1... | collective-permute-start | bytes 417800 | tf_op jit(solution)/shard_map/ppermute | solution.py:494
  73.5 17.8 %collective-permute-start.7 = (bf16[1024,128]{1,0:T(8,128)(2,1)S(1)}, bf16[1024,128]{1,0:T(8,128)(2,1)S(1)}, u32[]{:S(2)}, u32[]{:S(2)}) collective-permute-start(bf16[1024,128]{1,0:T(8,128)(2,1)S(1)} %get-tuple-element.49), channel_id=1, source_target_pairs={{0,8},{1,9},{2,10},{3,11},{4,12},{5,13},{6,14},{7,15},{8,0},{9,1},... | collective-permute-start | bytes 786440 | tf_op jit(solution)/shard_map/ppermute | solution.py:435
  75.0 16.4 %collective-permute-start.8 = (bf16[1024,128]{1,0:T(8,128)(2,1)S(1)}, bf16[1024,128]{1,0:T(8,128)(2,1)S(1)}, u32[]{:S(2)}, u32[]{:S(2)}) collective-permute-start(bf16[1024,128]{1,0:T(8,128)(2,1)S(1)} %get-tuple-element.50), channel_id=1, source_target_pairs={{0,12},{1,13},{2,14},{3,15},{4,0},{5,1},{6,2},{7,3},{8,4},{9,5},{1... | collective-permute-start | bytes 786440 | tf_op jit(solution)/shard_map/ppermute | solution.py:435
  76.5 14.8 %collective-permute-start.16 = (f32[136,256]{1,0:T(8,128)S(1)}, f32[136,256]{1,0:T(8,128)S(1)}, u32[]{:S(2)}, u32[]{:S(2)}) collective-permute-start(f32[136,256]{1,0:T(8,128)S(1)} %get-tuple-element.58), channel_id=1, source_target_pairs={{0,4},{1,5},{2,6},{3,7},{4,8},{5,9},{6,10},{7,11},{8,12},{9,13},{1... | collective-permute-start | bytes 417800 | tf_op jit(solution)/shard_map/ppermute | solution.py:435
  81.9 9.5 %collective-permute-start.17 = (f32[136,256]{1,0:T(8,128)S(1)}, f32[136,256]{1,0:T(8,128)S(1)}, u32[]{:S(2)}, u32[]{:S(2)}) collective-permute-start(f32[136,256]{1,0:T(8,128)S(1)} %get-tuple-element.59), channel_id=1, source_target_pairs={{0,8},{1,9},{2,10},{3,11},{4,12},{5,13},{6,14},{7,15},{8,0},{9,1},... | collective-permute-start | bytes 417800 | tf_op jit(solution)/shard_map/ppermute | solution.py:435
  84.5 6.8 %collective-permute-start.18 = (f32[136,256]{1,0:T(8,128)S(1)}, f32[136,256]{1,0:T(8,128)S(1)}, u32[]{:S(2)}, u32[]{:S(2)}) collective-permute-start(f32[136,256]{1,0:T(8,128)S(1)} %get-tuple-element.60), channel_id=1, source_target_pairs={{0,12},{1,13},{2,14},{3,15},{4,0},{5,1},{6,2},{7,3},{8,4},{9,5},{1... | collective-permute-start | bytes 417800 | tf_op jit(solution)/shard_map/ppermute | solution.py:435
  94.9 7.0 %collective-permute-start.22 = (f32[136,256]{1,0:T(8,128)S(1)}, f32[136,256]{1,0:T(8,128)S(1)}, u32[]{:S(2)}, u32[]{:S(2)}) collective-permute-start(f32[136,256]{1,0:T(8,128)S(1)} %get-tuple-element.71), channel_id=1, source_target_pairs={{0,4},{1,5},{2,6},{3,7},{4,8},{5,9},{6,10},{7,11},{8,12},{9,13},{1... | collective-permute-start | bytes 417800 | tf_op jit(solution)/shard_map/ppermute | solution.py:435
  96.5 8.5 %collective-permute-start.23 = (f32[136,256]{1,0:T(8,128)S(1)}, f32[136,256]{1,0:T(8,128)S(1)}, u32[]{:S(2)}, u32[]{:S(2)}) collective-permute-start(f32[136,256]{1,0:T(8,128)S(1)} %get-tuple-element.72), channel_id=1, source_target_pairs={{0,8},{1,9},{2,10},{3,11},{4,12},{5,13},{6,14},{7,15},{8,0},{9,1},... | collective-permute-start | bytes 417800 | tf_op jit(solution)/shard_map/ppermute | solution.py:435
  98.9 6.1 %collective-permute-start.24 = (f32[136,256]{1,0:T(8,128)S(1)}, f32[136,256]{1,0:T(8,128)S(1)}, u32[]{:S(2)}, u32[]{:S(2)}) collective-permute-start(f32[136,256]{1,0:T(8,128)S(1)} %get-tuple-element.73), channel_id=1, source_target_pairs={{0,12},{1,13},{2,14},{3,15},{4,0},{5,1},{6,2},{7,3},{8,4},{9,5},{1... | collective-permute-start | bytes 417800 | tf_op jit(solution)/shard_map/ppermute | solution.py:435
  105.0 1.8 %collective-permute-start.25 = (f32[136,256]{1,0:T(8,128)S(1)}, f32[136,256]{1,0:T(8,128)S(1)}, u32[]{:S(2)}, u32[]{:S(2)}) collective-permute-start(f32[136,256]{1,0:T(8,128)S(1)} %shard_map.78.refs_0_), channel_id=1, source_target_pairs={{0,16},{16,0},{32,48},{48,32},{64,80},{80,64},{96,112},{112,96},{1... | collective-permute-start | bytes 417800 | tf_op jit(solution)/shard_map/ppermute | solution.py:489
  106.3 29.5 %collective-permute-start.20 = (bf16[4,256,256]{2,1,0:T(8,128)(2,1)S(1)}, bf16[4,256,256]{2,1,0:T(8,128)(2,1)S(1)}, u32[]{:S(2)}, u32[]{:S(2)}) collective-permute-start(bf16[4,256,256]{2,1,0:T(8,128)(2,1)S(1)} %get-tuple-element.65), channel_id=1, source_target_pairs={{0,2},{1,3},{2,0},{3,1},{4,6},{5,7},{6,4},{7,5},{8,10},{9,11},{10,... | collective-permute-start | bytes 1572872 | tf_op jit(solution)/shard_map/ppermute | solution.py:431
  106.9 9.1 %collective-permute-start.26 = (f32[136,256]{1,0:T(8,128)S(1)}, f32[136,256]{1,0:T(8,128)S(1)}, u32[]{:S(2)}, u32[]{:S(2)}) collective-permute-start(f32[136,256]{1,0:T(8,128)S(1)} %get-tuple-element.74), channel_id=1, source_target_pairs={{0,32},{16,112},{32,64},{48,16},{64,96},{80,48},{96,0},{112,80},{1... | collective-permute-start | bytes 417800 | tf_op jit(solution)/shard_map/ppermute | solution.py:492
  108.4 7.5 %collective-permute-start.27 = (f32[72,256]{1,0:T(8,128)S(1)}, f32[72,256]{1,0:T(8,128)S(1)}, u32[]{:S(2)}, u32[]{:S(2)}) collective-permute-start(f32[72,256]{1,0:T(8,128)S(1)} %get-tuple-element.75), channel_id=1, source_target_pairs={{0,64},{16,80},{32,96},{48,112},{64,0},{80,16},{96,32},{112,48},{1... | collective-permute-start | bytes 221192 | tf_op jit(solution)/shard_map/ppermute | solution.py:491
  116.0 1.4 collective-permute-start.28
  117.6 10.9 %collective-permute-start.29 = (f32[136,256]{1,0:T(8,128)S(1)}, f32[136,256]{1,0:T(8,128)S(1)}, u32[]{:S(2)}, u32[]{:S(2)}) collective-permute-start(f32[136,256]{1,0:T(8,128)S(1)} %get-tuple-element.77), channel_id=1, source_target_pairs={{0,4},{1,5},{2,6},{3,7},{4,8},{5,9},{6,10},{7,11},{8,12},{9,13},{1... | collective-permute-start | bytes 417800 | tf_op jit(solution)/shard_map/ppermute | solution.py:435
  118.7 12.7 %collective-permute-start.30 = (f32[136,256]{1,0:T(8,128)S(1)}, f32[136,256]{1,0:T(8,128)S(1)}, u32[]{:S(2)}, u32[]{:S(2)}) collective-permute-start(f32[136,256]{1,0:T(8,128)S(1)} %get-tuple-element.78), channel_id=1, source_target_pairs={{0,8},{1,9},{2,10},{3,11},{4,12},{5,13},{6,14},{7,15},{8,0},{9,1},... | collective-permute-start | bytes 417800 | tf_op jit(solution)/shard_map/ppermute | solution.py:435
  121.8 9.6 %collective-permute-start.31 = (f32[136,256]{1,0:T(8,128)S(1)}, f32[136,256]{1,0:T(8,128)S(1)}, u32[]{:S(2)}, u32[]{:S(2)}) collective-permute-start(f32[136,256]{1,0:T(8,128)S(1)} %get-tuple-element.79), channel_id=1, source_target_pairs={{0,12},{1,13},{2,14},{3,15},{4,0},{5,1},{6,2},{7,3},{8,4},{9,5},{1... | collective-permute-start | bytes 417800 | tf_op jit(solution)/shard_map/ppermute | solution.py:435
  125.5 16.1 %collective-permute-start.19 = (bf16[4,256,256]{2,1,0:T(8,128)(2,1)S(1)}, bf16[4,256,256]{2,1,0:T(8,128)(2,1)S(1)}, u32[]{:S(2)}, u32[]{:S(2)}) collective-permute-start(bf16[4,256,256]{2,1,0:T(8,128)(2,1)S(1)} %get-tuple-element.64), channel_id=1, source_target_pairs={{0,1},{1,2},{2,3},{3,0},{4,5},{5,6},{6,7},{7,4},{8,9},{9,10},{10,1... | collective-permute-start | bytes 1572872 | tf_op jit(solution)/shard_map/ppermute | solution.py:431
  128.5 15.8 %collective-permute-start.21 = (bf16[4,256,256]{2,1,0:T(8,128)(2,1)S(1)}, bf16[4,256,256]{2,1,0:T(8,128)(2,1)S(1)}, u32[]{:S(2)}, u32[]{:S(2)}) collective-permute-start(bf16[4,256,256]{2,1,0:T(8,128)(2,1)S(1)} %get-tuple-element.66), channel_id=1, source_target_pairs={{0,3},{1,0},{2,1},{3,2},{4,7},{5,4},{6,5},{7,6},{8,11},{9,8},{10,9... | collective-permute-start | bytes 1572872 | tf_op jit(solution)/shard_map/ppermute | solution.py:431
  132.1 20.0 %collective-permute-start.32 = (bf16[4,256,256]{2,1,0:T(8,128)(2,1)S(1)}, bf16[4,256,256]{2,1,0:T(8,128)(2,1)S(1)}, u32[]{:S(2)}, u32[]{:S(2)}) collective-permute-start(bf16[4,256,256]{2,1,0:T(8,128)(2,1)S(1)} %get-tuple-element.80), channel_id=1, source_target_pairs={{0,1},{1,2},{2,3},{3,0},{4,5},{5,6},{6,7},{7,4},{8,9},{9,10},{10,1... | collective-permute-start | bytes 1572872 | tf_op jit(solution)/shard_map/ppermute | solution.py:431
  132.4 23.2 %collective-permute-start.34 = (bf16[4,256,256]{2,1,0:T(8,128)(2,1)S(1)}, bf16[4,256,256]{2,1,0:T(8,128)(2,1)S(1)}, u32[]{:S(2)}, u32[]{:S(2)}) collective-permute-start(bf16[4,256,256]{2,1,0:T(8,128)(2,1)S(1)} %get-tuple-element.81), channel_id=1, source_target_pairs={{0,3},{1,0},{2,1},{3,2},{4,7},{5,4},{6,5},{7,6},{8,11},{9,8},{10,9... | collective-permute-start | bytes 1572872 | tf_op jit(solution)/shard_map/ppermute | solution.py:431
  135.8 27.1 %collective-permute-start.33 = (bf16[4,256,256]{2,1,0:T(8,128)(2,1)S(1)}, bf16[4,256,256]{2,1,0:T(8,128)(2,1)S(1)}, u32[]{:S(2)}, u32[]{:S(2)}) collective-permute-start(bf16[4,256,256]{2,1,0:T(8,128)(2,1)S(1)} %shard_map.84), channel_id=1, source_target_pairs={{0,2},{1,3},{2,0},{3,1},{4,6},{5,7},{6,4},{7,5},{8,10},{9,11},{10,... | collective-permute-start | bytes 1572872 | tf_op jit(solution)/shard_map/ppermute | solution.py:431

commit v3 on v2

--- a/solution.py
+++ b/solution.py
@@ -302,7 +302,7 @@
     return call(pre_kernel, shape(HL, NZ, TB, 2 * D), vmem(9), vmem(1)[0], (pos, *kvs, *qs, lines))
 
 
-PR = 64
+PR = 32
 
 
 def post_kernel(pos, *refs):
@@ -382,11 +382,12 @@
     return out[0:n], out[n]
 
 
-REST = (1, 3, 0)
+NEAR = (1, 3)
 
 
 def inner_kernel(pos, *refs):
-    kvs, qs, far, rest, adj, out = refs[0:4], refs[4:8], refs[8], refs[9], refs[10], refs[11]
+    kvs, qs, far, near, own, adj, out = refs[0:4], refs[4:8], refs[8], refs[9], refs[10], refs[11], refs[12]
+    held = {2: (far, 0), 0: (own, 0), 1: (near, 0), 3: (near, 1)}
     x, z = pos[0], pos[1]
     for r in range(HL):
         hd = mod4(x - r)
@@ -394,13 +395,13 @@
         for b in range(NZ):
             q = qs[b][hd]
             va = augmented(kvs[b][hd, :, F : F + D])
-            mixed = far.at[r, 0] if b == 2 else rest.at[r, REST.index(b)]
+            mixed = held[b][0].at[r, held[b][1]]
             a_hi, a_lo = split(full_state(lines[b]))
             out[r, b] = tn(mixed[0:TB, :], q) + tn(mixed[TB:, :], q) + nn(va, a_hi) + nn(va, a_lo)
 
 
-def inner(pos, kvs, qs, far, rest, adj):
-    return call(inner_kernel, shape(HL, NZ, TB, F), vmem(11), vmem(1)[0], (pos, *kvs, *qs, far, rest, adj))
+def inner(pos, kvs, qs, far, near, own, adj):
+    return call(inner_kernel, shape(HL, NZ, TB, F), vmem(12), vmem(1)[0], (pos, *kvs, *qs, far, near, own, adj))
 
 
 def last_kernel(scale, blocks, pos, *refs):
@@ -526,9 +527,10 @@
     d_hi, d_lo, adj, adj_sums = post(pos, qs, nd, teas, states)
     qparts = [None] * NZ
     (qparts[2],), far = qgrad(pos, kvs, d_hi, d_lo, lines, states, scale, (2,))
-    (qparts[3], qparts[1], qparts[0]), rest = qgrad(pos, kvs, d_hi, d_lo, lines, states, scale, REST)
+    (qparts[3], qparts[1]), near = qgrad(pos, kvs, d_hi, d_lo, lines, states, scale, NEAR)
+    (qparts[0],), own = qgrad(pos, kvs, d_hi, d_lo, lines, states, scale, (0,))
     query_grad = unpack_all(pos, exchange_z(qparts))
-    part = inner(pos, kvs, qs, far, rest, adj)
+    part = inner(pos, kvs, qs, far, near, own, adj)
     after = scan_states(adj_sums, pos, True)
     kg = [None] * NZ
     (kg[2],) = last(pos, kvs, part, after, scale, (2,))

time: 167 us -> 167 us (level)
  the two profiles are of different devices: /device:TPU:0 before, /device:TPU:32 now
where the time goes in v3:
time: 167 us
  waiting for transfers between devices  85 us (51%)
  starting transfers between devices  51.7 us (31%)
  Pallas kernels  28.9 us (17%)
    ppermute x12, waiting for transfers between devices, send_z(): return lax.ppermute(part, 'grp', grp_pairs(0, r))  60.8 us
    pallas_call x28, Pallas kernels, call(): pl.pallas_call(body, out_shape=out_shape, in_specs=in_specs, out_specs=ou...  28.9 us
    ppermute x15, starting transfers between devices, send_x(): return lax.ppermute(part, 'grp', grp_pairs(r, 0))  24 us
    ppermute x12, starting transfers between devices, send_z(): return lax.ppermute(part, 'grp', grp_pairs(0, r))  18.9 us
    ppermute x15, waiting for transfers between devices, send_x(): return lax.ppermute(part, 'grp', grp_pairs(r, 0))  15.2 us
    ppermute x2, starting transfers between devices, scan_states(): far = lax.ppermute(half, 'ctx', y_pairs(2))  6.17 us
    ppermute x2, waiting for transfers between devices, scan_states(): far = lax.ppermute(half, 'ctx', y_pairs(2))  5.37 us
  transfers between devices with their start and end apart: 35, of which 18 were waited for; matrix products, arithmetic and copies ran while one was open for 0% of the time, Pallas kernels for 13%

profile of v3, /device:TPU:32, one launch (start us, length us, event | category | flops | bytes accessed | tf_op | source)
XLA Modules:
  0.0 166.6 jit_solution(10647441618337316638)
XLA Ops:
  0.6 1.3 shard_map.63
  1.9 3.1 %collective-permute-start.4 = (bf16[4,256,384]{2,1,0:T(8,128)(2,1)S(1)}, bf16[4,256,384]{2,1,0:T(8,128)(2,1)S(1)}, u32[]{:S(2)}, u32[]{:S(2)}) collective-permute-start(bf16[4,256,384]{2,1,0:T(8,128)(2,1)S(1)} %shard_map.63), channel_id=1, source_target_pairs={{0,2},{1,3},{2,0},{3,1},{4,6},{5,7},{6,4},{7,5},{8,10},{9,11},{10,... | collective-permute-start | bytes 2359304 | tf_op jit(solution)/shard_map/ppermute | solution.py:432
  5.0 1.6 shard_map.62
  6.7 2.0 %collective-permute-start.5 = (bf16[4,256,384]{2,1,0:T(8,128)(2,1)S(1)}, bf16[4,256,384]{2,1,0:T(8,128)(2,1)S(1)}, u32[]{:S(2)}, u32[]{:S(2)}) collective-permute-start(bf16[4,256,384]{2,1,0:T(8,128)(2,1)S(1)} %get-tuple-element.47), channel_id=1, source_target_pairs={{0,3},{1,0},{2,1},{3,2},{4,7},{5,4},{6,5},{7,6},{8,11},{9,8},{10,9... | collective-permute-start | bytes 2359304 | tf_op jit(solution)/shard_map/ppermute | solution.py:432
  8.7 1.3 shard_map.59.refs_0_
  9.9 14.0 %collective-permute-done.4.refs_2_.refs_1_.refs_0_ = bf16[4,256,384]{2,1,0:T(8,128)(2,1)S(1)} collective-permute-done((bf16[4,256,384]{2,1,0:T(8,128)(2,1)S(1)}, bf16[4,256,384]{2,1,0:T(8,128)(2,1)S(1)}, u32[]{:S(2)}, u32[]{:S(2)}) %collective-permute-start.4) | collective-permute-done | bytes 786464 | tf_op jit(solution)/shard_map/ppermute | solution.py:432
  24.4 15.7 %collective-permute-done.3.refs_1_.refs_0_ = bf16[4,256,384]{2,1,0:T(8,128)(2,1)S(1)} collective-permute-done((bf16[4,256,384]{2,1,0:T(8,128)(2,1)S(1)}, bf16[4,256,384]{2,1,0:T(8,128)(2,1)S(1)}, u32[]{:S(2)}, u32[]{:S(2)}) %collective-permute-start.3) | collective-permute-done | bytes 786464 | tf_op jit(solution)/shard_map/ppermute | solution.py:432
  40.1 0.4 shard_map.68
  40.6 1.6 collective-permute-start.9
  42.1 2.7 %collective-permute-start.10 = (f32[136,256]{1,0:T(8,128)S(1)}, f32[136,256]{1,0:T(8,128)S(1)}, u32[]{:S(2)}, u32[]{:S(2)}) collective-permute-start(f32[136,256]{1,0:T(8,128)S(1)} %get-tuple-element.54), channel_id=1, source_target_pairs={{0,8},{1,9},{2,10},{3,11},{4,12},{5,13},{6,14},{7,15},{8,0},{9,1},... | collective-permute-start | bytes 417800 | tf_op jit(solution)/shard_map/ppermute | solution.py:436
  44.9 1.4 collective-permute-start.11
  46.3 1.1 collective-permute-done.9.m1.refs_4_
  47.4 3.5 %collective-permute-done.10.m2.refs_5_ = f32[136,256]{1,0:T(8,128)S(1)} collective-permute-done((f32[136,256]{1,0:T(8,128)S(1)}, f32[136,256]{1,0:T(8,128)S(1)}, u32[]{:S(2)}, u32[]{:S(2)}) %collective-permute-start.10) | collective-permute-done | bytes 139296 | tf_op jit(solution)/shard_map/ppermute | solution.py:436
  51.1 1.6 shard_map.61
  52.7 2.0 %collective-permute-start = (bf16[4,256,256]{2,1,0:T(8,128)(2,1)S(1)}, bf16[4,256,256]{2,1,0:T(8,128)(2,1)S(1)}, u32[]{:S(2)}, u32[]{:S(2)}) collective-permute-start(bf16[4,256,256]{2,1,0:T(8,128)(2,1)S(1)} %get-tuple-element.43), channel_id=1, source_target_pairs={{0,1},{1,2},{2,3},{3,0},{4,5},{5,6},{6,7},{7,4},{8,9},{9,10},{10,1... | collective-permute-start | bytes 1572872 | tf_op jit(solution)/shard_map/ppermute | solution.py:432
  54.6 1.1 collective-permute-start.1
  55.8 2.5 %collective-permute-start.2 = (bf16[4,256,256]{2,1,0:T(8,128)(2,1)S(1)}, bf16[4,256,256]{2,1,0:T(8,128)(2,1)S(1)}, u32[]{:S(2)}, u32[]{:S(2)}) collective-permute-start(bf16[4,256,256]{2,1,0:T(8,128)(2,1)S(1)} %get-tuple-element.45), channel_id=1, source_target_pairs={{0,3},{1,0},{2,1},{3,2},{4,7},{5,4},{6,5},{7,6},{8,11},{9,8},{10,9... | collective-permute-start | bytes 1572872 | tf_op jit(solution)/shard_map/ppermute | solution.py:432
  58.4 3.3 %collective-permute-start.14 = (f32[72,256]{1,0:T(8,128)S(1)}, f32[72,256]{1,0:T(8,128)S(1)}, u32[]{:S(2)}, u32[]{:S(2)}) collective-permute-start(f32[72,256]{1,0:T(8,128)S(1)} %get-tuple-element.57), channel_id=1, source_target_pairs={{0,64},{16,80},{32,96},{48,112},{64,0},{80,16},{96,32},{112,48},{1... | collective-permute-start | bytes 221192 | tf_op jit(solution)/shard_map/ppermute | solution.py:492
  61.6 0.7 collective-permute-start.13
  62.3 1.2 shard_map.66
  63.5 0.8 collective-permute-done.14.refs_1_
  64.3 1.3 collective-permute-start.6
  65.6 2.3 %collective-permute-done.13.refs_0_ = f32[136,256]{1,0:T(8,128)S(1)} collective-permute-done((f32[136,256]{1,0:T(8,128)S(1)}, f32[136,256]{1,0:T(8,128)S(1)}, u32[]{:S(2)}, u32[]{:S(2)}) %collective-permute-start.13) | collective-permute-done | bytes 139296 | tf_op jit(solution)/shard_map/ppermute | solution.py:493
  68.0 4.5 %collective-permute-done.6.refs_6_ = bf16[1024,128]{1,0:T(8,128)(2,1)S(1)} collective-permute-done((bf16[1024,128]{1,0:T(8,128)(2,1)S(1)}, bf16[1024,128]{1,0:T(8,128)(2,1)S(1)}, u32[]{:S(2)}, u32[]{:S(2)}) %collective-permute-start.6) | collective-permute-done | bytes 262176 | tf_op jit(solution)/shard_map/ppermute | solution.py:436
  72.5 1.4 collective-permute-start.7
  74.0 1.4 collective-permute-start.8
  75.5 2.2 %collective-permute-done.refs_5_.refs_1_ = bf16[4,256,256]{2,1,0:T(8,128)(2,1)S(1)} collective-permute-done((bf16[4,256,256]{2,1,0:T(8,128)(2,1)S(1)}, bf16[4,256,256]{2,1,0:T(8,128)(2,1)S(1)}, u32[]{:S(2)}, u32[]{:S(2)}) %collective-permute-start) | collective-permute-done | bytes 524320 | tf_op jit(solution)/shard_map/ppermute | solution.py:432
  77.7 1.3 collective-permute-start.16
  79.1 1.3 collective-permute-start.17
  80.4 0.6 collective-permute-done.2.refs_7_.refs_3_
  81.1 2.3 %collective-permute-start.18 = (f32[136,256]{1,0:T(8,128)S(1)}, f32[136,256]{1,0:T(8,128)S(1)}, u32[]{:S(2)}, u32[]{:S(2)}) collective-permute-start(f32[136,256]{1,0:T(8,128)S(1)} %get-tuple-element.61), channel_id=1, source_target_pairs={{0,12},{1,13},{2,14},{3,15},{4,0},{5,1},{6,2},{7,3},{8,4},{9,5},{1... | collective-permute-start | bytes 417800 | tf_op jit(solution)/shard_map/ppermute | solution.py:436
  83.3 1.1 shard_map.60.refs_4_.refs_0_
  84.5 0.8 shard_map.64.refs_8_.refs_3_.refs_4_
  85.2 3.5 %shard_map.65.refs_4_ = f32[4,4,256,256]{3,2,1,0:T(8,128)S(1)} custom-call(bf16[4,256,384]{2,1,0:T(8,128)(2,1)S(1)} %shard_map.59.refs_0_, bf16[4,256,384]{2,1,0:T(8,128)(2,1)S(1)} %collective-permute-done.3.refs_1_.refs_0_, bf16[4,256,384]{2,1,0:T(8,128)(2,1)S(1)} %collective-permute-done.4.refs_2_.refs_1_.refs_0_, ...), custom_call_target="tpu_custom_call" | custom-call | tf_op jit(solution)/shard_map/pallas_call | solution.py:90
  88.8 1.3 collective-permute-done.18.refs_12_.refs_7_.refs_8_
  90.2 3.6 %shard_map.73 = (bf16[4,4,256,256]{3,2,1,0:T(8,128)(2,1)S(1)}, bf16[4,4,256,256]{3,2,1,0:T(8,128)(2,1)S(1)}, f32[4,4,136,256]{3,2,1,0:T(8,128)S(1)}, f32[136,256...) custom-call(bf16[4,256,256]{2,1,0:T(8,128)(2,1)S(1)} %shard_map.60.refs_4_.refs_0_, ...), custom_call_target="tpu_custom_call" | custom-call | tf_op jit(solution)/shard_map/pallas_call | solution.py:90
  93.7 1.7 %collective-permute-start.22 = (f32[136,256]{1,0:T(8,128)S(1)}, f32[136,256]{1,0:T(8,128)S(1)}, u32[]{:S(2)}, u32[]{:S(2)}) collective-permute-start(f32[136,256]{1,0:T(8,128)S(1)} %get-tuple-element.73), channel_id=1, source_target_pairs={{0,4},{1,5},{2,6},{3,7},{4,8},{5,9},{6,10},{7,11},{8,12},{9,13},{1... | collective-permute-start | bytes 417800 | tf_op jit(solution)/shard_map/ppermute | solution.py:436
  95.4 2.4 %collective-permute-start.23 = (f32[136,256]{1,0:T(8,128)S(1)}, f32[136,256]{1,0:T(8,128)S(1)}, u32[]{:S(2)}, u32[]{:S(2)}) collective-permute-start(f32[136,256]{1,0:T(8,128)S(1)} %get-tuple-element.74), channel_id=1, source_target_pairs={{0,8},{1,9},{2,10},{3,11},{4,12},{5,13},{6,14},{7,15},{8,0},{9,1},... | collective-permute-start | bytes 417800 | tf_op jit(solution)/shard_map/ppermute | solution.py:436
  97.8 0.9 collective-permute-start.24
  98.8 2.6 %collective-permute-done.22.m1.refs_4_ = f32[136,256]{1,0:T(8,128)S(1)} collective-permute-done((f32[136,256]{1,0:T(8,128)S(1)}, f32[136,256]{1,0:T(8,128)S(1)}, u32[]{:S(2)}, u32[]{:S(2)}) %collective-permute-start.22) | collective-permute-done | bytes 139296 | tf_op jit(solution)/shard_map/ppermute | solution.py:436
  101.3 2.2 %collective-permute-done.23.m2.refs_5_ = f32[136,256]{1,0:T(8,128)S(1)} collective-permute-done((f32[136,256]{1,0:T(8,128)S(1)}, f32[136,256]{1,0:T(8,128)S(1)}, u32[]{:S(2)}, u32[]{:S(2)}) %collective-permute-start.23) | collective-permute-done | bytes 139296 | tf_op jit(solution)/shard_map/ppermute | solution.py:436
  103.6 1.2 shard_map.76
  104.9 1.0 collective-permute-start.20
  105.9 1.5 collective-permute-start.26
  107.4 2.9 %collective-permute-start.27 = (f32[72,256]{1,0:T(8,128)S(1)}, f32[72,256]{1,0:T(8,128)S(1)}, u32[]{:S(2)}, u32[]{:S(2)}) collective-permute-start(f32[72,256]{1,0:T(8,128)S(1)} %get-tuple-element.77), channel_id=1, source_target_pairs={{0,64},{16,80},{32,96},{48,112},{64,0},{80,16},{96,32},{112,48},{1... | collective-permute-start | bytes 221192 | tf_op jit(solution)/shard_map/ppermute | solution.py:492
  110.3 4.6 %collective-permute-done.27.refs_1_ = f32[72,256]{1,0:T(8,128)S(1)} collective-permute-done((f32[72,256]{1,0:T(8,128)S(1)}, f32[72,256]{1,0:T(8,128)S(1)}, u32[]{:S(2)}, u32[]{:S(2)}) %collective-permute-start.27) | collective-permute-done | bytes 73760 | tf_op jit(solution)/shard_map/ppermute | solution.py:492
  115.1 1.3 collective-permute-done.28.refs_1_
  116.6 0.9 collective-permute-start.29
  117.5 3.3 %collective-permute-start.30 = (f32[136,256]{1,0:T(8,128)S(1)}, f32[136,256]{1,0:T(8,128)S(1)}, u32[]{:S(2)}, u32[]{:S(2)}) collective-permute-start(f32[136,256]{1,0:T(8,128)S(1)} %get-tuple-element.80), channel_id=1, source_target_pairs={{0,8},{1,9},{2,10},{3,11},{4,12},{5,13},{6,14},{7,15},{8,0},{9,1},... | collective-permute-start | bytes 417800 | tf_op jit(solution)/shard_map/ppermute | solution.py:436
  120.8 2.2 %shard_map.75 = (bf16[4,256,256]{2,1,0:T(8,128)(2,1)S(1)}, bf16[4,256,256]{2,1,0:T(8,128)(2,1)S(1)}, bf16[4,2,512,256]{3,2,1,0:T(8,128)(2,1)S(1)}) custom-call(bf16[4,256,384]{2,1,0:T(8,128)(2,1)S(1)} %collective-permute-done.3.refs_1_.refs_0_, bf16[4,256,384]{2,1,0:T(8,128)(2,1)S(1)} %collective-permute-done.5.refs_3_.refs_1_, ...), custom_call_target="tpu_custom_call" | custom-call | tf_op jit(solution)/shard_map/pallas_call | solution.py:90
  123.0 3.0 %collective-permute-start.19 = (bf16[4,256,256]{2,1,0:T(8,128)(2,1)S(1)}, bf16[4,256,256]{2,1,0:T(8,128)(2,1)S(1)}, u32[]{:S(2)}, u32[]{:S(2)}) collective-permute-start(bf16[4,256,256]{2,1,0:T(8,128)(2,1)S(1)} %get-tuple-element.65), channel_id=1, source_target_pairs={{0,1},{1,2},{2,3},{3,0},{4,5},{5,6},{6,7},{7,4},{8,9},{9,10},{10,1... | collective-permute-start | bytes 1572872 | tf_op jit(solution)/shard_map/ppermute | solution.py:432
  126.0 1.2 shard_map.74
  127.2 2.4 %shard_map.78.refs_1_.refs_2_ = f32[4,4,256,256]{3,2,1,0:T(8,128)S(1)} custom-call(bf16[4,256,384]{2,1,0:T(8,128)(2,1)S(1)} %shard_map.59.refs_0_, bf16[4,256,384]{2,1,0:T(8,128)(2,1)S(1)} %collective-permute-done.3.refs_1_.refs_0_, bf16[4,256,384]{2,1,0:T(8,128)(2,1)S(1)} %collective-permute-done.4.refs_2_.refs_1_.refs_0_, ...), custom_call_target="tpu_custom_call" | custom-call | tf_op jit(solution)/shard_map/pallas_call | solution.py:90
  129.7 0.7 shard_map.84
  130.5 2.1 %collective-permute-start.32 = (bf16[4,256,256]{2,1,0:T(8,128)(2,1)S(1)}, bf16[4,256,256]{2,1,0:T(8,128)(2,1)S(1)}, u32[]{:S(2)}, u32[]{:S(2)}) collective-permute-start(bf16[4,256,256]{2,1,0:T(8,128)(2,1)S(1)} %get-tuple-element.82), channel_id=1, source_target_pairs={{0,1},{1,2},{2,3},{3,0},{4,5},{5,6},{6,7},{7,4},{8,9},{9,10},{10,1... | collective-permute-start | bytes 1572872 | tf_op jit(solution)/shard_map/ppermute | solution.py:432
  132.6 0.4 shard_map.85
  133.0 1.9 %collective-permute-start.33 = (bf16[4,256,256]{2,1,0:T(8,128)(2,1)S(1)}, bf16[4,256,256]{2,1,0:T(8,128)(2,1)S(1)}, u32[]{:S(2)}, u32[]{:S(2)}) collective-permute-start(bf16[4,256,256]{2,1,0:T(8,128)(2,1)S(1)} %shard_map.85), channel_id=1, source_target_pairs={{0,2},{1,3},{2,0},{3,1},{4,6},{5,7},{6,4},{7,5},{8,10},{9,11},{10,... | collective-permute-start | bytes 1572872 | tf_op jit(solution)/shard_map/ppermute | solution.py:432
  135.0 3.3 %collective-permute-done.19.refs_1_ = bf16[4,256,256]{2,1,0:T(8,128)(2,1)S(1)} collective-permute-done((bf16[4,256,256]{2,1,0:T(8,128)(2,1)S(1)}, bf16[4,256,256]{2,1,0:T(8,128)(2,1)S(1)}, u32[]{:S(2)}, u32[]{:S(2)}) %collective-permute-start.19) | collective-permute-done | bytes 524320 | tf_op jit(solution)/shard_map/ppermute | solution.py:432
  138.3 6.2 %collective-permute-done.21.refs_3_ = bf16[4,256,256]{2,1,0:T(8,128)(2,1)S(1)} collective-permute-done((bf16[4,256,256]{2,1,0:T(8,128)(2,1)S(1)}, bf16[4,256,256]{2,1,0:T(8,128)(2,1)S(1)}, u32[]{:S(2)}, u32[]{:S(2)}) %collective-permute-start.21) | collective-permute-done | bytes 524320 | tf_op jit(solution)/shard_map/ppermute | solution.py:432
  144.5 1.4 shard_map.77
  145.9 0.5 shard_map.83.refs_0_
  146.4 12.7 %collective-permute-done.32.refs_1_ = bf16[4,256,256]{2,1,0:T(8,128)(2,1)S(1)} collective-permute-done((bf16[4,256,256]{2,1,0:T(8,128)(2,1)S(1)}, bf16[4,256,256]{2,1,0:T(8,128)(2,1)S(1)}, u32[]{:S(2)}, u32[]{:S(2)}) %collective-permute-start.32) | collective-permute-done | bytes 524320 | tf_op jit(solution)/shard_map/ppermute | solution.py:432
  159.1 5.9 %collective-permute-done.34.refs_3_ = bf16[4,256,256]{2,1,0:T(8,128)(2,1)S(1)} collective-permute-done((bf16[4,256,256]{2,1,0:T(8,128)(2,1)S(1)}, bf16[4,256,256]{2,1,0:T(8,128)(2,1)S(1)}, u32[]{:S(2)}, u32[]{:S(2)}) %collective-permute-start.34) | collective-permute-done | bytes 524320 | tf_op jit(solution)/shard_map/ppermute | solution.py:432
  165.0 1.4 shard_map.86
  (34 shorter events, 1.6 us)
Async XLA Ops:
  1.9 22.0 %collective-permute-start.4 = (bf16[4,256,384]{2,1,0:T(8,128)(2,1)S(1)}, bf16[4,256,384]{2,1,0:T(8,128)(2,1)S(1)}, u32[]{:S(2)}, u32[]{:S(2)}) collective-permute-start(bf16[4,256,384]{2,1,0:T(8,128)(2,1)S(1)} %shard_map.63), channel_id=1, source_target_pairs={{0,2},{1,3},{2,0},{3,1},{4,6},{5,7},{6,4},{7,5},{8,10},{9,11},{10,... | collective-permute-start | bytes 2359304 | tf_op jit(solution)/shard_map/ppermute | solution.py:432
  6.6 33.6 %collective-permute-start.3 = (bf16[4,256,384]{2,1,0:T(8,128)(2,1)S(1)}, bf16[4,256,384]{2,1,0:T(8,128)(2,1)S(1)}, u32[]{:S(2)}, u32[]{:S(2)}) collective-permute-start(bf16[4,256,384]{2,1,0:T(8,128)(2,1)S(1)} %get-tuple-element.46), channel_id=1, source_target_pairs={{0,1},{1,2},{2,3},{3,0},{4,5},{5,6},{6,7},{7,4},{8,9},{9,10},{10,1... | collective-permute-start | bytes 2359304 | tf_op jit(solution)/shard_map/ppermute | solution.py:432
  6.7 33.5 %collective-permute-start.5 = (bf16[4,256,384]{2,1,0:T(8,128)(2,1)S(1)}, bf16[4,256,384]{2,1,0:T(8,128)(2,1)S(1)}, u32[]{:S(2)}, u32[]{:S(2)}) collective-permute-start(bf16[4,256,384]{2,1,0:T(8,128)(2,1)S(1)} %get-tuple-element.47), channel_id=1, source_target_pairs={{0,3},{1,0},{2,1},{3,2},{4,7},{5,4},{6,5},{7,6},{8,11},{9,8},{10,9... | collective-permute-start | bytes 2359304 | tf_op jit(solution)/shard_map/ppermute | solution.py:432
  40.6 6.8 %collective-permute-start.9 = (f32[136,256]{1,0:T(8,128)S(1)}, f32[136,256]{1,0:T(8,128)S(1)}, u32[]{:S(2)}, u32[]{:S(2)}) collective-permute-start(f32[136,256]{1,0:T(8,128)S(1)} %get-tuple-element.53), channel_id=1, source_target_pairs={{0,4},{1,5},{2,6},{3,7},{4,8},{5,9},{6,10},{7,11},{8,12},{9,13},{1... | collective-permute-start | bytes 417800 | tf_op jit(solution)/shard_map/ppermute | solution.py:436
  42.1 8.8 %collective-permute-start.10 = (f32[136,256]{1,0:T(8,128)S(1)}, f32[136,256]{1,0:T(8,128)S(1)}, u32[]{:S(2)}, u32[]{:S(2)}) collective-permute-start(f32[136,256]{1,0:T(8,128)S(1)} %get-tuple-element.54), channel_id=1, source_target_pairs={{0,8},{1,9},{2,10},{3,11},{4,12},{5,13},{6,14},{7,15},{8,0},{9,1},... | collective-permute-start | bytes 417800 | tf_op jit(solution)/shard_map/ppermute | solution.py:436
  44.9 6.1 %collective-permute-start.11 = (f32[136,256]{1,0:T(8,128)S(1)}, f32[136,256]{1,0:T(8,128)S(1)}, u32[]{:S(2)}, u32[]{:S(2)}) collective-permute-start(f32[136,256]{1,0:T(8,128)S(1)} %get-tuple-element.55), channel_id=1, source_target_pairs={{0,12},{1,13},{2,14},{3,15},{4,0},{5,1},{6,2},{7,3},{8,4},{9,5},{1... | collective-permute-start | bytes 417800 | tf_op jit(solution)/shard_map/ppermute | solution.py:436
  51.0 7.4 %collective-permute-start.12 = (f32[136,256]{1,0:T(8,128)S(1)}, f32[136,256]{1,0:T(8,128)S(1)}, u32[]{:S(2)}, u32[]{:S(2)}) collective-permute-start(f32[136,256]{1,0:T(8,128)S(1)} %shard_map.69.refs_0_), channel_id=1, source_target_pairs={{0,16},{16,0},{32,48},{48,32},{64,80},{80,64},{96,112},{112,96},{1... | collective-permute-start | bytes 417800 | tf_op jit(solution)/shard_map/ppermute | solution.py:490
  52.7 25.1 %collective-permute-start = (bf16[4,256,256]{2,1,0:T(8,128)(2,1)S(1)}, bf16[4,256,256]{2,1,0:T(8,128)(2,1)S(1)}, u32[]{:S(2)}, u32[]{:S(2)}) collective-permute-start(bf16[4,256,256]{2,1,0:T(8,128)(2,1)S(1)} %get-tuple-element.43), channel_id=1, source_target_pairs={{0,1},{1,2},{2,3},{3,0},{4,5},{5,6},{6,7},{7,4},{8,9},{9,10},{10,1... | collective-permute-start | bytes 1572872 | tf_op jit(solution)/shard_map/ppermute | solution.py:432
  54.6 24.4 %collective-permute-start.1 = (bf16[4,256,256]{2,1,0:T(8,128)(2,1)S(1)}, bf16[4,256,256]{2,1,0:T(8,128)(2,1)S(1)}, u32[]{:S(2)}, u32[]{:S(2)}) collective-permute-start(bf16[4,256,256]{2,1,0:T(8,128)(2,1)S(1)} %get-tuple-element.44), channel_id=1, source_target_pairs={{0,2},{1,3},{2,0},{3,1},{4,6},{5,7},{6,4},{7,5},{8,10},{9,11},{10,... | collective-permute-start | bytes 1572872 | tf_op jit(solution)/shard_map/ppermute | solution.py:432
  55.8 25.3 %collective-permute-start.2 = (bf16[4,256,256]{2,1,0:T(8,128)(2,1)S(1)}, bf16[4,256,256]{2,1,0:T(8,128)(2,1)S(1)}, u32[]{:S(2)}, u32[]{:S(2)}) collective-permute-start(bf16[4,256,256]{2,1,0:T(8,128)(2,1)S(1)} %get-tuple-element.45), channel_id=1, source_target_pairs={{0,3},{1,0},{2,1},{3,2},{4,7},{5,4},{6,5},{7,6},{8,11},{9,8},{10,9... | collective-permute-start | bytes 1572872 | tf_op jit(solution)/shard_map/ppermute | solution.py:432
  58.4 5.9 %collective-permute-start.14 = (f32[72,256]{1,0:T(8,128)S(1)}, f32[72,256]{1,0:T(8,128)S(1)}, u32[]{:S(2)}, u32[]{:S(2)}) collective-permute-start(f32[72,256]{1,0:T(8,128)S(1)} %get-tuple-element.57), channel_id=1, source_target_pairs={{0,64},{16,80},{32,96},{48,112},{64,0},{80,16},{96,32},{112,48},{1... | collective-permute-start | bytes 221192 | tf_op jit(solution)/shard_map/ppermute | solution.py:492
  61.6 6.3 %collective-permute-start.13 = (f32[136,256]{1,0:T(8,128)S(1)}, f32[136,256]{1,0:T(8,128)S(1)}, u32[]{:S(2)}, u32[]{:S(2)}) collective-permute-start(f32[136,256]{1,0:T(8,128)S(1)} %get-tuple-element.56), channel_id=1, source_target_pairs={{0,32},{16,112},{32,64},{48,16},{64,96},{80,48},{96,0},{112,80},{1... | collective-permute-start | bytes 417800 | tf_op jit(solution)/shard_map/ppermute | solution.py:493
  64.3 8.2 %collective-permute-start.6 = (bf16[1024,128]{1,0:T(8,128)(2,1)S(1)}, bf16[1024,128]{1,0:T(8,128)(2,1)S(1)}, u32[]{:S(2)}, u32[]{:S(2)}) collective-permute-start(bf16[1024,128]{1,0:T(8,128)(2,1)S(1)} %get-tuple-element.49), channel_id=1, source_target_pairs={{0,4},{1,5},{2,6},{3,7},{4,8},{5,9},{6,10},{7,11},{8,12},{9,13},{1... | collective-permute-start | bytes 786440 | tf_op jit(solution)/shard_map/ppermute | solution.py:436
  67.9 6.0 %collective-permute-start.15 = (f32[136,256]{1,0:T(8,128)S(1)}, f32[136,256]{1,0:T(8,128)S(1)}, u32[]{:S(2)}, u32[]{:S(2)}) collective-permute-start(f32[136,256]{1,0:T(8,128)S(1)} %shard_map.71.refs_0_), channel_id=1, source_target_pairs={{0,16},{16,0},{32,48},{48,32},{64,80},{80,64},{96,112},{112,96},{1... | collective-permute-start | bytes 417800 | tf_op jit(solution)/shard_map/ppermute | solution.py:495
  72.5 16.3 %collective-permute-start.7 = (bf16[1024,128]{1,0:T(8,128)(2,1)S(1)}, bf16[1024,128]{1,0:T(8,128)(2,1)S(1)}, u32[]{:S(2)}, u32[]{:S(2)}) collective-permute-start(bf16[1024,128]{1,0:T(8,128)(2,1)S(1)} %get-tuple-element.50), channel_id=1, source_target_pairs={{0,8},{1,9},{2,10},{3,11},{4,12},{5,13},{6,14},{7,15},{8,0},{9,1},... | collective-permute-start | bytes 786440 | tf_op jit(solution)/shard_map/ppermute | solution.py:436
  74.0 14.8 %collective-permute-start.8 = (bf16[1024,128]{1,0:T(8,128)(2,1)S(1)}, bf16[1024,128]{1,0:T(8,128)(2,1)S(1)}, u32[]{:S(2)}, u32[]{:S(2)}) collective-permute-start(bf16[1024,128]{1,0:T(8,128)(2,1)S(1)} %get-tuple-element.51), channel_id=1, source_target_pairs={{0,12},{1,13},{2,14},{3,15},{4,0},{5,1},{6,2},{7,3},{8,4},{9,5},{1... | collective-permute-start | bytes 786440 | tf_op jit(solution)/shard_map/ppermute | solution.py:436
  77.7 11.1 %collective-permute-start.16 = (f32[136,256]{1,0:T(8,128)S(1)}, f32[136,256]{1,0:T(8,128)S(1)}, u32[]{:S(2)}, u32[]{:S(2)}) collective-permute-start(f32[136,256]{1,0:T(8,128)S(1)} %get-tuple-element.59), channel_id=1, source_target_pairs={{0,4},{1,5},{2,6},{3,7},{4,8},{5,9},{6,10},{7,11},{8,12},{9,13},{1... | collective-permute-start | bytes 417800 | tf_op jit(solution)/shard_map/ppermute | solution.py:436
  79.1 9.7 %collective-permute-start.17 = (f32[136,256]{1,0:T(8,128)S(1)}, f32[136,256]{1,0:T(8,128)S(1)}, u32[]{:S(2)}, u32[]{:S(2)}) collective-permute-start(f32[136,256]{1,0:T(8,128)S(1)} %get-tuple-element.60), channel_id=1, source_target_pairs={{0,8},{1,9},{2,10},{3,11},{4,12},{5,13},{6,14},{7,15},{8,0},{9,1},... | collective-permute-start | bytes 417800 | tf_op jit(solution)/shard_map/ppermute | solution.py:436
  81.1 9.1 %collective-permute-start.18 = (f32[136,256]{1,0:T(8,128)S(1)}, f32[136,256]{1,0:T(8,128)S(1)}, u32[]{:S(2)}, u32[]{:S(2)}) collective-permute-start(f32[136,256]{1,0:T(8,128)S(1)} %get-tuple-element.61), channel_id=1, source_target_pairs={{0,12},{1,13},{2,14},{3,15},{4,0},{5,1},{6,2},{7,3},{8,4},{9,5},{1... | collective-permute-start | bytes 417800 | tf_op jit(solution)/shard_map/ppermute | solution.py:436
  93.7 7.6 %collective-permute-start.22 = (f32[136,256]{1,0:T(8,128)S(1)}, f32[136,256]{1,0:T(8,128)S(1)}, u32[]{:S(2)}, u32[]{:S(2)}) collective-permute-start(f32[136,256]{1,0:T(8,128)S(1)} %get-tuple-element.73), channel_id=1, source_target_pairs={{0,4},{1,5},{2,6},{3,7},{4,8},{5,9},{6,10},{7,11},{8,12},{9,13},{1... | collective-permute-start | bytes 417800 | tf_op jit(solution)/shard_map/ppermute | solution.py:436
  95.4 8.1 %collective-permute-start.23 = (f32[136,256]{1,0:T(8,128)S(1)}, f32[136,256]{1,0:T(8,128)S(1)}, u32[]{:S(2)}, u32[]{:S(2)}) collective-permute-start(f32[136,256]{1,0:T(8,128)S(1)} %get-tuple-element.74), channel_id=1, source_target_pairs={{0,8},{1,9},{2,10},{3,11},{4,12},{5,13},{6,14},{7,15},{8,0},{9,1},... | collective-permute-start | bytes 417800 | tf_op jit(solution)/shard_map/ppermute | solution.py:436
  97.8 5.7 %collective-permute-start.24 = (f32[136,256]{1,0:T(8,128)S(1)}, f32[136,256]{1,0:T(8,128)S(1)}, u32[]{:S(2)}, u32[]{:S(2)}) collective-permute-start(f32[136,256]{1,0:T(8,128)S(1)} %get-tuple-element.75), channel_id=1, source_target_pairs={{0,12},{1,13},{2,14},{3,15},{4,0},{5,1},{6,2},{7,3},{8,4},{9,5},{1... | collective-permute-start | bytes 417800 | tf_op jit(solution)/shard_map/ppermute | solution.py:436
  103.5 2.3 %collective-permute-start.25 = (f32[136,256]{1,0:T(8,128)S(1)}, f32[136,256]{1,0:T(8,128)S(1)}, u32[]{:S(2)}, u32[]{:S(2)}) collective-permute-start(f32[136,256]{1,0:T(8,128)S(1)} %shard_map.79.refs_0_), channel_id=1, source_target_pairs={{0,16},{16,0},{32,48},{48,32},{64,80},{80,64},{96,112},{112,96},{1... | collective-permute-start | bytes 417800 | tf_op jit(solution)/shard_map/ppermute | solution.py:490
  104.9 28.2 %collective-permute-start.20 = (bf16[4,256,256]{2,1,0:T(8,128)(2,1)S(1)}, bf16[4,256,256]{2,1,0:T(8,128)(2,1)S(1)}, u32[]{:S(2)}, u32[]{:S(2)}) collective-permute-start(bf16[4,256,256]{2,1,0:T(8,128)(2,1)S(1)} %get-tuple-element.66), channel_id=1, source_target_pairs={{0,2},{1,3},{2,0},{3,1},{4,6},{5,7},{6,4},{7,5},{8,10},{9,11},{10,... | collective-permute-start | bytes 1572872 | tf_op jit(solution)/shard_map/ppermute | solution.py:432
  105.9 9.0 %collective-permute-start.26 = (f32[136,256]{1,0:T(8,128)S(1)}, f32[136,256]{1,0:T(8,128)S(1)}, u32[]{:S(2)}, u32[]{:S(2)}) collective-permute-start(f32[136,256]{1,0:T(8,128)S(1)} %get-tuple-element.76), channel_id=1, source_target_pairs={{0,32},{16,112},{32,64},{48,16},{64,96},{80,48},{96,0},{112,80},{1... | collective-permute-start | bytes 417800 | tf_op jit(solution)/shard_map/ppermute | solution.py:493
  107.4 7.5 %collective-permute-start.27 = (f32[72,256]{1,0:T(8,128)S(1)}, f32[72,256]{1,0:T(8,128)S(1)}, u32[]{:S(2)}, u32[]{:S(2)}) collective-permute-start(f32[72,256]{1,0:T(8,128)S(1)} %get-tuple-element.77), channel_id=1, source_target_pairs={{0,64},{16,80},{32,96},{48,112},{64,0},{80,16},{96,32},{112,48},{1... | collective-permute-start | bytes 221192 | tf_op jit(solution)/shard_map/ppermute | solution.py:492
  115.0 1.4 collective-permute-start.28
  116.6 13.0 %collective-permute-start.29 = (f32[136,256]{1,0:T(8,128)S(1)}, f32[136,256]{1,0:T(8,128)S(1)}, u32[]{:S(2)}, u32[]{:S(2)}) collective-permute-start(f32[136,256]{1,0:T(8,128)S(1)} %get-tuple-element.79), channel_id=1, source_target_pairs={{0,4},{1,5},{2,6},{3,7},{4,8},{5,9},{6,10},{7,11},{8,12},{9,13},{1... | collective-permute-start | bytes 417800 | tf_op jit(solution)/shard_map/ppermute | solution.py:436
  117.5 12.2 %collective-permute-start.30 = (f32[136,256]{1,0:T(8,128)S(1)}, f32[136,256]{1,0:T(8,128)S(1)}, u32[]{:S(2)}, u32[]{:S(2)}) collective-permute-start(f32[136,256]{1,0:T(8,128)S(1)} %get-tuple-element.80), channel_id=1, source_target_pairs={{0,8},{1,9},{2,10},{3,11},{4,12},{5,13},{6,14},{7,15},{8,0},{9,1},... | collective-permute-start | bytes 417800 | tf_op jit(solution)/shard_map/ppermute | solution.py:436
  120.8 8.9 %collective-permute-start.31 = (f32[136,256]{1,0:T(8,128)S(1)}, f32[136,256]{1,0:T(8,128)S(1)}, u32[]{:S(2)}, u32[]{:S(2)}) collective-permute-start(f32[136,256]{1,0:T(8,128)S(1)} %get-tuple-element.81), channel_id=1, source_target_pairs={{0,12},{1,13},{2,14},{3,15},{4,0},{5,1},{6,2},{7,3},{8,4},{9,5},{1... | collective-permute-start | bytes 417800 | tf_op jit(solution)/shard_map/ppermute | solution.py:436
  123.0 15.3 %collective-permute-start.19 = (bf16[4,256,256]{2,1,0:T(8,128)(2,1)S(1)}, bf16[4,256,256]{2,1,0:T(8,128)(2,1)S(1)}, u32[]{:S(2)}, u32[]{:S(2)}) collective-permute-start(bf16[4,256,256]{2,1,0:T(8,128)(2,1)S(1)} %get-tuple-element.65), channel_id=1, source_target_pairs={{0,1},{1,2},{2,3},{3,0},{4,5},{5,6},{6,7},{7,4},{8,9},{9,10},{10,1... | collective-permute-start | bytes 1572872 | tf_op jit(solution)/shard_map/ppermute | solution.py:432
  129.6 14.9 %collective-permute-start.21 = (bf16[4,256,256]{2,1,0:T(8,128)(2,1)S(1)}, bf16[4,256,256]{2,1,0:T(8,128)(2,1)S(1)}, u32[]{:S(2)}, u32[]{:S(2)}) collective-permute-start(bf16[4,256,256]{2,1,0:T(8,128)(2,1)S(1)} %get-tuple-element.67), channel_id=1, source_target_pairs={{0,3},{1,0},{2,1},{3,2},{4,7},{5,4},{6,5},{7,6},{8,11},{9,8},{10,9... | collective-permute-start | bytes 1572872 | tf_op jit(solution)/shard_map/ppermute | solution.py:432
  130.5 28.6 %collective-permute-start.32 = (bf16[4,256,256]{2,1,0:T(8,128)(2,1)S(1)}, bf16[4,256,256]{2,1,0:T(8,128)(2,1)S(1)}, u32[]{:S(2)}, u32[]{:S(2)}) collective-permute-start(bf16[4,256,256]{2,1,0:T(8,128)(2,1)S(1)} %get-tuple-element.82), channel_id=1, source_target_pairs={{0,1},{1,2},{2,3},{3,0},{4,5},{5,6},{6,7},{7,4},{8,9},{9,10},{10,1... | collective-permute-start | bytes 1572872 | tf_op jit(solution)/shard_map/ppermute | solution.py:432
  132.5 32.5 %collective-permute-start.34 = (bf16[4,256,256]{2,1,0:T(8,128)(2,1)S(1)}, bf16[4,256,256]{2,1,0:T(8,128)(2,1)S(1)}, u32[]{:S(2)}, u32[]{:S(2)}) collective-permute-start(bf16[4,256,256]{2,1,0:T(8,128)(2,1)S(1)} %get-tuple-element.83), channel_id=1, source_target_pairs={{0,3},{1,0},{2,1},{3,2},{4,7},{5,4},{6,5},{7,6},{8,11},{9,8},{10,9... | collective-permute-start | bytes 1572872 | tf_op jit(solution)/shard_map/ppermute | solution.py:432
  133.0 32.0 %collective-permute-start.33 = (bf16[4,256,256]{2,1,0:T(8,128)(2,1)S(1)}, bf16[4,256,256]{2,1,0:T(8,128)(2,1)S(1)}, u32[]{:S(2)}, u32[]{:S(2)}) collective-permute-start(bf16[4,256,256]{2,1,0:T(8,128)(2,1)S(1)} %shard_map.85), channel_id=1, source_target_pairs={{0,2},{1,3},{2,0},{3,1},{4,6},{5,7},{6,4},{7,5},{8,10},{9,11},{10,... | collective-permute-start | bytes 1572872 | tf_op jit(solution)/shard_map/ppermute | solution.py:432

commit v4 on v3

--- a/solution.py
+++ b/solution.py
@@ -16,7 +16,7 @@
 D = 128
 SR = D + 8
 BF, F32 = jnp.bfloat16, jnp.float32
-VMEM_LIMIT = 8 * 1024 * 1024
+VMEM_LIMIT = 12 * 1024 * 1024
 
 
 def grp_pairs(dx, dz):
@@ -48,7 +48,9 @@
 
 def split(x):
     hi = x.astype(BF)
-    return hi, (x - hi.astype(F32)).astype(BF)
+    rest = x - hi.astype(F32)
+    mid = rest.astype(BF)
+    return hi, mid, (rest - mid.astype(F32)).astype(BF)
 
 
 def mod4(a):
@@ -265,9 +267,9 @@
     return jnp.concatenate(split(x), axis=0)
 
 
-def halves(x):
-    n = x.shape[0] // 2
-    return x[:n] + x[n:]
+def thirds(x):
+    n = x.shape[0] // 3
+    return x[:n] + (x[n : 2 * n] + x[2 * n :])
 
 
 def lines_kernel(pos, *refs):
@@ -293,9 +295,9 @@
         for b in range(NZ):
             q, k = qs[b][hd], kvs[b][hd, :, 0:F]
             va = augmented(kvs[b][hd, :, F : F + D])
-            st_hi, st_lo = split(full_state(lines[r, b]))
+            st_hi, st_mid, st_lo = split(full_state(lines[r, b]))
             sc = rows_of(jnp.where(mask, nt(q, k), 0.0))
-            nd_out[r, b] = halves(nn(sc, va)) + nt(q, st_hi) + nt(q, st_lo)
+            nd_out[r, b] = thirds(nn(sc, va)) + (nt(q, st_hi) + (nt(q, st_mid) + nt(q, st_lo)))
 
 
 def pre(pos, kvs, qs, lines):
@@ -307,32 +309,31 @@
 
 def post_kernel(pos, *refs):
     qs, nd, teas, states = refs[0:4], refs[4], refs[5:9], refs[9:13]
-    dhi_out, dlo_out, adj_out, sums, both_s = refs[13], refs[14], refs[15], refs[16:20], refs[20]
+    d_out, adj_out, sums, both_s = refs[13], refs[14], refs[15:19], refs[19]
     x, z = pos[0], pos[1]
     for r in range(HL):
         hd = mod4(x - r)
-        e_hi, e_lo = split(full_state(states[r]))
+        e_hi, e_mid, e_lo = split(full_state(states[r]))
         total = jnp.zeros((SR, F), F32)
         for b in range(NZ):
             q = qs[b][hd]
             held = both_s.at[b % 2]
-            held[...] = nd[r, b] + nt(q, e_hi) + nt(q, e_lo)
+            held[...] = nd[r, b] + (nt(q, e_hi) + (nt(q, e_mid) + nt(q, e_lo)))
             for i in range(TB // PR):
                 rows = slice(i * PR, (i + 1) * PR)
                 inverse = 1.0 / held[rows, D:]
                 student = held[rows, 0:D] * inverse
                 there = pl.ds(pl.multiple_of(mod4(z - b) * TB + i * PR, PR), PR)
                 resid = student - teas[r][there, :].astype(F32)
-                n_hi, n_lo = split(resid * inverse)
                 dd = -jnp.sum(resid * student, axis=1, keepdims=True) * inverse
-                c_hi, c_lo = split(dd * (1.0 / D))
-                dhi_out[r, b, rows, 0:D] = n_hi
-                dhi_out[r, b, rows, D:] = c_hi
-                dlo_out[r, b, rows, 0:D] = n_lo
-                dlo_out[r, b, rows, D:] = c_lo
-            sides = tn(jnp.concatenate([dhi_out[r, b, :, 0:D], dlo_out[r, b, :, 0:D]], axis=1), q)
-            ends = tn(dhi_out[r, b, :, D : D + 8], q) + tn(dlo_out[r, b, :, D : D + 8], q)
-            adj = jnp.concatenate([sides[0:D] + sides[D:], ends], axis=0)
+                for t, (n, c) in enumerate(zip(split(resid * inverse), split(dd * (1.0 / D)))):
+                    out_rows = slice(t * TB + i * PR, t * TB + (i + 1) * PR)
+                    d_out[r, b, out_rows, 0:D] = n
+                    d_out[r, b, out_rows, D:] = c
+            terms = [d_out[r, b, t * TB : (t + 1) * TB, :] for t in range(3)]
+            sides = thirds(tn(jnp.concatenate([d[:, 0:D] for d in terms], axis=1), q))
+            ends = [tn(d[:, D : D + 8], q) for d in terms]
+            adj = jnp.concatenate([sides, ends[0] + (ends[1] + ends[2])], axis=0)
             adj_out[r, b] = adj
             total = total + adj
         sums[(-r) % NX][...] = total
@@ -341,19 +342,19 @@
 def post(pos, qs, nd, teas, states):
     out = call(
         post_kernel,
-        [shape(HL, NZ, TB, 2 * D, kind=BF)] * 2 + [shape(HL, NZ, SR, F)] + [shape(SR, F)] * NX,
+        [shape(HL, NZ, 3 * TB, 2 * D, kind=BF), shape(HL, NZ, SR, F)] + [shape(SR, F)] * NX,
         vmem(13),
-        vmem(3 + NX),
+        vmem(2 + NX),
         (pos, *qs, nd, *teas, *states),
         [pltpu.VMEM((2, TB, 2 * D), F32)],
     )
-    return out[0], out[1], out[2], out[3:7]
+    return out[0], out[1], out[2:6]
 
 
 def qgrad_kernel(scale, blocks, pos, *refs):
     n = len(blocks)
-    kvs, dhi, dlo, lines, states = refs[0:n], refs[n], refs[n + 1], refs[n + 2], refs[n + 3 : n + 7]
-    outs, mixed_out = refs[n + 7 : 2 * n + 7], refs[2 * n + 7]
+    kvs, d, lines, states = refs[0:n], refs[n], refs[n + 1], refs[n + 2 : n + 6]
+    outs, mixed_out = refs[n + 6 : 2 * n + 6], refs[2 * n + 6]
     x = pos[0]
     mask = causal_mask()
     for r in range(HL):
@@ -361,23 +362,24 @@
         for i, b in enumerate(blocks):
             k = kvs[i][hd, :, 0:F]
             va = augmented(kvs[i][hd, :, F : F + D])
-            d_hi = dhi[r, b]
-            d_rows = jnp.concatenate([d_hi, dlo[r, b]], axis=0)
-            mixed = rows_of(jnp.where(mask, halves(nt(d_rows, va)), 0.0))
+            d_rows = d[r, b]
+            mixed = rows_of(jnp.where(mask, thirds(nt(d_rows, va)), 0.0))
             mixed_out[r, i] = mixed
-            st_hi, st_lo = split(full_state(states[r][...] + lines[r, b]))
-            qg = halves(nn(mixed, k) + nn(d_rows, st_hi)) + nn(d_hi, st_lo)
+            st_hi, st_mid, st_lo = split(full_state(states[r][...] + lines[r, b]))
+            small = nn(d_rows[0 : 2 * TB], st_mid)
+            small = small[0:TB] + (small[TB:] + nn(d_rows[0:TB], st_lo))
+            qg = thirds(nn(mixed, k) + nn(d_rows, st_hi)) + small
             outs[i][hd] = (qg * scale).astype(BF)
 
 
-def qgrad(pos, kvs, dhi, dlo, lines, states, scale, blocks):
+def qgrad(pos, kvs, d, lines, states, scale, blocks):
     n = len(blocks)
     out = call(
         functools.partial(qgrad_kernel, scale, blocks),
-        [piece(F)] * n + [shape(HL, n, 2 * TB, TB, kind=BF)],
-        vmem(n + 7),
+        [piece(F)] * n + [shape(HL, n, 3 * TB, TB, kind=BF)],
+        vmem(n + 6),
         vmem(n + 1),
-        (pos, *[kvs[b] for b in blocks], dhi, dlo, lines, *states),
+        (pos, *[kvs[b] for b in blocks], d, lines, *states),
     )
     return out[0:n], out[n]
 
@@ -396,8 +398,9 @@
             q = qs[b][hd]
             va = augmented(kvs[b][hd, :, F : F + D])
             mixed = held[b][0].at[r, held[b][1]]
-            a_hi, a_lo = split(full_state(lines[b]))
-            out[r, b] = tn(mixed[0:TB, :], q) + tn(mixed[TB:, :], q) + nn(va, a_hi) + nn(va, a_lo)
+            kg = [tn(mixed[t * TB : (t + 1) * TB, :], q) for t in range(3)]
+            kg += [nn(va, a) for a in split(full_state(lines[b]))]
+            out[r, b] = (kg[0] + kg[3]) + ((kg[1] + kg[4]) + (kg[2] + kg[5]))
 
 
 def inner(pos, kvs, qs, far, near, own, adj):
@@ -410,10 +413,10 @@
     x = pos[0]
     for r in range(HL):
         hd = mod4(x - r)
-        a_hi, a_lo = split(full_state(states[r]))
+        a_hi, a_mid, a_lo = split(full_state(states[r]))
         for i, b in enumerate(blocks):
             va = augmented(kvs[i][hd, :, F : F + D])
-            kg = part[r, b] + nn(va, a_hi) + nn(va, a_lo)
+            kg = part[r, b] + (nn(va, a_hi) + (nn(va, a_mid) + nn(va, a_lo)))
             outs[i][hd] = (kg * scale).astype(BF)
 
 
@@ -524,11 +527,11 @@
     lines = earlier_in_line(pos, kvs)
     nd = pre(pos, kvs, qs, lines)
     states = scan_states(sums, pos, False)
-    d_hi, d_lo, adj, adj_sums = post(pos, qs, nd, teas, states)
+    d, adj, adj_sums = post(pos, qs, nd, teas, states)
     qparts = [None] * NZ
-    (qparts[2],), far = qgrad(pos, kvs, d_hi, d_lo, lines, states, scale, (2,))
-    (qparts[3], qparts[1]), near = qgrad(pos, kvs, d_hi, d_lo, lines, states, scale, NEAR)
-    (qparts[0],), own = qgrad(pos, kvs, d_hi, d_lo, lines, states, scale, (0,))
+    (qparts[2],), far = qgrad(pos, kvs, d, lines, states, scale, (2,))
+    (qparts[3], qparts[1]), near = qgrad(pos, kvs, d, lines, states, scale, NEAR)
+    (qparts[0],), own = qgrad(pos, kvs, d, lines, states, scale, (0,))
     query_grad = unpack_all(pos, exchange_z(qparts))
     part = inner(pos, kvs, qs, far, near, own, adj)
     after = scan_states(adj_sums, pos, True)

time: 167 us -> 171 us (1.024)
  the two profiles are of different devices: /device:TPU:32 before, /device:TPU:0 now
where the time goes in v4:
time: 171 us
  waiting for transfers between devices  82 us (48%)
  starting transfers between devices  53.1 us (31%)
  Pallas kernels  34.8 us (20%)
    ppermute x12, waiting for transfers between devices, send_z(): return lax.ppermute(part, 'grp', grp_pairs(0, r))  58.6 us
    pallas_call x28, Pallas kernels, call(): pl.pallas_call(body, out_shape=out_shape, in_specs=in_specs, out_specs=ou...  34.8 us
    ppermute x15, starting transfers between devices, send_x(): return lax.ppermute(part, 'grp', grp_pairs(r, 0))  22.6 us
    ppermute x12, starting transfers between devices, send_z(): return lax.ppermute(part, 'grp', grp_pairs(0, r))  21.7 us
    ppermute x15, waiting for transfers between devices, send_x(): return lax.ppermute(part, 'grp', grp_pairs(r, 0))  14.4 us
    ppermute x2, starting transfers between devices, scan_states(): far = lax.ppermute(half, 'ctx', y_pairs(2))  6.16 us
    ppermute x2, waiting for transfers between devices, scan_states(): far = lax.ppermute(half, 'ctx', y_pairs(2))  5.37 us
  transfers between devices with their start and end apart: 35, of which 17 were waited for; matrix products, arithmetic and copies ran while one was open for 0% of the time, Pallas kernels for 16%

profile of v4, /device:TPU:0, one launch (start us, length us, event | category | flops | bytes accessed | tf_op | source)
XLA Modules:
  0.0 171.0 jit_solution(12691807011171553610)
XLA Ops:
  0.6 1.3 shard_map.63
  1.9 4.1 %collective-permute-start.4 = (bf16[4,256,384]{2,1,0:T(8,128)(2,1)S(1)}, bf16[4,256,384]{2,1,0:T(8,128)(2,1)S(1)}, u32[]{:S(2)}, u32[]{:S(2)}) collective-permute-start(bf16[4,256,384]{2,1,0:T(8,128)(2,1)S(1)} %shard_map.63), channel_id=1, source_target_pairs={{0,2},{1,3},{2,0},{3,1},{4,6},{5,7},{6,4},{7,5},{8,10},{9,11},{10,... | collective-permute-start | bytes 2359304 | tf_op jit(solution)/shard_map/ppermute | solution.py:435
  6.0 1.6 shard_map.62
  7.6 1.1 collective-permute-start.3
  8.7 2.2 %collective-permute-start.5 = (bf16[4,256,384]{2,1,0:T(8,128)(2,1)S(1)}, bf16[4,256,384]{2,1,0:T(8,128)(2,1)S(1)}, u32[]{:S(2)}, u32[]{:S(2)}) collective-permute-start(bf16[4,256,384]{2,1,0:T(8,128)(2,1)S(1)} %get-tuple-element.46), channel_id=1, source_target_pairs={{0,3},{1,0},{2,1},{3,2},{4,7},{5,4},{6,5},{7,6},{8,11},{9,8},{10,9... | collective-permute-start | bytes 2359304 | tf_op jit(solution)/shard_map/ppermute | solution.py:435
  10.9 1.3 shard_map.59.refs_0_
  12.2 12.3 %collective-permute-done.4.refs_2_.refs_1_.refs_0_ = bf16[4,256,384]{2,1,0:T(8,128)(2,1)S(1)} collective-permute-done((bf16[4,256,384]{2,1,0:T(8,128)(2,1)S(1)}, bf16[4,256,384]{2,1,0:T(8,128)(2,1)S(1)}, u32[]{:S(2)}, u32[]{:S(2)}) %collective-permute-start.4) | collective-permute-done | bytes 786464 | tf_op jit(solution)/shard_map/ppermute | solution.py:435
  24.9 15.5 %collective-permute-done.3.refs_1_.refs_0_ = bf16[4,256,384]{2,1,0:T(8,128)(2,1)S(1)} collective-permute-done((bf16[4,256,384]{2,1,0:T(8,128)(2,1)S(1)}, bf16[4,256,384]{2,1,0:T(8,128)(2,1)S(1)}, u32[]{:S(2)}, u32[]{:S(2)}) %collective-permute-start.3) | collective-permute-done | bytes 786464 | tf_op jit(solution)/shard_map/ppermute | solution.py:435
  40.4 0.8 collective-permute-done.5.refs_3_.refs_1_
  41.2 0.4 shard_map.68
  41.6 1.6 collective-permute-start.9
  43.2 2.7 %collective-permute-start.10 = (f32[136,256]{1,0:T(8,128)S(1)}, f32[136,256]{1,0:T(8,128)S(1)}, u32[]{:S(2)}, u32[]{:S(2)}) collective-permute-start(f32[136,256]{1,0:T(8,128)S(1)} %get-tuple-element.53), channel_id=1, source_target_pairs={{0,8},{1,9},{2,10},{3,11},{4,12},{5,13},{6,14},{7,15},{8,0},{9,1},... | collective-permute-start | bytes 417800 | tf_op jit(solution)/shard_map/ppermute | solution.py:439
  45.9 1.4 collective-permute-start.11
  47.3 1.6 collective-permute-done.9.m1.refs_4_
  48.9 2.8 %collective-permute-done.10.m2.refs_5_ = f32[136,256]{1,0:T(8,128)S(1)} collective-permute-done((f32[136,256]{1,0:T(8,128)S(1)}, f32[136,256]{1,0:T(8,128)S(1)}, u32[]{:S(2)}, u32[]{:S(2)}) %collective-permute-start.10) | collective-permute-done | bytes 139296 | tf_op jit(solution)/shard_map/ppermute | solution.py:439
  51.8 1.6 shard_map.61
  53.4 1.4 collective-permute-start
  54.8 3.6 %collective-permute-start.1 = (bf16[4,256,256]{2,1,0:T(8,128)(2,1)S(1)}, bf16[4,256,256]{2,1,0:T(8,128)(2,1)S(1)}, u32[]{:S(2)}, u32[]{:S(2)}) collective-permute-start(bf16[4,256,256]{2,1,0:T(8,128)(2,1)S(1)} %get-tuple-element.43), channel_id=1, source_target_pairs={{0,2},{1,3},{2,0},{3,1},{4,6},{5,7},{6,4},{7,5},{8,10},{9,11},{10,... | collective-permute-start | bytes 1572872 | tf_op jit(solution)/shard_map/ppermute | solution.py:435
  58.3 1.0 collective-permute-start.2
  59.4 3.3 %collective-permute-start.14 = (f32[72,256]{1,0:T(8,128)S(1)}, f32[72,256]{1,0:T(8,128)S(1)}, u32[]{:S(2)}, u32[]{:S(2)}) collective-permute-start(f32[72,256]{1,0:T(8,128)S(1)} %get-tuple-element.56), channel_id=1, source_target_pairs={{0,64},{16,80},{32,96},{48,112},{64,0},{80,16},{96,32},{112,48},{1... | collective-permute-start | bytes 221192 | tf_op jit(solution)/shard_map/ppermute | solution.py:495
  62.7 0.7 collective-permute-start.13
  63.3 1.2 shard_map.66
  64.6 0.8 collective-permute-done.14.refs_1_
  65.3 1.3 collective-permute-start.6
  66.7 2.3 %collective-permute-done.13.refs_0_ = f32[136,256]{1,0:T(8,128)S(1)} collective-permute-done((f32[136,256]{1,0:T(8,128)S(1)}, f32[136,256]{1,0:T(8,128)S(1)}, u32[]{:S(2)}, u32[]{:S(2)}) %collective-permute-start.13) | collective-permute-done | bytes 139296 | tf_op jit(solution)/shard_map/ppermute | solution.py:496
  69.1 4.5 %collective-permute-done.6.refs_6_ = bf16[1024,128]{1,0:T(8,128)(2,1)S(1)} collective-permute-done((bf16[1024,128]{1,0:T(8,128)(2,1)S(1)}, bf16[1024,128]{1,0:T(8,128)(2,1)S(1)}, u32[]{:S(2)}, u32[]{:S(2)}) %collective-permute-start.6) | collective-permute-done | bytes 262176 | tf_op jit(solution)/shard_map/ppermute | solution.py:439
  73.5 1.4 collective-permute-start.7
  75.0 1.4 collective-permute-start.8
  76.5 0.7 collective-permute-start.16
  77.3 4.6 %collective-permute-done.1.refs_6_.refs_2_ = bf16[4,256,256]{2,1,0:T(8,128)(2,1)S(1)} collective-permute-done((bf16[4,256,256]{2,1,0:T(8,128)(2,1)S(1)}, bf16[4,256,256]{2,1,0:T(8,128)(2,1)S(1)}, u32[]{:S(2)}, u32[]{:S(2)}) %collective-permute-start.1) | collective-permute-done | bytes 524320 | tf_op jit(solution)/shard_map/ppermute | solution.py:435
  81.9 2.7 %collective-permute-start.17 = (f32[136,256]{1,0:T(8,128)S(1)}, f32[136,256]{1,0:T(8,128)S(1)}, u32[]{:S(2)}, u32[]{:S(2)}) collective-permute-start(f32[136,256]{1,0:T(8,128)S(1)} %get-tuple-element.59), channel_id=1, source_target_pairs={{0,8},{1,9},{2,10},{3,11},{4,12},{5,13},{6,14},{7,15},{8,0},{9,1},... | collective-permute-start | bytes 417800 | tf_op jit(solution)/shard_map/ppermute | solution.py:439
  84.5 1.4 collective-permute-start.18
  85.9 1.1 shard_map.60.refs_4_.refs_0_
  87.0 0.8 shard_map.64.refs_8_.refs_2_.refs_3_
  87.8 4.5 %shard_map.65.refs_4_ = f32[4,4,256,256]{3,2,1,0:T(8,128)S(1)} custom-call(bf16[4,256,384]{2,1,0:T(8,128)(2,1)S(1)} %shard_map.59.refs_0_, bf16[4,256,384]{2,1,0:T(8,128)(2,1)S(1)} %collective-permute-done.3.refs_1_.refs_0_, bf16[4,256,384]{2,1,0:T(8,128)(2,1)S(1)} %collective-permute-done.4.refs_2_.refs_1_.refs_0_, ...), custom_call_target="tpu_custom_call" | custom-call | tf_op jit(solution)/shard_map/pallas_call | solution.py:92
  92.4 4.0 %shard_map.73 = (bf16[4,4,768,256]{3,2,1,0:T(8,128)(2,1)S(1)}, f32[4,4,136,256]{3,2,1,0:T(8,128)S(1)}, f32[136,256]{1,0:T(8,128)S(1)}, f32[136,256]{1,0:T(8,128)...) custom-call(bf16[4,256,256]{2,1,0:T(8,128)(2,1)S(1)} %shard_map.60.refs_4_.refs_0_, ...), custom_call_target="tpu_custom_call" | custom-call | tf_op jit(solution)/shard_map/pallas_call | solution.py:92
  96.4 0.7 collective-permute-start.22
  97.1 2.2 %collective-permute-start.23 = (f32[136,256]{1,0:T(8,128)S(1)}, f32[136,256]{1,0:T(8,128)S(1)}, u32[]{:S(2)}, u32[]{:S(2)}) collective-permute-start(f32[136,256]{1,0:T(8,128)S(1)} %get-tuple-element.72), channel_id=1, source_target_pairs={{0,8},{1,9},{2,10},{3,11},{4,12},{5,13},{6,14},{7,15},{8,0},{9,1},... | collective-permute-start | bytes 417800 | tf_op jit(solution)/shard_map/ppermute | solution.py:439
  99.3 0.9 collective-permute-start.24
  100.2 5.3 %collective-permute-done.22.m1.refs_4_ = f32[136,256]{1,0:T(8,128)S(1)} collective-permute-done((f32[136,256]{1,0:T(8,128)S(1)}, f32[136,256]{1,0:T(8,128)S(1)}, u32[]{:S(2)}, u32[]{:S(2)}) %collective-permute-start.22) | collective-permute-done | bytes 139296 | tf_op jit(solution)/shard_map/ppermute | solution.py:439
  106.0 1.9 %shard_map.76 = (bf16[4,256,256]{2,1,0:T(8,128)(2,1)S(1)}, bf16[4,1,768,256]{3,2,1,0:T(8,128)(2,1)S(1)}) custom-call(bf16[4,256,384]{2,1,0:T(8,128)(2,1)S(1)} %collective-permute-done.4.refs_2_.refs_1_.refs_0_, bf16[4,4,768,256]{3,2,1,0:T(8,128)(2,1)S(1)} %get-tuple-element.61.refs_1_.refs_2_, f32[4,4,136,256]{3,2,1,0:T(8,128)S(1)} %shard_map.64.refs_8_.refs_2_.refs_3_, ...), custom_call_target="tpu_custom_call" | custom-call | tf_op jit(solution)/shard_map/pallas_call | solution.py:92
  107.9 1.0 collective-permute-start.20
  108.9 1.6 collective-permute-start.26
  110.6 2.9 %collective-permute-start.27 = (f32[72,256]{1,0:T(8,128)S(1)}, f32[72,256]{1,0:T(8,128)S(1)}, u32[]{:S(2)}, u32[]{:S(2)}) collective-permute-start(f32[72,256]{1,0:T(8,128)S(1)} %get-tuple-element.75), channel_id=1, source_target_pairs={{0,64},{16,80},{32,96},{48,112},{64,0},{80,16},{96,32},{112,48},{1... | collective-permute-start | bytes 221192 | tf_op jit(solution)/shard_map/ppermute | solution.py:495
  113.5 4.6 %collective-permute-done.27.refs_1_ = f32[72,256]{1,0:T(8,128)S(1)} collective-permute-done((f32[72,256]{1,0:T(8,128)S(1)}, f32[72,256]{1,0:T(8,128)S(1)}, u32[]{:S(2)}, u32[]{:S(2)}) %collective-permute-start.27) | collective-permute-done | bytes 73760 | tf_op jit(solution)/shard_map/ppermute | solution.py:495
  118.2 1.3 collective-permute-done.28.refs_1_
  119.8 0.6 collective-permute-start.29
  120.3 3.6 %collective-permute-start.30 = (f32[136,256]{1,0:T(8,128)S(1)}, f32[136,256]{1,0:T(8,128)S(1)}, u32[]{:S(2)}, u32[]{:S(2)}) collective-permute-start(f32[136,256]{1,0:T(8,128)S(1)} %get-tuple-element.78), channel_id=1, source_target_pairs={{0,8},{1,9},{2,10},{3,11},{4,12},{5,13},{6,14},{7,15},{8,0},{9,1},... | collective-permute-start | bytes 417800 | tf_op jit(solution)/shard_map/ppermute | solution.py:439
  123.9 3.6 %shard_map.75 = (bf16[4,256,256]{2,1,0:T(8,128)(2,1)S(1)}, bf16[4,256,256]{2,1,0:T(8,128)(2,1)S(1)}, bf16[4,2,768,256]{3,2,1,0:T(8,128)(2,1)S(1)}) custom-call(bf16[4,256,384]{2,1,0:T(8,128)(2,1)S(1)} %collective-permute-done.3.refs_1_.refs_0_, bf16[4,256,384]{2,1,0:T(8,128)(2,1)S(1)} %collective-permute-done.5.refs_3_.refs_1_, ...), custom_call_target="tpu_custom_call" | custom-call | tf_op jit(solution)/shard_map/pallas_call | solution.py:92
  127.5 1.1 collective-permute-start.19
  128.6 1.9 %shard_map.74 = (bf16[4,256,256]{2,1,0:T(8,128)(2,1)S(1)}, bf16[4,1,768,256]{3,2,1,0:T(8,128)(2,1)S(1)}) custom-call(bf16[4,256,384]{2,1,0:T(8,128)(2,1)S(1)} %shard_map.59.refs_0_, bf16[4,4,768,256]{3,2,1,0:T(8,128)(2,1)S(1)} %get-tuple-element.61.refs_1_.refs_2_, f32[4,4,136,256]{3,2,1,0:T(8,128)S(1)} %shard_map.64.refs_8_.refs_2_.refs_3_, ...), custom_call_target="tpu_custom_call" | custom-call | tf_op jit(solution)/shard_map/pallas_call | solution.py:92
  130.5 3.5 %shard_map.78.refs_1_.refs_2_ = f32[4,4,256,256]{3,2,1,0:T(8,128)S(1)} custom-call(bf16[4,256,384]{2,1,0:T(8,128)(2,1)S(1)} %shard_map.59.refs_0_, bf16[4,256,384]{2,1,0:T(8,128)(2,1)S(1)} %collective-permute-done.3.refs_1_.refs_0_, bf16[4,256,384]{2,1,0:T(8,128)(2,1)S(1)} %collective-permute-done.4.refs_2_.refs_1_.refs_0_, ...), custom_call_target="tpu_custom_call" | custom-call | tf_op jit(solution)/shard_map/pallas_call | solution.py:92
  134.0 2.3 %collective-permute-start.21 = (bf16[4,256,256]{2,1,0:T(8,128)(2,1)S(1)}, bf16[4,256,256]{2,1,0:T(8,128)(2,1)S(1)}, u32[]{:S(2)}, u32[]{:S(2)}) collective-permute-start(bf16[4,256,256]{2,1,0:T(8,128)(2,1)S(1)} %get-tuple-element.65), channel_id=1, source_target_pairs={{0,3},{1,0},{2,1},{3,2},{4,7},{5,4},{6,5},{7,6},{8,11},{9,8},{10,9... | collective-permute-start | bytes 1572872 | tf_op jit(solution)/shard_map/ppermute | solution.py:435
  136.3 1.0 shard_map.84
  137.4 3.2 %collective-permute-start.34 = (bf16[4,256,256]{2,1,0:T(8,128)(2,1)S(1)}, bf16[4,256,256]{2,1,0:T(8,128)(2,1)S(1)}, u32[]{:S(2)}, u32[]{:S(2)}) collective-permute-start(bf16[4,256,256]{2,1,0:T(8,128)(2,1)S(1)} %get-tuple-element.81), channel_id=1, source_target_pairs={{0,3},{1,0},{2,1},{3,2},{4,7},{5,4},{6,5},{7,6},{8,11},{9,8},{10,9... | collective-permute-start | bytes 1572872 | tf_op jit(solution)/shard_map/ppermute | solution.py:435
  140.6 0.6 shard_map.85
  141.2 0.7 collective-permute-start.33
  141.9 1.6 collective-permute-done.19.refs_1_
  143.5 5.3 %collective-permute-done.21.refs_3_ = bf16[4,256,256]{2,1,0:T(8,128)(2,1)S(1)} collective-permute-done((bf16[4,256,256]{2,1,0:T(8,128)(2,1)S(1)}, bf16[4,256,256]{2,1,0:T(8,128)(2,1)S(1)}, u32[]{:S(2)}, u32[]{:S(2)}) %collective-permute-start.21) | collective-permute-done | bytes 524320 | tf_op jit(solution)/shard_map/ppermute | solution.py:435
  148.9 1.4 shard_map.77
  150.3 0.6 shard_map.83.refs_0_
  150.9 13.7 %collective-permute-done.32.refs_1_ = bf16[4,256,256]{2,1,0:T(8,128)(2,1)S(1)} collective-permute-done((bf16[4,256,256]{2,1,0:T(8,128)(2,1)S(1)}, bf16[4,256,256]{2,1,0:T(8,128)(2,1)S(1)}, u32[]{:S(2)}, u32[]{:S(2)}) %collective-permute-start.32) | collective-permute-done | bytes 524320 | tf_op jit(solution)/shard_map/ppermute | solution.py:435
  164.6 4.8 %collective-permute-done.34.refs_3_ = bf16[4,256,256]{2,1,0:T(8,128)(2,1)S(1)} collective-permute-done((bf16[4,256,256]{2,1,0:T(8,128)(2,1)S(1)}, bf16[4,256,256]{2,1,0:T(8,128)(2,1)S(1)}, u32[]{:S(2)}, u32[]{:S(2)}) %collective-permute-start.34) | collective-permute-done | bytes 524320 | tf_op jit(solution)/shard_map/ppermute | solution.py:435
  169.4 1.4 shard_map.86
  (34 shorter events, 1.8 us)
Async XLA Ops:
  1.9 22.5 %collective-permute-start.4 = (bf16[4,256,384]{2,1,0:T(8,128)(2,1)S(1)}, bf16[4,256,384]{2,1,0:T(8,128)(2,1)S(1)}, u32[]{:S(2)}, u32[]{:S(2)}) collective-permute-start(bf16[4,256,384]{2,1,0:T(8,128)(2,1)S(1)} %shard_map.63), channel_id=1, source_target_pairs={{0,2},{1,3},{2,0},{3,1},{4,6},{5,7},{6,4},{7,5},{8,10},{9,11},{10,... | collective-permute-start | bytes 2359304 | tf_op jit(solution)/shard_map/ppermute | solution.py:435
  7.6 32.8 %collective-permute-start.3 = (bf16[4,256,384]{2,1,0:T(8,128)(2,1)S(1)}, bf16[4,256,384]{2,1,0:T(8,128)(2,1)S(1)}, u32[]{:S(2)}, u32[]{:S(2)}) collective-permute-start(bf16[4,256,384]{2,1,0:T(8,128)(2,1)S(1)} %get-tuple-element.45), channel_id=1, source_target_pairs={{0,1},{1,2},{2,3},{3,0},{4,5},{5,6},{6,7},{7,4},{8,9},{9,10},{10,1... | collective-permute-start | bytes 2359304 | tf_op jit(solution)/shard_map/ppermute | solution.py:435
  8.7 32.5 %collective-permute-start.5 = (bf16[4,256,384]{2,1,0:T(8,128)(2,1)S(1)}, bf16[4,256,384]{2,1,0:T(8,128)(2,1)S(1)}, u32[]{:S(2)}, u32[]{:S(2)}) collective-permute-start(bf16[4,256,384]{2,1,0:T(8,128)(2,1)S(1)} %get-tuple-element.46), channel_id=1, source_target_pairs={{0,3},{1,0},{2,1},{3,2},{4,7},{5,4},{6,5},{7,6},{8,11},{9,8},{10,9... | collective-permute-start | bytes 2359304 | tf_op jit(solution)/shard_map/ppermute | solution.py:435
  41.6 7.3 %collective-permute-start.9 = (f32[136,256]{1,0:T(8,128)S(1)}, f32[136,256]{1,0:T(8,128)S(1)}, u32[]{:S(2)}, u32[]{:S(2)}) collective-permute-start(f32[136,256]{1,0:T(8,128)S(1)} %get-tuple-element.52), channel_id=1, source_target_pairs={{0,4},{1,5},{2,6},{3,7},{4,8},{5,9},{6,10},{7,11},{8,12},{9,13},{1... | collective-permute-start | bytes 417800 | tf_op jit(solution)/shard_map/ppermute | solution.py:439
  43.2 8.5 %collective-permute-start.10 = (f32[136,256]{1,0:T(8,128)S(1)}, f32[136,256]{1,0:T(8,128)S(1)}, u32[]{:S(2)}, u32[]{:S(2)}) collective-permute-start(f32[136,256]{1,0:T(8,128)S(1)} %get-tuple-element.53), channel_id=1, source_target_pairs={{0,8},{1,9},{2,10},{3,11},{4,12},{5,13},{6,14},{7,15},{8,0},{9,1},... | collective-permute-start | bytes 417800 | tf_op jit(solution)/shard_map/ppermute | solution.py:439
  45.9 5.8 %collective-permute-start.11 = (f32[136,256]{1,0:T(8,128)S(1)}, f32[136,256]{1,0:T(8,128)S(1)}, u32[]{:S(2)}, u32[]{:S(2)}) collective-permute-start(f32[136,256]{1,0:T(8,128)S(1)} %get-tuple-element.54), channel_id=1, source_target_pairs={{0,12},{1,13},{2,14},{3,15},{4,0},{5,1},{6,2},{7,3},{8,4},{9,5},{1... | collective-permute-start | bytes 417800 | tf_op jit(solution)/shard_map/ppermute | solution.py:439
  51.7 7.6 %collective-permute-start.12 = (f32[136,256]{1,0:T(8,128)S(1)}, f32[136,256]{1,0:T(8,128)S(1)}, u32[]{:S(2)}, u32[]{:S(2)}) collective-permute-start(f32[136,256]{1,0:T(8,128)S(1)} %shard_map.69.refs_0_), channel_id=1, source_target_pairs={{0,16},{16,0},{32,48},{48,32},{64,80},{80,64},{96,112},{112,96},{1... | collective-permute-start | bytes 417800 | tf_op jit(solution)/shard_map/ppermute | solution.py:493
  53.4 23.1 %collective-permute-start = (bf16[4,256,256]{2,1,0:T(8,128)(2,1)S(1)}, bf16[4,256,256]{2,1,0:T(8,128)(2,1)S(1)}, u32[]{:S(2)}, u32[]{:S(2)}) collective-permute-start(bf16[4,256,256]{2,1,0:T(8,128)(2,1)S(1)} %get-tuple-element.42), channel_id=1, source_target_pairs={{0,1},{1,2},{2,3},{3,0},{4,5},{5,6},{6,7},{7,4},{8,9},{9,10},{10,1... | collective-permute-start | bytes 1572872 | tf_op jit(solution)/shard_map/ppermute | solution.py:435
  54.8 27.1 %collective-permute-start.1 = (bf16[4,256,256]{2,1,0:T(8,128)(2,1)S(1)}, bf16[4,256,256]{2,1,0:T(8,128)(2,1)S(1)}, u32[]{:S(2)}, u32[]{:S(2)}) collective-permute-start(bf16[4,256,256]{2,1,0:T(8,128)(2,1)S(1)} %get-tuple-element.43), channel_id=1, source_target_pairs={{0,2},{1,3},{2,0},{3,1},{4,6},{5,7},{6,4},{7,5},{8,10},{9,11},{10,... | collective-permute-start | bytes 1572872 | tf_op jit(solution)/shard_map/ppermute | solution.py:435
  58.3 26.2 %collective-permute-start.2 = (bf16[4,256,256]{2,1,0:T(8,128)(2,1)S(1)}, bf16[4,256,256]{2,1,0:T(8,128)(2,1)S(1)}, u32[]{:S(2)}, u32[]{:S(2)}) collective-permute-start(bf16[4,256,256]{2,1,0:T(8,128)(2,1)S(1)} %get-tuple-element.44), channel_id=1, source_target_pairs={{0,3},{1,0},{2,1},{3,2},{4,7},{5,4},{6,5},{7,6},{8,11},{9,8},{10,9... | collective-permute-start | bytes 1572872 | tf_op jit(solution)/shard_map/ppermute | solution.py:435
  59.4 5.9 %collective-permute-start.14 = (f32[72,256]{1,0:T(8,128)S(1)}, f32[72,256]{1,0:T(8,128)S(1)}, u32[]{:S(2)}, u32[]{:S(2)}) collective-permute-start(f32[72,256]{1,0:T(8,128)S(1)} %get-tuple-element.56), channel_id=1, source_target_pairs={{0,64},{16,80},{32,96},{48,112},{64,0},{80,16},{96,32},{112,48},{1... | collective-permute-start | bytes 221192 | tf_op jit(solution)/shard_map/ppermute | solution.py:495
  62.7 6.3 %collective-permute-start.13 = (f32[136,256]{1,0:T(8,128)S(1)}, f32[136,256]{1,0:T(8,128)S(1)}, u32[]{:S(2)}, u32[]{:S(2)}) collective-permute-start(f32[136,256]{1,0:T(8,128)S(1)} %get-tuple-element.55), channel_id=1, source_target_pairs={{0,32},{16,112},{32,64},{48,16},{64,96},{80,48},{96,0},{112,80},{1... | collective-permute-start | bytes 417800 | tf_op jit(solution)/shard_map/ppermute | solution.py:496
  65.3 8.2 %collective-permute-start.6 = (bf16[1024,128]{1,0:T(8,128)(2,1)S(1)}, bf16[1024,128]{1,0:T(8,128)(2,1)S(1)}, u32[]{:S(2)}, u32[]{:S(2)}) collective-permute-start(bf16[1024,128]{1,0:T(8,128)(2,1)S(1)} %get-tuple-element.48), channel_id=1, source_target_pairs={{0,4},{1,5},{2,6},{3,7},{4,8},{5,9},{6,10},{7,11},{8,12},{9,13},{1... | collective-permute-start | bytes 786440 | tf_op jit(solution)/shard_map/ppermute | solution.py:439
  69.0 6.0 %collective-permute-start.15 = (f32[136,256]{1,0:T(8,128)S(1)}, f32[136,256]{1,0:T(8,128)S(1)}, u32[]{:S(2)}, u32[]{:S(2)}) collective-permute-start(f32[136,256]{1,0:T(8,128)S(1)} %shard_map.71.refs_0_), channel_id=1, source_target_pairs={{0,16},{16,0},{32,48},{48,32},{64,80},{80,64},{96,112},{112,96},{1... | collective-permute-start | bytes 417800 | tf_op jit(solution)/shard_map/ppermute | solution.py:498
  73.5 18.8 %collective-permute-start.7 = (bf16[1024,128]{1,0:T(8,128)(2,1)S(1)}, bf16[1024,128]{1,0:T(8,128)(2,1)S(1)}, u32[]{:S(2)}, u32[]{:S(2)}) collective-permute-start(bf16[1024,128]{1,0:T(8,128)(2,1)S(1)} %get-tuple-element.49), channel_id=1, source_target_pairs={{0,8},{1,9},{2,10},{3,11},{4,12},{5,13},{6,14},{7,15},{8,0},{9,1},... | collective-permute-start | bytes 786440 | tf_op jit(solution)/shard_map/ppermute | solution.py:439
  75.0 17.4 %collective-permute-start.8 = (bf16[1024,128]{1,0:T(8,128)(2,1)S(1)}, bf16[1024,128]{1,0:T(8,128)(2,1)S(1)}, u32[]{:S(2)}, u32[]{:S(2)}) collective-permute-start(bf16[1024,128]{1,0:T(8,128)(2,1)S(1)} %get-tuple-element.50), channel_id=1, source_target_pairs={{0,12},{1,13},{2,14},{3,15},{4,0},{5,1},{6,2},{7,3},{8,4},{9,5},{1... | collective-permute-start | bytes 786440 | tf_op jit(solution)/shard_map/ppermute | solution.py:439
  76.5 15.8 %collective-permute-start.16 = (f32[136,256]{1,0:T(8,128)S(1)}, f32[136,256]{1,0:T(8,128)S(1)}, u32[]{:S(2)}, u32[]{:S(2)}) collective-permute-start(f32[136,256]{1,0:T(8,128)S(1)} %get-tuple-element.58), channel_id=1, source_target_pairs={{0,4},{1,5},{2,6},{3,7},{4,8},{5,9},{6,10},{7,11},{8,12},{9,13},{1... | collective-permute-start | bytes 417800 | tf_op jit(solution)/shard_map/ppermute | solution.py:439
  81.9 10.5 %collective-permute-start.17 = (f32[136,256]{1,0:T(8,128)S(1)}, f32[136,256]{1,0:T(8,128)S(1)}, u32[]{:S(2)}, u32[]{:S(2)}) collective-permute-start(f32[136,256]{1,0:T(8,128)S(1)} %get-tuple-element.59), channel_id=1, source_target_pairs={{0,8},{1,9},{2,10},{3,11},{4,12},{5,13},{6,14},{7,15},{8,0},{9,1},... | collective-permute-start | bytes 417800 | tf_op jit(solution)/shard_map/ppermute | solution.py:439
  84.5 7.8 %collective-permute-start.18 = (f32[136,256]{1,0:T(8,128)S(1)}, f32[136,256]{1,0:T(8,128)S(1)}, u32[]{:S(2)}, u32[]{:S(2)}) collective-permute-start(f32[136,256]{1,0:T(8,128)S(1)} %get-tuple-element.60), channel_id=1, source_target_pairs={{0,12},{1,13},{2,14},{3,15},{4,0},{5,1},{6,2},{7,3},{8,4},{9,5},{1... | collective-permute-start | bytes 417800 | tf_op jit(solution)/shard_map/ppermute | solution.py:439
  96.4 9.2 %collective-permute-start.22 = (f32[136,256]{1,0:T(8,128)S(1)}, f32[136,256]{1,0:T(8,128)S(1)}, u32[]{:S(2)}, u32[]{:S(2)}) collective-permute-start(f32[136,256]{1,0:T(8,128)S(1)} %get-tuple-element.71), channel_id=1, source_target_pairs={{0,4},{1,5},{2,6},{3,7},{4,8},{5,9},{6,10},{7,11},{8,12},{9,13},{1... | collective-permute-start | bytes 417800 | tf_op jit(solution)/shard_map/ppermute | solution.py:439
  97.1 8.5 %collective-permute-start.23 = (f32[136,256]{1,0:T(8,128)S(1)}, f32[136,256]{1,0:T(8,128)S(1)}, u32[]{:S(2)}, u32[]{:S(2)}) collective-permute-start(f32[136,256]{1,0:T(8,128)S(1)} %get-tuple-element.72), channel_id=1, source_target_pairs={{0,8},{1,9},{2,10},{3,11},{4,12},{5,13},{6,14},{7,15},{8,0},{9,1},... | collective-permute-start | bytes 417800 | tf_op jit(solution)/shard_map/ppermute | solution.py:439
  99.3 6.5 %collective-permute-start.24 = (f32[136,256]{1,0:T(8,128)S(1)}, f32[136,256]{1,0:T(8,128)S(1)}, u32[]{:S(2)}, u32[]{:S(2)}) collective-permute-start(f32[136,256]{1,0:T(8,128)S(1)} %get-tuple-element.73), channel_id=1, source_target_pairs={{0,12},{1,13},{2,14},{3,15},{4,0},{5,1},{6,2},{7,3},{8,4},{9,5},{1... | collective-permute-start | bytes 417800 | tf_op jit(solution)/shard_map/ppermute | solution.py:439
  105.9 3.0 %collective-permute-start.25 = (f32[136,256]{1,0:T(8,128)S(1)}, f32[136,256]{1,0:T(8,128)S(1)}, u32[]{:S(2)}, u32[]{:S(2)}) collective-permute-start(f32[136,256]{1,0:T(8,128)S(1)} %shard_map.79.refs_0_), channel_id=1, source_target_pairs={{0,16},{16,0},{32,48},{48,32},{64,80},{80,64},{96,112},{112,96},{1... | collective-permute-start | bytes 417800 | tf_op jit(solution)/shard_map/ppermute | solution.py:493
  107.9 33.3 %collective-permute-start.20 = (bf16[4,256,256]{2,1,0:T(8,128)(2,1)S(1)}, bf16[4,256,256]{2,1,0:T(8,128)(2,1)S(1)}, u32[]{:S(2)}, u32[]{:S(2)}) collective-permute-start(bf16[4,256,256]{2,1,0:T(8,128)(2,1)S(1)} %get-tuple-element.64), channel_id=1, source_target_pairs={{0,2},{1,3},{2,0},{3,1},{4,6},{5,7},{6,4},{7,5},{8,10},{9,11},{10,... | collective-permute-start | bytes 1572872 | tf_op jit(solution)/shard_map/ppermute | solution.py:435
  108.9 9.2 %collective-permute-start.26 = (f32[136,256]{1,0:T(8,128)S(1)}, f32[136,256]{1,0:T(8,128)S(1)}, u32[]{:S(2)}, u32[]{:S(2)}) collective-permute-start(f32[136,256]{1,0:T(8,128)S(1)} %get-tuple-element.74), channel_id=1, source_target_pairs={{0,32},{16,112},{32,64},{48,16},{64,96},{80,48},{96,0},{112,80},{1... | collective-permute-start | bytes 417800 | tf_op jit(solution)/shard_map/ppermute | solution.py:496
  110.6 7.5 %collective-permute-start.27 = (f32[72,256]{1,0:T(8,128)S(1)}, f32[72,256]{1,0:T(8,128)S(1)}, u32[]{:S(2)}, u32[]{:S(2)}) collective-permute-start(f32[72,256]{1,0:T(8,128)S(1)} %get-tuple-element.75), channel_id=1, source_target_pairs={{0,64},{16,80},{32,96},{48,112},{64,0},{80,16},{96,32},{112,48},{1... | collective-permute-start | bytes 221192 | tf_op jit(solution)/shard_map/ppermute | solution.py:495
  118.1 1.4 collective-permute-start.28
  119.8 14.2 %collective-permute-start.29 = (f32[136,256]{1,0:T(8,128)S(1)}, f32[136,256]{1,0:T(8,128)S(1)}, u32[]{:S(2)}, u32[]{:S(2)}) collective-permute-start(f32[136,256]{1,0:T(8,128)S(1)} %get-tuple-element.77), channel_id=1, source_target_pairs={{0,4},{1,5},{2,6},{3,7},{4,8},{5,9},{6,10},{7,11},{8,12},{9,13},{1... | collective-permute-start | bytes 417800 | tf_op jit(solution)/shard_map/ppermute | solution.py:439
  120.3 15.9 %collective-permute-start.30 = (f32[136,256]{1,0:T(8,128)S(1)}, f32[136,256]{1,0:T(8,128)S(1)}, u32[]{:S(2)}, u32[]{:S(2)}) collective-permute-start(f32[136,256]{1,0:T(8,128)S(1)} %get-tuple-element.78), channel_id=1, source_target_pairs={{0,8},{1,9},{2,10},{3,11},{4,12},{5,13},{6,14},{7,15},{8,0},{9,1},... | collective-permute-start | bytes 417800 | tf_op jit(solution)/shard_map/ppermute | solution.py:439
  123.9 12.4 %collective-permute-start.31 = (f32[136,256]{1,0:T(8,128)S(1)}, f32[136,256]{1,0:T(8,128)S(1)}, u32[]{:S(2)}, u32[]{:S(2)}) collective-permute-start(f32[136,256]{1,0:T(8,128)S(1)} %get-tuple-element.79), channel_id=1, source_target_pairs={{0,12},{1,13},{2,14},{3,15},{4,0},{5,1},{6,2},{7,3},{8,4},{9,5},{1... | collective-permute-start | bytes 417800 | tf_op jit(solution)/shard_map/ppermute | solution.py:439
  127.5 16.1 %collective-permute-start.19 = (bf16[4,256,256]{2,1,0:T(8,128)(2,1)S(1)}, bf16[4,256,256]{2,1,0:T(8,128)(2,1)S(1)}, u32[]{:S(2)}, u32[]{:S(2)}) collective-permute-start(bf16[4,256,256]{2,1,0:T(8,128)(2,1)S(1)} %get-tuple-element.63), channel_id=1, source_target_pairs={{0,1},{1,2},{2,3},{3,0},{4,5},{5,6},{6,7},{7,4},{8,9},{9,10},{10,1... | collective-permute-start | bytes 1572872 | tf_op jit(solution)/shard_map/ppermute | solution.py:435
  134.0 14.9 %collective-permute-start.21 = (bf16[4,256,256]{2,1,0:T(8,128)(2,1)S(1)}, bf16[4,256,256]{2,1,0:T(8,128)(2,1)S(1)}, u32[]{:S(2)}, u32[]{:S(2)}) collective-permute-start(bf16[4,256,256]{2,1,0:T(8,128)(2,1)S(1)} %get-tuple-element.65), channel_id=1, source_target_pairs={{0,3},{1,0},{2,1},{3,2},{4,7},{5,4},{6,5},{7,6},{8,11},{9,8},{10,9... | collective-permute-start | bytes 1572872 | tf_op jit(solution)/shard_map/ppermute | solution.py:435
  137.3 27.4 %collective-permute-start.32 = (bf16[4,256,256]{2,1,0:T(8,128)(2,1)S(1)}, bf16[4,256,256]{2,1,0:T(8,128)(2,1)S(1)}, u32[]{:S(2)}, u32[]{:S(2)}) collective-permute-start(bf16[4,256,256]{2,1,0:T(8,128)(2,1)S(1)} %get-tuple-element.80), channel_id=1, source_target_pairs={{0,1},{1,2},{2,3},{3,0},{4,5},{5,6},{6,7},{7,4},{8,9},{9,10},{10,1... | collective-permute-start | bytes 1572872 | tf_op jit(solution)/shard_map/ppermute | solution.py:435
  137.4 32.1 %collective-permute-start.34 = (bf16[4,256,256]{2,1,0:T(8,128)(2,1)S(1)}, bf16[4,256,256]{2,1,0:T(8,128)(2,1)S(1)}, u32[]{:S(2)}, u32[]{:S(2)}) collective-permute-start(bf16[4,256,256]{2,1,0:T(8,128)(2,1)S(1)} %get-tuple-element.81), channel_id=1, source_target_pairs={{0,3},{1,0},{2,1},{3,2},{4,7},{5,4},{6,5},{7,6},{8,11},{9,8},{10,9... | collective-permute-start | bytes 1572872 | tf_op jit(solution)/shard_map/ppermute | solution.py:435
  141.2 28.2 %collective-permute-start.33 = (bf16[4,256,256]{2,1,0:T(8,128)(2,1)S(1)}, bf16[4,256,256]{2,1,0:T(8,128)(2,1)S(1)}, u32[]{:S(2)}, u32[]{:S(2)}) collective-permute-start(bf16[4,256,256]{2,1,0:T(8,128)(2,1)S(1)} %shard_map.85), channel_id=1, source_target_pairs={{0,2},{1,3},{2,0},{3,1},{4,6},{5,7},{6,4},{7,5},{8,10},{9,11},{10,... | collective-permute-start | bytes 1572872 | tf_op jit(solution)/shard_map/ppermute | solution.py:435
